TPU v7x, 32 devices: a whole 2x2x4 slice. The times are simulated.
32 devices in a mesh: dp: 8 (over z, y), expert: 4 (over x, core).
Axes of the slice: x: 2, y: 2, z: 4, core: 2. Of those that a mesh axis runs over, the one named last changes fastest.
Arguments:
- tokens: bfloat16 [4096, 2048], P(('dp', 'expert')), may hold values from -6 to 6
- cotangent: bfloat16 [4096, 2048], P(('dp', 'expert')), may hold values from -6 to 6
- lengths: int32 [4], replicated, may hold values from 512 to 1024, as said below
- piece_order: int32 [4, 8], replicated, may hold values from 0 to 7, each once within a row
- routes: int32 [4096, 8], P(('dp', 'expert')), may hold values from 0 to 15, all different within a row; in each aligned block of 128 rows (0 to 127, 128 to 255, ...) at most 96 rows name the same one
- attn_gain: float32 [2048], P(('dp', 'expert')), may hold values from 0.5 to 1.5
- w_query: float32 [2048, 2048], P(('dp', 'expert')), may hold values from -0.125 to 0.125
- w_key: float32 [2048, 2048], P(('dp', 'expert')), may hold values from -0.125 to 0.125
- w_value: float32 [2048, 2048], P(('dp', 'expert')), may hold values from -0.125 to 0.125
- w_output: float32 [2048, 2048], P(('dp', 'expert')), may hold values from -3 to 3
- query_gain: float32 [128], P(('dp', 'expert')), may hold values from 0.5 to 1.5
- key_gain: float32 [128], P(('dp', 'expert')), may hold values from 0.5 to 1.5
- moe_gain: float32 [2048], P(('dp', 'expert')), may hold values from 0.5 to 1.5
- w_router: float32 [2048, 16], P(('dp', 'expert')), may hold values from -0.0625 to 0.0625
- w_gate: float32 [16, 2048, 1024], P('expert', 'dp'), may hold values from -0.125 to 0.125
- w_up: float32 [16, 2048, 1024], P('expert', 'dp'), may hold values from -0.125 to 0.125
- w_down: float32 [16, 1024, 2048], P('expert', 'dp'), may hold values from -1 to 1
Outputs:
- block_out: bfloat16 [4096, 2048], P(('dp', 'expert'))
- grad_tokens: bfloat16 [4096, 2048], P(('dp', 'expert'))
- grad_attn_gain: float32 [2048], P(('dp', 'expert'))
- grad_query_w: float32 [2048, 2048], P(('dp', 'expert'))
- grad_key_w: float32 [2048, 2048], P(('dp', 'expert'))
- grad_value_w: float32 [2048, 2048], P(('dp', 'expert'))
- grad_output_w: float32 [2048, 2048], P(('dp', 'expert'))
- grad_query_gain: float32 [128], P(('dp', 'expert'))
- grad_key_gain: float32 [128], P(('dp', 'expert'))
- grad_moe_gain: float32 [2048], P(('dp', 'expert'))
- grad_router: float32 [2048, 16], P(('dp', 'expert'))
- grad_gate: float32 [16, 2048, 1024], P('expert', 'dp')
- grad_up: float32 [16, 2048, 1024], P('expert', 'dp')
- grad_down: float32 [16, 1024, 2048], P('expert', 'dp')
Inputs may be any that keep to these rules, and one draw needn't show every extreme that they name: `lengths`: every length lies between 512 and 1024, and one sequence is 1024 long. `piece_order`: each row is a permutation of the 8 pieces. `routes`: each token names 8 different experts; among the rows of one device at most 96 name one expert, and some expert is named that often.
All inputs are finite; a program needn't handle non-finite values.
Results may differ from a plain program's by a relative error of at most 0.03.
Values may be sent and summed in bfloat16 or wider, within the bound.
No kernel may reach another device: no remote copies, remote signals or barrier semaphores. Data moves between devices by JAX's collectives and lax.ppermute only.
A program may use at most 384 MiB of HBM per device.

v0:
```python
from functools import partial
import math

import jax
import jax.numpy as jnp
from jax import lax
from jax.sharding import PartitionSpec as P

HEADS = 16
HD = 128


norm_eps = 1e-06
rope_base = 10000.0


def rms_scale(features, gain_vec):
    return (
        features
        * lax.rsqrt(jnp.mean(features * features, axis=-1, keepdims=True) + norm_eps)
        * gain_vec
    )


def rotary(features, angles):
    half_dim = features.shape[-1] // 2
    cosine = jnp.cos(angles)[:, None, :]
    sine_part = jnp.sin(angles)[:, None, :]
    front_half = features[..., :half_dim]
    back_half = features[..., half_dim:]
    return jnp.concatenate(
        [front_half * cosine - back_half * sine_part, back_half * cosine + front_half * sine_part],
        axis=-1,
    )


def head_piece(angles, flat_vals, gain_vec):
    count = flat_vals.shape[0]
    shaped = flat_vals.reshape(count, HEADS, HD)
    return rotary(rms_scale(shaped, gain_vec), angles).reshape(count, HEADS * HD)


def swiglu(gate_part, up_part):
    return jax.nn.silu(gate_part) * up_part


def contract_rows(left_mat, right_mat):
    return lax.dot_general(
        left_mat, right_mat, (((0,), (0,)), ((), ())), preferred_element_type=jnp.float32
    )


def times_transpose(left_mat, right_mat):
    return lax.dot_general(
        left_mat, right_mat, (((1,), (1,)), ((), ())), preferred_element_type=jnp.float32
    )


def on_device(
    tokens,
    cotangent,
    lengths,
    piece_order,
    routes,
    attn_gain,
    w_query,
    w_key,
    w_value,
    w_output,
    query_gain,
    key_gain,
    moe_gain,
    w_router,
    w_gate,
    w_up,
    w_down,
):
    tok_rows = tokens.shape[0]
    model_width = tokens.shape[1]
    group_index = lax.axis_index("expert")
    member = lax.axis_index("dp")
    n_groups = lax.axis_size("expert")
    local_count = w_gate.shape[0]
    expert_total = local_count * n_groups
    top_count = routes.shape[1]
    capacity = 3 * tok_rows * top_count // (2 * expert_total)
    score_scale = 1.0 / math.sqrt(HD)
    norm_one, norm_two, gain_query, gain_key = (
        lax.all_gather(attn_gain, ("dp", "expert"), axis=0, tiled=True),
        lax.all_gather(moe_gain, ("dp", "expert"), axis=0, tiled=True),
        lax.all_gather(query_gain, ("dp", "expert"), axis=0, tiled=True),
        lax.all_gather(key_gain, ("dp", "expert"), axis=0, tiled=True),
    )
    wq_all, wk_all, wv_all, wo_all, wr_all = (
        lax.all_gather(w_query.astype(jnp.bfloat16), ("dp", "expert"), axis=0, tiled=True),
        lax.all_gather(w_key.astype(jnp.bfloat16), ("dp", "expert"), axis=0, tiled=True),
        lax.all_gather(w_value.astype(jnp.bfloat16), ("dp", "expert"), axis=0, tiled=True),
        lax.all_gather(w_output.astype(jnp.bfloat16), ("dp", "expert"), axis=0, tiled=True),
        lax.all_gather(w_router.astype(jnp.bfloat16), ("dp", "expert"), axis=0, tiled=True),
    )
    inputs = tokens.astype(jnp.float32)
    normed_one = rms_scale(inputs, norm_one).astype(jnp.bfloat16)
    query_flat = jnp.dot(normed_one, wq_all, preferred_element_type=jnp.float32)
    key_flat = jnp.dot(normed_one, wk_all, preferred_element_type=jnp.float32)
    value_bf = jnp.dot(normed_one, wv_all, preferred_element_type=jnp.float32).astype(jnp.bfloat16)
    offsets = jnp.arange(tok_rows, dtype=jnp.int32)
    own_piece = piece_order[group_index, member]
    position = (own_piece * tok_rows + offsets).astype(jnp.float32)
    half_dim = HD // 2
    frequency = rope_base ** (-(jnp.arange(half_dim, dtype=jnp.float32) * 2.0 / HD))
    angles = position[:, None] * frequency[None, :]
    query_rot, query_back = jax.vjp(partial(head_piece, angles), query_flat, gain_query)
    key_rot, key_back = jax.vjp(partial(head_piece, angles), key_flat, gain_key)
    query_bf = query_rot.astype(jnp.bfloat16).reshape(tok_rows, HEADS, HD)
    key_bf = key_rot.astype(jnp.bfloat16)
    all_keys, all_values = (
        lax.all_gather(key_bf, "dp", axis=0, tiled=True),
        lax.all_gather(value_bf, "dp", axis=0, tiled=True),
    )
    key_pos = (piece_order[group_index][:, None] * tok_rows + offsets[None, :]).reshape(-1)
    visible = key_pos < lengths[group_index]

    def scores_of(keys_all):
        raw_scores = (
            jnp.einsum(
                "qhd,khd->hqk",
                query_bf,
                keys_all.reshape(-1, HEADS, HD),
                preferred_element_type=jnp.float32,
            )
            * score_scale
        )
        return jnp.where(visible[None, None, :], raw_scores, -jnp.inf)

    scores = scores_of(all_keys)
    score_top = jnp.max(scores, axis=-1, keepdims=True)
    log_total = score_top + jnp.log(jnp.sum(jnp.exp(scores - score_top), axis=-1, keepdims=True))
    attn_probs = jnp.exp(scores - log_total).astype(jnp.bfloat16)
    attended = jnp.einsum(
        "hqk,khd->qhd",
        attn_probs,
        all_values.reshape(-1, HEADS, HD),
        preferred_element_type=jnp.float32,
    )
    attended_bf = attended.reshape(tok_rows, model_width).astype(jnp.bfloat16)
    hidden_one = inputs + jnp.dot(attended_bf, wo_all, preferred_element_type=jnp.float32)
    normed_two = rms_scale(hidden_one, norm_two).astype(jnp.bfloat16)
    router_logits = jnp.dot(normed_two, wr_all, preferred_element_type=jnp.float32)
    expert_ids = jnp.arange(expert_total, dtype=jnp.int32)
    route_hot = (routes[:, :, None] == expert_ids[None, None, :]).astype(jnp.float32)

    def gate_piece(logit_rows):
        picked = jnp.sum(route_hot * logit_rows[:, None, :], axis=-1)
        return jax.nn.softmax(picked, axis=-1)

    gate_weights, gate_back = jax.vjp(gate_piece, router_logits)
    flat_routes = routes.reshape(-1)
    flat_hot = (flat_routes[:, None] == expert_ids[None, :]).astype(jnp.int32)
    slot_rank = jnp.sum((jnp.cumsum(flat_hot, axis=0) - flat_hot) * flat_hot, axis=1)
    slot_index = flat_routes * capacity + slot_rank
    slot_ids = jnp.arange(expert_total * capacity, dtype=jnp.int32)
    slot_hot = (slot_index[:, None] == slot_ids[None, :]).astype(jnp.float32)
    route_numbers = jnp.arange(1, tok_rows * top_count + 1, dtype=jnp.int32).astype(jnp.float32)
    filler = jnp.dot(route_numbers, slot_hot, precision=lax.Precision.HIGHEST).astype(jnp.int32)
    token_of_slot = jnp.where(filler > 0, (filler - 1) // top_count + 1, 0)
    padded_two = jnp.concatenate([jnp.zeros((1, model_width), jnp.bfloat16), normed_two], axis=0)
    dispatched = jnp.take(padded_two, token_of_slot, axis=0)
    received = lax.all_to_all(
        dispatched, "expert", split_axis=0, concat_axis=0, tiled=True
    ).reshape(n_groups, local_count, capacity, model_width)
    saved_state = []
    produced = []
    for local_id in range(local_count):
        gate_all, up_all, down_all = (
            lax.all_gather(w_gate[local_id].astype(jnp.bfloat16), "dp", axis=0, tiled=True),
            lax.all_gather(w_up[local_id].astype(jnp.bfloat16), "dp", axis=0, tiled=True),
            lax.all_gather(w_down[local_id].astype(jnp.bfloat16), "dp", axis=0, tiled=True),
        )
        expert_rows = received[:, local_id].reshape(-1, model_width)
        gate_val = jnp.dot(expert_rows, gate_all, preferred_element_type=jnp.float32)
        up_val = jnp.dot(expert_rows, up_all, preferred_element_type=jnp.float32)
        inner_act = swiglu(gate_val, up_val).astype(jnp.bfloat16)
        expert_out = jnp.dot(inner_act, down_all, preferred_element_type=jnp.float32).astype(
            jnp.bfloat16
        )
        produced.append(expert_out.reshape(n_groups, capacity, model_width))
        saved_state.append((expert_rows, gate_val, up_val, inner_act, gate_all, up_all, down_all))
    outgoing = jnp.stack(produced, axis=1).reshape(-1, model_width)
    returned = lax.all_to_all(outgoing, "expert", split_axis=0, concat_axis=0, tiled=True)
    gathered_out = (
        jnp.take(returned, slot_index, axis=0)
        .reshape(tok_rows, top_count, model_width)
        .astype(jnp.float32)
    )
    mixture = jnp.sum(gate_weights[:, :, None] * gathered_out, axis=1)
    block_out = (hidden_one + mixture).astype(jnp.bfloat16)
    upstream = cotangent.astype(jnp.float32)
    gate_grads = jnp.sum(upstream[:, None, :] * gathered_out, axis=-1)
    scaled_back = (
        (gate_weights[:, :, None] * upstream[:, None, :])
        .astype(jnp.bfloat16)
        .reshape(-1, model_width)
    )
    padded_back = jnp.concatenate([jnp.zeros((1, model_width), jnp.bfloat16), scaled_back], axis=0)
    slot_grads = jnp.take(padded_back, filler, axis=0)
    expert_side = lax.all_to_all(
        slot_grads, "expert", split_axis=0, concat_axis=0, tiled=True
    ).reshape(n_groups, local_count, capacity, model_width)
    row_grads = []
    gate_w_grads = []
    up_w_grads = []
    down_w_grads = []
    for local_id in range(local_count):
        expert_rows, gate_val, up_val, inner_act, gate_all, up_all, down_all = saved_state[local_id]
        gate_all, up_all, down_all = (
            lax.all_gather(w_gate[local_id].astype(jnp.bfloat16), "dp", axis=0, tiled=True),
            lax.all_gather(w_up[local_id].astype(jnp.bfloat16), "dp", axis=0, tiled=True),
            lax.all_gather(w_down[local_id].astype(jnp.bfloat16), "dp", axis=0, tiled=True),
        )
        out_grad = expert_side[:, local_id].reshape(-1, model_width)
        down_grad = contract_rows(inner_act, out_grad)
        inner_grad = times_transpose(out_grad, down_all)
        _, act_back = jax.vjp(swiglu, gate_val, up_val)
        gate_val_grad, up_val_grad = act_back(inner_grad)
        gate_val_bf = gate_val_grad.astype(jnp.bfloat16)
        up_val_bf = up_val_grad.astype(jnp.bfloat16)
        gate_grad = contract_rows(expert_rows, gate_val_bf)
        up_grad = contract_rows(expert_rows, up_val_bf)
        row_grad = (
            times_transpose(gate_val_bf, gate_all) + times_transpose(up_val_bf, up_all)
        ).astype(jnp.bfloat16)
        gate_share, up_share, down_share = (
            lax.psum_scatter(
                gate_grad.astype(jnp.bfloat16), "dp", scatter_dimension=0, tiled=True
            ).astype(jnp.float32),
            lax.psum_scatter(
                up_grad.astype(jnp.bfloat16), "dp", scatter_dimension=0, tiled=True
            ).astype(jnp.float32),
            lax.psum_scatter(
                down_grad.astype(jnp.bfloat16), "dp", scatter_dimension=0, tiled=True
            ).astype(jnp.float32),
        )
        gate_w_grads.append(gate_share)
        up_w_grads.append(up_share)
        down_w_grads.append(down_share)
        row_grads.append(row_grad.reshape(n_groups, capacity, model_width))
    back_rows = lax.all_to_all(
        jnp.stack(row_grads, axis=1).reshape(-1, model_width),
        "expert",
        split_axis=0,
        concat_axis=0,
        tiled=True,
    )
    token_grads = jnp.sum(
        jnp.take(back_rows, slot_index, axis=0)
        .reshape(tok_rows, top_count, model_width)
        .astype(jnp.float32),
        axis=1,
    )
    wq_all, wk_all, wv_all, wo_all, wr_all = (
        lax.all_gather(w_query.astype(jnp.bfloat16), ("dp", "expert"), axis=0, tiled=True),
        lax.all_gather(w_key.astype(jnp.bfloat16), ("dp", "expert"), axis=0, tiled=True),
        lax.all_gather(w_value.astype(jnp.bfloat16), ("dp", "expert"), axis=0, tiled=True),
        lax.all_gather(w_output.astype(jnp.bfloat16), ("dp", "expert"), axis=0, tiled=True),
        lax.all_gather(w_router.astype(jnp.bfloat16), ("dp", "expert"), axis=0, tiled=True),
    )
    (logit_grad,) = gate_back(gate_grads)
    logit_bf = logit_grad.astype(jnp.bfloat16)
    router_grad = contract_rows(normed_two, logit_bf)
    normed_two_grad = token_grads + times_transpose(logit_bf, wr_all)
    _, norm_two_back = jax.vjp(rms_scale, hidden_one, norm_two)
    hidden_part, norm_two_grad = norm_two_back(normed_two_grad)
    hidden_grad = upstream + hidden_part
    attn_grad_bf = hidden_grad.astype(jnp.bfloat16)
    output_grad = contract_rows(attended_bf, attn_grad_bf)
    attended_grad = (
        times_transpose(attn_grad_bf, wo_all).astype(jnp.bfloat16).reshape(tok_rows, HEADS, HD)
    )
    keys_three = all_keys.reshape(-1, HEADS, HD)
    values_three = all_values.reshape(-1, HEADS, HD)
    probs_full = jnp.exp(scores_of(all_keys) - log_total)
    probs_bf = probs_full.astype(jnp.bfloat16)
    prob_grad = jnp.einsum(
        "qhd,khd->hqk", attended_grad, values_three, preferred_element_type=jnp.float32
    )
    score_grad = (
        probs_full * (prob_grad - jnp.sum(probs_full * prob_grad, axis=-1, keepdims=True))
    ).astype(jnp.bfloat16)
    query_grad = (
        jnp.einsum("hqk,khd->qhd", score_grad, keys_three, preferred_element_type=jnp.float32)
        * score_scale
    )
    key_part = (
        jnp.einsum("hqk,qhd->khd", score_grad, query_bf, preferred_element_type=jnp.float32)
        * score_scale
    )
    value_part = jnp.einsum(
        "hqk,qhd->khd", probs_bf, attended_grad, preferred_element_type=jnp.float32
    )
    key_grad, value_grad = (
        lax.psum_scatter(
            key_part.reshape(-1, model_width).astype(jnp.bfloat16),
            "dp",
            scatter_dimension=0,
            tiled=True,
        ).astype(jnp.float32),
        lax.psum_scatter(
            value_part.reshape(-1, model_width).astype(jnp.bfloat16),
            "dp",
            scatter_dimension=0,
            tiled=True,
        ).astype(jnp.float32),
    )
    query_flat_grad, query_gain_grad = query_back(query_grad.reshape(tok_rows, model_width))
    key_flat_grad, key_gain_grad = key_back(key_grad)
    query_flat_bf = query_flat_grad.astype(jnp.bfloat16)
    key_flat_bf = key_flat_grad.astype(jnp.bfloat16)
    value_grad_bf = value_grad.astype(jnp.bfloat16)
    wq_grad = contract_rows(normed_one, query_flat_bf)
    wk_grad = contract_rows(normed_one, key_flat_bf)
    wv_grad = contract_rows(normed_one, value_grad_bf)
    normed_one_grad = (
        times_transpose(query_flat_bf, wq_all)
        + times_transpose(key_flat_bf, wk_all)
        + times_transpose(value_grad_bf, wv_all)
    )
    _, norm_one_back = jax.vjp(rms_scale, inputs, norm_one)
    input_part, norm_one_grad = norm_one_back(normed_one_grad)
    grad_tokens = (hidden_grad + input_part).astype(jnp.bfloat16)
    shares = (
        lax.psum_scatter(wq_grad, ("dp", "expert"), scatter_dimension=0, tiled=True),
        lax.psum_scatter(wk_grad, ("dp", "expert"), scatter_dimension=0, tiled=True),
        lax.psum_scatter(wv_grad, ("dp", "expert"), scatter_dimension=0, tiled=True),
        lax.psum_scatter(output_grad, ("dp", "expert"), scatter_dimension=0, tiled=True),
        lax.psum_scatter(router_grad, ("dp", "expert"), scatter_dimension=0, tiled=True),
        lax.psum_scatter(norm_one_grad, ("dp", "expert"), scatter_dimension=0, tiled=True),
        lax.psum_scatter(norm_two_grad, ("dp", "expert"), scatter_dimension=0, tiled=True),
        lax.psum_scatter(query_gain_grad, ("dp", "expert"), scatter_dimension=0, tiled=True),
        lax.psum_scatter(key_gain_grad, ("dp", "expert"), scatter_dimension=0, tiled=True),
    )
    return (
        block_out,
        grad_tokens,
        shares[5],
        shares[0],
        shares[1],
        shares[2],
        shares[3],
        shares[7],
        shares[8],
        shares[6],
        shares[4],
        jnp.stack(gate_w_grads, axis=0),
        jnp.stack(up_w_grads, axis=0),
        jnp.stack(down_w_grads, axis=0),
    )


def solution(mesh):
    placed = (
        P(("dp", "expert"), None),
        P(("dp", "expert"), None),
        P(),
        P(),
        P(("dp", "expert"), None),
        P(("dp", "expert")),
        P(("dp", "expert"), None),
        P(("dp", "expert"), None),
        P(("dp", "expert"), None),
        P(("dp", "expert"), None),
        P(("dp", "expert")),
        P(("dp", "expert")),
        P(("dp", "expert")),
        P(("dp", "expert"), None),
        P("expert", "dp", None),
        P("expert", "dp", None),
        P("expert", "dp", None),
    )
    return jax.shard_map(
        on_device,
        mesh=mesh,
        in_specs=placed,
        out_specs=(
            P(("dp", "expert"), None),
            P(("dp", "expert"), None),
            P(("dp", "expert")),
            P(("dp", "expert"), None),
            P(("dp", "expert"), None),
            P(("dp", "expert"), None),
            P(("dp", "expert"), None),
            P(("dp", "expert")),
            P(("dp", "expert")),
            P(("dp", "expert")),
            P(("dp", "expert"), None),
            P("expert", "dp", None),
            P("expert", "dp", None),
            P("expert", "dp", None),
        ),
        check_vma=False,
    )
```

profile of v0, /device:TPU:13, one launch (start us, length us, event | category | flops | bytes accessed | tf_op | source)
XLA Modules:
  0.0 3763.7 jit_solution(3698394215440874441)
XLA Ops:
  95.7 73.8 %all-gather.38.cloned.1.call-done = bf16[2048,2048]{1,0:T(8,128)(2,1)} async-done(((bf16[64,2048]{1,0:T(8,128)(2,1)}), bf16[2048,2048]{1,0:T(8,128)(2,1)}) %all-gather.38.cloned.1.call-update) | async-done | bytes 8388624 | tf_op jit(solution)/shard_map/all_gather | solution.py:96
  177.8 70.8 %all-gather.32.cloned.1.call-done = bf16[2048,2048]{1,0:T(8,128)(2,1)} async-done(((bf16[64,2048]{1,0:T(8,128)(2,1)}), bf16[2048,2048]{1,0:T(8,128)(2,1)}) %all-gather.32.cloned.1.call-update) | async-done | bytes 8388624 | tf_op jit(solution)/shard_map/all_gather | solution.py:97
  328.0 66.6 %all-gather.34.cloned.1.call-done = bf16[1024,2048]{1,0:T(8,128)(2,1)} async-done(((bf16[128,2048]{1,0:T(8,128)(2,1)}), bf16[1024,2048]{1,0:T(8,128)(2,1)}) %all-gather.34.cloned.1.call-update) | async-done | bytes 4194320 | tf_op jit(solution)/shard_map/all_gather | solution.py:118
  401.8 75.1 %all-gather.42.cloned.1.call-done = bf16[2048,2048]{1,0:T(8,128)(2,1)} async-done(((bf16[64,2048]{1,0:T(8,128)(2,1)}), bf16[2048,2048]{1,0:T(8,128)(2,1)}) %all-gather.42.cloned.1.call-update) | async-done | bytes 8388624 | tf_op jit(solution)/shard_map/all_gather | solution.py:98
  502.5 93.9 %all-gather.12 = bf16[32,64,16]{1,2,0:T(8,128)(2,1)S(1)} all-gather(bf16[1,64,16]{1,2,0:T(8,128)(2,1)S(1)} %convert_bitcast_fusion.1), channel_id=1, replica_groups=mesh['dp'=8,'expert'=4] {'dp','expert'}, dimensions={0}, use_global_device_ids=true | all-gather | bytes 67584 | tf_op jit(solution)/shard_map/all_gather | solution.py:99
  636.0 63.3 %all-to-all-done.2 = bf16[4,384,2048]{2,1,0:T(8,128)(2,1)} async-done(((bf16[4,384,2048]{2,1,0:T(8,128)(2,1)}), bf16[4,384,2048]{2,1,0:T(8,128)(2,1)}, u32[]{:S(2)}, u32[]{:S(2)}) %all-to-all-start.2) | async-done | bytes 6291488 | tf_op jit(solution)/shard_map/all_to_all | solution.py:206
  775.2 68.5 %all-gather.60.cloned.1.call-done = bf16[1,1024,2048]{2,1,0:T(8,128)(2,1)} async-done(((bf16[1,128,2048]{2,1,0:T(8,128)(2,1)}), bf16[1,1024,2048]{2,1,0:T(8,128)(2,1)}) %all-gather.60.cloned.1.call-update) | async-done | bytes 4194320 | tf_op jit(solution)/shard_map/all_gather | solution.py:177
  849.3 67.7 %all-gather.58.cloned.1.call-done = bf16[1,2048,1024]{2,1,0:T(8,128)(2,1)} async-done(((bf16[1,256,1024]{2,1,0:T(8,128)(2,1)}), bf16[1,2048,1024]{2,1,0:T(8,128)(2,1)}) %all-gather.58.cloned.1.call-update) | async-done | bytes 4194320 | tf_op jit(solution)/shard_map/all_gather | solution.py:176
  928.7 62.3 %all-gather.50.cloned.1.call-done = bf16[1,2048,1024]{2,1,0:T(8,128)(2,1)} async-done(((bf16[1,256,1024]{2,1,0:T(8,128)(2,1)}), bf16[1,2048,1024]{2,1,0:T(8,128)(2,1)}) %all-gather.50.cloned.1.call-update) | async-done | bytes 4194320 | tf_op jit(solution)/shard_map/all_gather | solution.py:175
  996.7 67.7 %all-gather.54.cloned.1.call-done = bf16[1,1024,2048]{2,1,0:T(8,128)(2,1)} async-done(((bf16[1,128,2048]{2,1,0:T(8,128)(2,1)}), bf16[1,1024,2048]{2,1,0:T(8,128)(2,1)}) %all-gather.54.cloned.1.call-update) | async-done | bytes 4194320 | tf_op jit(solution)/shard_map/all_gather | solution.py:177
  1069.5 68.2 %all-gather.52.cloned.1.call-done = bf16[1,2048,1024]{2,1,0:T(8,128)(2,1)} async-done(((bf16[1,256,1024]{2,1,0:T(8,128)(2,1)}), bf16[1,2048,1024]{2,1,0:T(8,128)(2,1)}) %all-gather.52.cloned.1.call-update) | async-done | bytes 4194320 | tf_op jit(solution)/shard_map/all_gather | solution.py:176
  1149.2 62.4 %all-gather.44.cloned.1.call-done = bf16[1,2048,1024]{2,1,0:T(8,128)(2,1)} async-done(((bf16[1,256,1024]{2,1,0:T(8,128)(2,1)}), bf16[1,2048,1024]{2,1,0:T(8,128)(2,1)}) %all-gather.44.cloned.1.call-update) | async-done | bytes 4194320 | tf_op jit(solution)/shard_map/all_gather | solution.py:175
  1216.8 68.2 %all-gather.48.cloned.1.call-done = bf16[1,1024,2048]{2,1,0:T(8,128)(2,1)} async-done(((bf16[1,128,2048]{2,1,0:T(8,128)(2,1)}), bf16[1,1024,2048]{2,1,0:T(8,128)(2,1)}) %all-gather.48.cloned.1.call-update) | async-done | bytes 4194320 | tf_op jit(solution)/shard_map/all_gather | solution.py:177
  1290.1 68.2 %all-gather.46.cloned.1.call-done = bf16[1,2048,1024]{2,1,0:T(8,128)(2,1)} async-done(((bf16[1,256,1024]{2,1,0:T(8,128)(2,1)}), bf16[1,2048,1024]{2,1,0:T(8,128)(2,1)}) %all-gather.46.cloned.1.call-update) | async-done | bytes 4194320 | tf_op jit(solution)/shard_map/all_gather | solution.py:176
  1478.8 57.1 %all-to-all-done.1 = bf16[4,384,2048]{2,1,0:T(8,128)(2,1)} async-done(((bf16[4,384,2048]{2,1,0:T(8,128)(2,1)}), bf16[4,384,2048]{2,1,0:T(8,128)(2,1)}, u32[]{:S(2)}, u32[]{:S(2)}) %all-to-all-start.1) | async-done | bytes 6291488 | tf_op jit(solution)/shard_map/all_to_all | solution.py:189
  1780.9 96.7 %reduce-scatter.62.cloned.1.call-done = f32[64,16]{1,0:T(8,128)} async-done(((f32[2048,16]{1,0:T(8,128)}), f32[64,16]{1,0:T(8,128)}) %reduce-scatter.62.cloned.1.call-update) | async-done | bytes 4112
  1879.1 119.6 %reduce-scatter.40.cloned.1.call-done = bf16[256,1024]{1,0:T(8,128)(2,1)} async-done(((bf16[2048,1024]{1,0:T(8,128)(2,1)}), bf16[256,1024]{1,0:T(8,128)(2,1)}) %reduce-scatter.40.cloned.1.call-update) | async-done | bytes 524304 | tf_op jit(solution)/shard_map/reduce_scatter | solution.py:233
  1998.6 91.6 %reduce-scatter.38.cloned.1.call-done = bf16[256,1024]{1,0:T(8,128)(2,1)} async-done(((bf16[2048,1024]{1,0:T(8,128)(2,1)}), bf16[256,1024]{1,0:T(8,128)(2,1)}) %reduce-scatter.38.cloned.1.call-update) | async-done | bytes 524304 | tf_op jit(solution)/shard_map/reduce_scatter | solution.py:233
  2090.2 91.4 %reduce-scatter.36.cloned.1.call-done = bf16[256,1024]{1,0:T(8,128)(2,1)} async-done(((bf16[2048,1024]{1,0:T(8,128)(2,1)}), bf16[256,1024]{1,0:T(8,128)(2,1)}) %reduce-scatter.36.cloned.1.call-update) | async-done | bytes 524304 | tf_op jit(solution)/shard_map/reduce_scatter | solution.py:233
  2181.7 91.6 %reduce-scatter.34.cloned.1.call-done = bf16[256,1024]{1,0:T(8,128)(2,1)} async-done(((bf16[2048,1024]{1,0:T(8,128)(2,1)}), bf16[256,1024]{1,0:T(8,128)(2,1)}) %reduce-scatter.34.cloned.1.call-update) | async-done | bytes 524304 | tf_op jit(solution)/shard_map/reduce_scatter | solution.py:233
  2277.1 87.6 %reduce-scatter.48.cloned.1.call-done = bf16[256,1024]{1,0:T(8,128)(2,1)} async-done(((bf16[2048,1024]{1,0:T(8,128)(2,1)}), bf16[256,1024]{1,0:T(8,128)(2,1)}) %reduce-scatter.48.cloned.1.call-update) | async-done | bytes 524304 | tf_op jit(solution)/shard_map/reduce_scatter | solution.py:236
  2364.7 91.5 %reduce-scatter.46.cloned.1.call-done = bf16[256,1024]{1,0:T(8,128)(2,1)} async-done(((bf16[2048,1024]{1,0:T(8,128)(2,1)}), bf16[256,1024]{1,0:T(8,128)(2,1)}) %reduce-scatter.46.cloned.1.call-update) | async-done | bytes 524304 | tf_op jit(solution)/shard_map/reduce_scatter | solution.py:236
  2456.1 91.6 %reduce-scatter.44.cloned.1.call-done = bf16[256,1024]{1,0:T(8,128)(2,1)} async-done(((bf16[2048,1024]{1,0:T(8,128)(2,1)}), bf16[256,1024]{1,0:T(8,128)(2,1)}) %reduce-scatter.44.cloned.1.call-update) | async-done | bytes 524304 | tf_op jit(solution)/shard_map/reduce_scatter | solution.py:236
  2547.7 91.6 %reduce-scatter.42.cloned.1.call-done = bf16[256,1024]{1,0:T(8,128)(2,1)} async-done(((bf16[2048,1024]{1,0:T(8,128)(2,1)}), bf16[256,1024]{1,0:T(8,128)(2,1)}) %reduce-scatter.42.cloned.1.call-update) | async-done | bytes 524304 | tf_op jit(solution)/shard_map/reduce_scatter | solution.py:236
  2643.3 87.6 %reduce-scatter.56.cloned.1.call-done = bf16[128,2048]{1,0:T(8,128)(2,1)} async-done(((bf16[1024,2048]{1,0:T(8,128)(2,1)}), bf16[128,2048]{1,0:T(8,128)(2,1)}) %reduce-scatter.56.cloned.1.call-update) | async-done | bytes 524304 | tf_op jit(solution)/shard_map/reduce_scatter | solution.py:239
  2730.8 91.6 %reduce-scatter.54.cloned.1.call-done = bf16[128,2048]{1,0:T(8,128)(2,1)} async-done(((bf16[1024,2048]{1,0:T(8,128)(2,1)}), bf16[128,2048]{1,0:T(8,128)(2,1)}) %reduce-scatter.54.cloned.1.call-update) | async-done | bytes 524304 | tf_op jit(solution)/shard_map/reduce_scatter | solution.py:239
  2822.4 91.6 %reduce-scatter.52.cloned.1.call-done = bf16[128,2048]{1,0:T(8,128)(2,1)} async-done(((bf16[1024,2048]{1,0:T(8,128)(2,1)}), bf16[128,2048]{1,0:T(8,128)(2,1)}) %reduce-scatter.52.cloned.1.call-update) | async-done | bytes 524304 | tf_op jit(solution)/shard_map/reduce_scatter | solution.py:239
  2914.1 91.5 %reduce-scatter.50.cloned.1.call-done = bf16[128,2048]{1,0:T(8,128)(2,1)} async-done(((bf16[1024,2048]{1,0:T(8,128)(2,1)}), bf16[128,2048]{1,0:T(8,128)(2,1)}) %reduce-scatter.50.cloned.1.call-update) | async-done | bytes 524304 | tf_op jit(solution)/shard_map/reduce_scatter | solution.py:239
  3069.0 125.7 %reduce-scatter.32.cloned.1.call-done = f32[64,2048]{1,0:T(8,128)} async-done(((f32[2048,2048]{1,0:T(8,128)}), f32[64,2048]{1,0:T(8,128)}) %reduce-scatter.32.cloned.1.call-update) | async-done | bytes 524304 | tf_op jit(solution)/shard_map/reduce_scatter | solution.py:334
  3194.7 187.2 %reduce-scatter.26.cloned.1.call-done = f32[64,2048]{1,0:T(8,128)} async-done(((f32[2048,2048]{1,0:T(8,128)}), f32[64,2048]{1,0:T(8,128)}) %reduce-scatter.26.cloned.1.call-update) | async-done | bytes 524304 | tf_op jit(solution)/shard_map/reduce_scatter | solution.py:331
  3381.9 187.4 %reduce-scatter.28.cloned.1.call-done = f32[64,2048]{1,0:T(8,128)} async-done(((f32[2048,2048]{1,0:T(8,128)}), f32[64,2048]{1,0:T(8,128)}) %reduce-scatter.28.cloned.1.call-update) | async-done | bytes 524304 | tf_op jit(solution)/shard_map/reduce_scatter | solution.py:332
  3569.3 187.4 %reduce-scatter.30.cloned.1.call-done = f32[64,2048]{1,0:T(8,128)} async-done(((f32[2048,2048]{1,0:T(8,128)}), f32[64,2048]{1,0:T(8,128)}) %reduce-scatter.30.cloned.1.call-update) | async-done | bytes 524304 | tf_op jit(solution)/shard_map/reduce_scatter | solution.py:333
  (510 shorter events, 809.7 us)
Async XLA Ops:
  10.9 237.7 %all-gather.32.cloned.1.call-start = ((), (), s32[]{:S(2)}) async-start(), calls=%async_computation.23 | async-start | bytes 8650752 | tf_op jit(solution)/shard_map/all_gather | solution.py:97
  12.8 307.9 %all-gather.40.cloned.1.call-start = ((), (), s32[]{:S(2)}) async-start(), calls=%async_computation.27 | async-start | bytes 4718592 | tf_op jit(solution)/shard_map/all_gather | solution.py:117
  255.0 449.6 %all-gather.62.cloned.1.call-start = ((), (), s32[]{:S(2)}) async-start(), calls=%async_computation.54 | async-start | bytes 4718592 | tf_op jit(solution)/shard_map/all_gather | solution.py:175
  259.0 452.5 %all-gather.66.cloned.1.call-start = ((), (), s32[]{:S(2)}) async-start(), calls=%async_computation.56 | async-start | bytes 4718592 | tf_op jit(solution)/shard_map/all_gather | solution.py:177
  263.0 454.2 %all-gather.64.cloned.1.call-start = ((), (), s32[]{:S(2)}) async-start(), calls=%async_computation.55 | async-start | bytes 4718592 | tf_op jit(solution)/shard_map/all_gather | solution.py:176
  267.0 502.6 %all-gather.56.cloned.1.call-start = ((), (), s32[]{:S(2)}) async-start(), calls=%async_computation.51 | async-start | bytes 4718592 | tf_op jit(solution)/shard_map/all_gather | solution.py:175
  267.6 576.1 %all-gather.60.cloned.1.call-start = ((), (), s32[]{:S(2)}) async-start(), calls=%async_computation.53 | async-start | bytes 4718592 | tf_op jit(solution)/shard_map/all_gather | solution.py:177
  268.3 648.7 %all-gather.58.cloned.1.call-start = ((), (), s32[]{:S(2)}) async-start(), calls=%async_computation.52 | async-start | bytes 4718592 | tf_op jit(solution)/shard_map/all_gather | solution.py:176
  268.9 722.2 %all-gather.50.cloned.1.call-start = ((), (), s32[]{:S(2)}) async-start(), calls=%async_computation.48 | async-start | bytes 4718592 | tf_op jit(solution)/shard_map/all_gather | solution.py:175
  269.6 794.8 %all-gather.54.cloned.1.call-start = ((), (), s32[]{:S(2)}) async-start(), calls=%async_computation.50 | async-start | bytes 4718592 | tf_op jit(solution)/shard_map/all_gather | solution.py:177
  270.2 867.5 %all-gather.52.cloned.1.call-start = ((), (), s32[]{:S(2)}) async-start(), calls=%async_computation.49 | async-start | bytes 4718592 | tf_op jit(solution)/shard_map/all_gather | solution.py:176
  270.8 940.8 %all-gather.44.cloned.1.call-start = ((), (), s32[]{:S(2)}) async-start(), calls=%async_computation.45 | async-start | bytes 4718592 | tf_op jit(solution)/shard_map/all_gather | solution.py:175
  501.8 783.2 %all-gather.48.cloned.1.call-start = ((), (), s32[]{:S(2)}) async-start(), calls=%async_computation.47 | async-start | bytes 4718592 | tf_op jit(solution)/shard_map/all_gather | solution.py:177
  629.5 728.8 %all-gather.46.cloned.1.call-start = ((), (), s32[]{:S(2)}) async-start(), calls=%async_computation.46 | async-start | bytes 4718592 | tf_op jit(solution)/shard_map/all_gather | solution.py:176
  1466.2 237.2 %reduce-scatter.58.cloned.1.call-start = ((), (), s32[]{:S(2)}) async-start(), calls=%async_computation.57 | async-start | bytes 4718592
  1607.2 270.4 %reduce-scatter.62.cloned.1.call-start = ((), (), s32[]{:S(2)}) async-start(), calls=%async_computation.59 | async-start | bytes 1081344
  1609.7 389.0 %reduce-scatter.40.cloned.1.call-start = ((), (), s32[]{:S(2)}) async-start(), calls=%async_computation.36 | async-start | bytes 4718592 | tf_op jit(solution)/shard_map/reduce_scatter | solution.py:233
  1616.0 474.2 %reduce-scatter.38.cloned.1.call-start = ((), (), s32[]{:S(2)}) async-start(), calls=%async_computation.35 | async-start | bytes 4718592 | tf_op jit(solution)/shard_map/reduce_scatter | solution.py:233
  1623.2 558.5 %reduce-scatter.36.cloned.1.call-start = ((), (), s32[]{:S(2)}) async-start(), calls=%async_computation.34 | async-start | bytes 4718592 | tf_op jit(solution)/shard_map/reduce_scatter | solution.py:233
  1630.1 643.1 %reduce-scatter.34.cloned.1.call-start = ((), (), s32[]{:S(2)}) async-start(), calls=%async_computation.33 | async-start | bytes 4718592 | tf_op jit(solution)/shard_map/reduce_scatter | solution.py:233
  1637.1 727.6 %reduce-scatter.48.cloned.1.call-start = ((), (), s32[]{:S(2)}) async-start(), calls=%async_computation.40 | async-start | bytes 4718592 | tf_op jit(solution)/shard_map/reduce_scatter | solution.py:236
  1643.1 813.0 %reduce-scatter.46.cloned.1.call-start = ((), (), s32[]{:S(2)}) async-start(), calls=%async_computation.39 | async-start | bytes 4718592 | tf_op jit(solution)/shard_map/reduce_scatter | solution.py:236
  1649.5 898.3 %reduce-scatter.44.cloned.1.call-start = ((), (), s32[]{:S(2)}) async-start(), calls=%async_computation.38 | async-start | bytes 4718592 | tf_op jit(solution)/shard_map/reduce_scatter | solution.py:236
  1655.5 983.9 %reduce-scatter.42.cloned.1.call-start = ((), (), s32[]{:S(2)}) async-start(), calls=%async_computation.37 | async-start | bytes 4718592 | tf_op jit(solution)/shard_map/reduce_scatter | solution.py:236
  1661.1 1069.7 %reduce-scatter.56.cloned.1.call-start = ((), (), s32[]{:S(2)}) async-start(), calls=%async_computation.44 | async-start | bytes 4718592 | tf_op jit(solution)/shard_map/reduce_scatter | solution.py:239
  1668.0 1154.5 %reduce-scatter.54.cloned.1.call-start = ((), (), s32[]{:S(2)}) async-start(), calls=%async_computation.43 | async-start | bytes 4718592 | tf_op jit(solution)/shard_map/reduce_scatter | solution.py:239
  1675.0 1239.1 %reduce-scatter.52.cloned.1.call-start = ((), (), s32[]{:S(2)}) async-start(), calls=%async_computation.42 | async-start | bytes 4718592 | tf_op jit(solution)/shard_map/reduce_scatter | solution.py:239
  1681.9 1323.6 %reduce-scatter.50.cloned.1.call-start = ((), (), s32[]{:S(2)}) async-start(), calls=%async_computation.41 | async-start | bytes 4718592 | tf_op jit(solution)/shard_map/reduce_scatter | solution.py:239
  1688.9 1505.8 %reduce-scatter.32.cloned.1.call-start = ((), (), s32[]{:S(2)}) async-start(), calls=%async_computation.32 | async-start | bytes 17301504 | tf_op jit(solution)/shard_map/reduce_scatter | solution.py:334
  1698.1 1683.8 %reduce-scatter.26.cloned.1.call-start = ((), (), s32[]{:S(2)}) async-start(), calls=%async_computation.29 | async-start | bytes 17301504 | tf_op jit(solution)/shard_map/reduce_scatter | solution.py:331
  1723.6 1845.6 %reduce-scatter.28.cloned.1.call-start = ((), (), s32[]{:S(2)}) async-start(), calls=%async_computation.30 | async-start | bytes 17301504 | tf_op jit(solution)/shard_map/reduce_scatter | solution.py:332
  1739.8 2016.8 %reduce-scatter.30.cloned.1.call-start = ((), (), s32[]{:S(2)}) async-start(), calls=%async_computation.31 | async-start | bytes 17301504 | tf_op jit(solution)/shard_map/reduce_scatter | solution.py:333
  (126 other events, 5151.1 us)
Sparse Core Ops, SparseCore 0:
  11.4 78.9 all-gather.35
  93.8 75.6 all-gather.37
  173.0 75.6 all-gather.31
  323.2 71.3 all-gather.33
  397.9 78.9 all-gather.41
  550.4 71.8 all-gather.65
  772.3 71.3 all-gather.59
  845.6 71.3 all-gather.57
  919.7 71.3 all-gather.49
  993.0 71.3 all-gather.53
  1140.3 71.3 all-gather.43
  1213.6 71.3 all-gather.47
  1286.9 71.3 all-gather.45
  1592.9 87.2 reduce-scatter.57
  1683.7 87.9 reduce-scatter.59
  1773.9 103.6 reduce-scatter.61
  1881.8 116.7 reduce-scatter.39
  2002.3 87.9 reduce-scatter.37
  2093.7 87.9 reduce-scatter.35
  2185.3 87.9 reduce-scatter.33
  2276.7 87.9 reduce-scatter.47
  2368.2 87.9 reduce-scatter.45
  2459.8 87.9 reduce-scatter.43
  2551.4 87.9 reduce-scatter.41
  2642.8 87.9 reduce-scatter.55
  2734.5 87.9 reduce-scatter.53
  2826.1 87.9 reduce-scatter.51
  2917.5 87.9 reduce-scatter.49
  3008.4 186.2 reduce-scatter.31
  3197.5 184.3 reduce-scatter.25
  3384.6 184.6 reduce-scatter.27
  3572.0 184.6 reduce-scatter.29
  (5 shorter events, 351.1 us)
where the time goes:
time: 3770 us; the launch traced here: 3760 us
  waiting for transfers between devices  3030 us (80%)
  matrix products  282 us (7%)
  blocking collectives  178 us (5%)
  local copies, waits for them, and re-layouts  124 us (3%)
  other arithmetic  89.3 us (2%)
  starting transfers between devices  40.5 us (1%)
    reduce_scatter x4, waiting for transfers between devices, on_device(): lax.psum_scatter(gate_grad.astype(jnp.bfloat16), 'dp', scatter_dimension=...  394 us
    reduce_scatter x4, waiting for transfers between devices, on_device(): lax.psum_scatter(down_grad.astype(jnp.bfloat16), 'dp', scatter_dimension=...  362 us
    reduce_scatter x4, waiting for transfers between devices, on_device(): lax.psum_scatter(up_grad.astype(jnp.bfloat16), 'dp', scatter_dimension=0,...  362 us
    all_gather x4, waiting for transfers between devices, on_device(): lax.all_gather(w_down[local_id].astype(jnp.bfloat16), 'dp', axis=0, tiled...  204 us
    all_gather x4, waiting for transfers between devices, on_device(): lax.all_gather(w_up[local_id].astype(jnp.bfloat16), 'dp', axis=0, tiled=T...  204 us
    reduce_scatter x1, waiting for transfers between devices, on_device(): lax.psum_scatter(wv_grad, ('dp', 'expert'), scatter_dimension=0, tiled=True)  187 us
    reduce_scatter x1, waiting for transfers between devices, on_device(): lax.psum_scatter(wk_grad, ('dp', 'expert'), scatter_dimension=0, tiled=True)  187 us
    reduce_scatter x1, waiting for transfers between devices, on_device(): lax.psum_scatter(wq_grad, ('dp', 'expert'), scatter_dimension=0, tiled=True)  187 us
  transfers between devices with their start and end apart: 41, of which 36 were waited for; matrix products, arithmetic and copies ran while one was open for 10% of the time, Pallas kernels for 0%

commit v1 on v0

v1 whole, which is shorter than its diff:
```python
from functools import partial
import math

import jax
import jax.numpy as jnp
from jax import lax
from jax.sharding import PartitionSpec as P

HEADS = 16
HD = 128

norm_eps = 1e-06
rope_base = 10000.0
BF = jnp.bfloat16
F32 = jnp.float32


def rms_scale(features, gain_vec):
    return (
        features
        * lax.rsqrt(jnp.mean(features * features, axis=-1, keepdims=True) + norm_eps)
        * gain_vec
    )


def rotary(features, angles):
    half_dim = features.shape[-1] // 2
    cosine = jnp.cos(angles)[:, None, :]
    sine_part = jnp.sin(angles)[:, None, :]
    front_half = features[..., :half_dim]
    back_half = features[..., half_dim:]
    return jnp.concatenate(
        [front_half * cosine - back_half * sine_part, back_half * cosine + front_half * sine_part],
        axis=-1,
    )


def head_piece(angles, flat_vals, gain_vec):
    count = flat_vals.shape[0]
    shaped = flat_vals.reshape(count, -1, HD)
    return rotary(rms_scale(shaped, gain_vec), angles)


def dot(left_mat, right_mat):
    return jnp.dot(left_mat, right_mat, preferred_element_type=F32)


def dot_rows(left_mat, right_mat):
    return lax.dot_general(
        left_mat, right_mat, (((0,), (0,)), ((), ())), preferred_element_type=F32
    )


def dot_t(left_mat, right_mat):
    return lax.dot_general(
        left_mat, right_mat, (((1,), (1,)), ((), ())), preferred_element_type=F32
    )


BOTH = ("dp", "expert")


def swap(blocks, axes):
    return lax.all_to_all(blocks, axes, split_axis=0, concat_axis=0, tiled=True)


def gather(shard, axes):
    return lax.all_gather(shard, axes, axis=0, tiled=True)


def scatter(partial_sum, axes):
    return lax.psum_scatter(partial_sum, axes, scatter_dimension=0, tiled=True)


def on_device(
    tokens,
    cotangent,
    lengths,
    piece_order,
    routes,
    attn_gain,
    w_query,
    w_key,
    w_value,
    w_output,
    query_gain,
    key_gain,
    moe_gain,
    w_router,
    w_gate,
    w_up,
    w_down,
):
    rows, width = tokens.shape
    seq_id = lax.axis_index("expert")
    n_dp = lax.axis_size("dp")
    n_ex = lax.axis_size("expert")
    n_all = n_dp * n_ex
    local_count, _, ff = w_gate.shape
    expert_total = local_count * n_ex
    ff_part = ff // n_dp
    cols = width // n_dp
    wrows = w_query.shape[0]
    score_scale = 1.0 / math.sqrt(HD)

    gains = jnp.concatenate([attn_gain, moe_gain, query_gain, key_gain])
    gains_all = swap(jnp.broadcast_to(gains, (n_all, gains.shape[0])), BOTH)
    gw, hw = attn_gain.shape[0], query_gain.shape[0]
    gain_one = gains_all[:, :gw].reshape(-1)
    gain_two = gains_all[:, gw : 2 * gw].reshape(-1)
    gain_q = gains_all[:, 2 * gw : 2 * gw + hw].reshape(-1)
    gain_k = gains_all[:, 2 * gw + hw :].reshape(-1)

    seq_tokens = gather(tokens, "dp")
    qkv = jnp.stack([w_query, w_key, w_value]).astype(BF).reshape(3, wrows, n_dp, cols)
    qkv = swap(qkv.transpose(2, 1, 0, 3), "dp")
    qkv = gather(qkv.reshape(1, n_dp, wrows, 3 * cols), "expert")
    qkv = qkv.transpose(1, 0, 2, 3).reshape(width, 3 * cols)
    wo_all = gather(w_output.astype(BF), BOTH)
    wr_all = swap(
        jnp.broadcast_to(w_router.astype(BF).T, (n_all, expert_total, wrows)), BOTH
    )
    wr_all = wr_all.transpose(1, 0, 2).reshape(expert_total, width)
    w1 = jnp.stack([w_gate, w_up]).astype(BF).reshape(2, local_count, cols, n_dp, ff_part)
    w1 = swap(w1.transpose(3, 2, 0, 1, 4).reshape(n_dp, cols, -1), "dp").reshape(width, -1)
    w2 = w_down.astype(BF).reshape(local_count * ff_part, width)
    half = local_count * ff_part
    dy_all = gather(cotangent, BOTH)

    seq_in = seq_tokens.astype(F32)
    normed_one = rms_scale(seq_in, gain_one).astype(BF)
    qkv_flat = dot(normed_one, qkv)
    offsets = jnp.arange(rows, dtype=jnp.int32)
    position = (piece_order[seq_id][:, None] * rows + offsets[None, :]).reshape(-1)
    visible = position < lengths[seq_id]
    half_dim = HD // 2
    frequency = rope_base ** (-(jnp.arange(half_dim, dtype=F32) * 2.0 / HD))
    angles = position.astype(F32)[:, None] * frequency[None, :]
    query_rot, query_back = jax.vjp(partial(head_piece, angles), qkv_flat[:, :cols], gain_q)
    key_rot, key_back = jax.vjp(partial(head_piece, angles), qkv_flat[:, cols : 2 * cols], gain_k)
    query_bf = query_rot.astype(BF)
    key_bf = key_rot.astype(BF)
    value_bf = qkv_flat[:, 2 * cols :].astype(BF).reshape(-1, cols // HD, HD)
    scores = (
        jnp.einsum("qhd,khd->hqk", query_bf, key_bf, preferred_element_type=F32) * score_scale
    )
    scores = jnp.where(visible[None, None, :], scores, -jnp.inf)
    probs = jax.nn.softmax(scores, axis=-1)
    probs_bf = probs.astype(BF)
    attended = jnp.einsum("hqk,khd->qhd", probs_bf, value_bf, preferred_element_type=F32)
    attended = swap(attended.astype(BF).reshape(n_dp, rows, cols), "dp")
    attended = attended.transpose(1, 0, 2).reshape(rows, width)

    inputs = tokens.astype(F32)
    hidden_one = inputs + dot(attended, wo_all)
    normed_two = rms_scale(hidden_one, gain_two).astype(BF)
    router_logits = dot_t(normed_two, wr_all)
    expert_ids = jnp.arange(expert_total, dtype=jnp.int32)
    routed = jnp.any(routes[:, :, None] == expert_ids[None, None, :], axis=1)
    masked_logits = jnp.where(routed, router_logits, -jnp.inf)
    gates = jax.nn.softmax(masked_logits, axis=-1)
    gate_blocks = jnp.broadcast_to(
        gates.T.reshape(1, n_ex, local_count, rows), (n_dp, n_ex, local_count, rows)
    ).reshape(n_all, local_count, rows)
    my_gates = swap(gate_blocks, BOTH).transpose(0, 2, 1).reshape(n_all * rows, local_count)

    n2_all = gather(normed_two, BOTH)
    hidden_pre = dot(n2_all, w1)
    gate_val = hidden_pre[:, :half]
    up_val = hidden_pre[:, half:]
    wide_gates = jnp.repeat(my_gates, ff_part, axis=1)
    sig = jax.nn.sigmoid(gate_val)
    silu = gate_val * sig
    inner = (silu * up_val).astype(BF).astype(F32)
    gated_inner = (wide_gates * inner).astype(BF)
    back_inner = dot_t(dy_all, w2)
    gate_grads = jnp.sum(
        (inner * back_inner).reshape(-1, local_count, ff_part), axis=-1
    )
    inner_grad = wide_gates * back_inner
    pre_grad = jnp.concatenate(
        [inner_grad * up_val * sig * (1.0 + gate_val * (1.0 - sig)), inner_grad * silu], axis=1
    ).astype(BF)
    row_grads = dot_t(pre_grad, w1).astype(BF)
    token_grads = scatter(row_grads, BOTH).astype(F32)
    mixture = dot(gated_inner, w2).astype(BF)
    mixture, token_grads = lax.optimization_barrier((mixture, token_grads))
    mixed = scatter(mixture, BOTH).astype(F32)
    block_out = (hidden_one + mixed).astype(BF)
    down_grad = dot_rows(gated_inner, dy_all).reshape(local_count, ff_part, width)
    w1_grad = dot_rows(n2_all, pre_grad).astype(BF)
    w1_grad = swap(w1_grad.reshape(n_dp, cols, -1), "dp")
    w1_grad = (
        w1_grad.reshape(n_dp, cols, 2, local_count, ff_part)
        .transpose(2, 3, 1, 0, 4)
        .reshape(2, local_count, cols, ff)
        .astype(F32)
    )

    gg = swap(gate_grads.reshape(n_all, rows, local_count).transpose(0, 2, 1), BOTH)
    gg = gg.reshape(n_dp, n_ex, local_count, rows).sum(axis=0).reshape(expert_total, rows).T
    weighted = gates * gg
    logit_bf = (weighted - gates * jnp.sum(weighted, axis=-1, keepdims=True)).astype(BF)
    router_grad = dot_rows(normed_two, logit_bf)
    normed_two_grad = token_grads + dot(logit_bf, wr_all)
    _, norm_two_back = jax.vjp(rms_scale, hidden_one, gain_two)
    hidden_part, norm_two_grad = norm_two_back(normed_two_grad)
    hidden_grad = cotangent.astype(F32) + hidden_part
    attn_grad_bf = hidden_grad.astype(BF)
    output_grad = scatter(dot_rows(attended, attn_grad_bf).astype(BF), BOTH).astype(F32)
    attended_grad = dot_t(attn_grad_bf, wo_all).astype(BF)
    attended_grad = swap(attended_grad.reshape(rows, n_dp, cols).transpose(1, 0, 2), "dp")
    attended_grad = attended_grad.reshape(-1, cols // HD, HD)

    prob_grad = jnp.einsum("qhd,khd->hqk", attended_grad, value_bf, preferred_element_type=F32)
    score_grad = (
        probs * (prob_grad - jnp.sum(probs * prob_grad, axis=-1, keepdims=True))
    ).astype(BF)
    query_grad = (
        jnp.einsum("hqk,khd->qhd", score_grad, key_bf, preferred_element_type=F32) * score_scale
    )
    key_grad = (
        jnp.einsum("hqk,qhd->khd", score_grad, query_bf, preferred_element_type=F32) * score_scale
    )
    value_grad = jnp.einsum("hqk,qhd->khd", probs_bf, attended_grad, preferred_element_type=F32)
    query_flat_grad, query_gain_grad = query_back(query_grad)
    key_flat_grad, key_gain_grad = key_back(key_grad)
    qkv_grad = jnp.concatenate(
        [query_flat_grad.astype(BF), key_flat_grad.astype(BF), value_grad.reshape(-1, cols).astype(BF)],
        axis=1,
    )
    part_grad = dot_t(qkv_grad, qkv)
    seq_scale = lax.rsqrt(jnp.mean(seq_in * seq_in, axis=-1, keepdims=True) + norm_eps)
    norm_one_grad = jnp.sum(part_grad * (seq_in * seq_scale), axis=0)
    normed_one_grad = scatter(part_grad.astype(BF), "dp").astype(F32)
    _, norm_one_back = jax.vjp(lambda v: rms_scale(v, gain_one), inputs)
    (input_part,) = norm_one_back(normed_one_grad)
    grad_tokens = (hidden_grad + input_part).astype(BF)
    qkv_w = dot_rows(normed_one, qkv_grad).astype(BF)
    qkv_w = qkv_w.reshape(n_dp, n_ex, wrows, 3 * cols).transpose(1, 0, 2, 3)
    qkv_w = swap(qkv_w, "expert").astype(F32).sum(axis=0).astype(BF)
    qkv_w = swap(qkv_w, "dp").reshape(n_dp, wrows, 3, cols).transpose(2, 1, 0, 3)
    qkv_w = qkv_w.reshape(3, wrows, width).astype(F32)

    small = jnp.concatenate(
        [
            norm_one_grad.reshape(n_all, -1),
            norm_two_grad.reshape(n_all, -1),
            query_gain_grad.reshape(n_all, -1),
            key_gain_grad.reshape(n_all, -1),
            router_grad.reshape(n_all, -1),
        ],
        axis=1,
    )
    small = jnp.sum(swap(small, BOTH).reshape(n_all, -1), axis=0)
    return (
        block_out,
        grad_tokens,
        small[:gw],
        qkv_w[0],
        qkv_w[1],
        qkv_w[2],
        output_grad,
        small[2 * gw : 2 * gw + hw],
        small[2 * gw + hw : 2 * gw + 2 * hw],
        small[gw : 2 * gw],
        small[2 * gw + 2 * hw :].reshape(wrows, expert_total),
        w1_grad[0],
        w1_grad[1],
        down_grad,
    )


def solution(mesh):
    rows2 = P(("dp", "expert"), None)
    rows1 = P(("dp", "expert"))
    experts = P("expert", "dp", None)
    return jax.shard_map(
        on_device,
        mesh=mesh,
        in_specs=(rows2, rows2, P(), P(), rows2, rows1, rows2, rows2, rows2, rows2)
        + (rows1, rows1, rows1, rows2, experts, experts, experts),
        out_specs=(rows2, rows2, rows1, rows2, rows2, rows2, rows2)
        + (rows1, rows1, rows1, rows2, experts, experts, experts),
        check_vma=False,
    )
```

time: 3770 us -> 1370 us (0.36)
  waiting for transfers between devices: 3030 us -> 896 us
  blocking collectives: 178 us -> 48.3 us
  matrix products: 282 us -> 190 us
  local copies, waits for them, and re-layouts: 124 us -> 83.7 us
    reduce_scatter x16 -> x4, waiting for transfers between devices: 1810 us -> 377 us  [scatter(): return lax.psum_scatter(partial_sum, axes, scatter_dimension=0, tiled=True)]
    all_gather x18 -> x5, waiting for transfers between devices: 918 us -> 207 us  [gather(): return lax.all_gather(shard, axes, axis=0, tiled=True)]
    all_to_all x4 -> x9, waiting for transfers between devices: 176 us -> 310 us  [swap(): return lax.all_to_all(blocks, axes, split_axis=0, concat_axis=0, tiled=True)]
    unnamed x40 -> x9, waiting for transfers between devices: 133 us -> 1.34 us
    dot_general x56 -> x19, matrix products: 272 us -> 176 us  [the longest x5 62.2 us: dot_t(): lax.dot_general(left_mat, right_mat, (((1,), (1,)), ((), ())), preferred_...]
    all_gather x1 -> x0, blocking collectives: 93.9 us -> none  [on_device(): lax.all_gather(w_router.astype(jnp.bfloat16), ('dp', 'expert'), axis=0, t...]
    unnamed x2 -> x0, blocking collectives: 83.9 us -> none
    all_to_all x0 -> x3, blocking collectives: none -> 48.3 us  [swap(): return lax.all_to_all(blocks, axes, split_axis=0, concat_axis=0, tiled=True)]
  transfers between devices with their start and end apart: 41 -> 18, of which waited for: 36 -> 14; matrix products, arithmetic and copies ran while one was open for 10% -> 16% of each run, Pallas kernels for 0% -> 0%
where the time goes in v1:
time: 1370 us; the launch traced here: 1350 us
  waiting for transfers between devices  896 us (65%)
  matrix products  190 us (14%)
  local copies, waits for them, and re-layouts  83.7 us (6%)
  other arithmetic  57.9 us (4%)
  starting transfers between devices  54.3 us (4%)
  blocking collectives  48.3 us (4%)
  between operations  15.4 us (1%)
    reduce_scatter x4, waiting for transfers between devices, scatter(): return lax.psum_scatter(partial_sum, axes, scatter_dimension=0, tiled=True)  377 us
    all_to_all x9, waiting for transfers between devices, swap(): return lax.all_to_all(blocks, axes, split_axis=0, concat_axis=0, tiled=True)  310 us
    all_gather x5, waiting for transfers between devices, gather(): return lax.all_gather(shard, axes, axis=0, tiled=True)  207 us
    dot_general x5, matrix products, dot_t(): lax.dot_general(left_mat, right_mat, (((1,), (1,)), ((), ())), preferred_...  62.2 us
    all_to_all x9, starting transfers between devices, swap(): return lax.all_to_all(blocks, axes, split_axis=0, concat_axis=0, tiled=True)  53.6 us
    dot_general x5, matrix products, dot_rows(): lax.dot_general(left_mat, right_mat, (((0,), (0,)), ((), ())), preferred_...  51.3 us
    dot_general x5, matrix products, dot(): return jnp.dot(left_mat, right_mat, preferred_element_type=F32)  50.5 us
    all_to_all x3, blocking collectives, swap(): return lax.all_to_all(blocks, axes, split_axis=0, concat_axis=0, tiled=True)  48.3 us
  transfers between devices with their start and end apart: 18, of which 14 were waited for; matrix products, arithmetic and copies ran while one was open for 16% of the time, Pallas kernels for 0%

profile of v1, /device:TPU:13, one launch (start us, length us, event | category | flops | bytes accessed | tf_op | source)
XLA Modules:
  0.0 1345.7 jit_solution(15329309357172275781)
XLA Ops:
  11.1 22.6 %all_to_all.68 = bf16[8,64,3,256]{3,1,2,0:T(8,128)(2,1)S(1)} all-to-all(bf16[8,64,3,256]{3,1,2,0:T(8,128)(2,1)S(1)} %copy.192), channel_id=1, replica_groups=mesh['dp'=8,'expert'=4] {'dp'}, dimensions={0} | all-to-all | bytes 1572864 | tf_op jit(solution)/shard_map/all_to_all | solution.py:64
  38.4 7.5 all-to-all-start
  51.4 16.1 %all-gather.8.cloned.1.call-done = bf16[4,8,64,768]{3,2,1,0:T(8,128)(2,1)} async-done(((bf16[1,8,64,768]{3,2,1,0:T(8,128)(2,1)}), bf16[4,8,64,768]{3,2,1,0:T(8,128)(2,1)}) %all-gather.8.cloned.1.call-update) | async-done | bytes 3145744 | tf_op jit(solution)/shard_map/all_gather | solution.py:68
  71.3 67.7 %all-gather.6.cloned.1.call-done = bf16[1024,2048]{1,0:T(8,128)(2,1)} async-done(((bf16[128,2048]{1,0:T(8,128)(2,1)}), bf16[1024,2048]{1,0:T(8,128)(2,1)}) %all-gather.6.cloned.1.call-update) | async-done | bytes 4194320 | tf_op jit(solution)/shard_map/all_gather | solution.py:68
  142.1 6.6 fusion.27
  159.4 8.1 fusion.65
  172.7 6.2 all-to-all-start.2
  179.5 15.7 %all-to-all-done.2 = bf16[8,128,256]{1,2,0:T(8,128)(2,1)S(1)} async-done(((bf16[8,128,256]{1,2,0:T(8,128)(2,1)}), bf16[8,128,256]{1,2,0:T(8,128)(2,1)S(1)}, u32[]{:S(2)}, u32[]{:S(2)}) %all-to-all-start.2) | async-done | bytes 524320 | tf_op jit(solution)/shard_map/all_to_all | solution.py:64
  195.2 32.1 %all-gather.10.cloned.1.call-done = bf16[2048,2048]{1,0:T(8,128)(2,1)} async-done(((bf16[64,2048]{1,0:T(8,128)(2,1)}), bf16[2048,2048]{1,0:T(8,128)(2,1)}) %all-gather.10.cloned.1.call-update) | async-done | bytes 8388624 | tf_op jit(solution)/shard_map/all_gather | solution.py:68
  259.8 154.5 %all-to-all-done.5 = bf16[8,256,1024]{1,2,0:T(8,128)(2,1)} async-done(((bf16[8,256,1024]{1,2,0:T(8,128)(2,1)}), bf16[8,256,1024]{1,2,0:T(8,128)(2,1)}, u32[]{:S(2)}, u32[]{:S(2)}) %all-to-all-start.5) | async-done | bytes 4194336 | tf_op jit(solution)/shard_map/all_to_all | solution.py:64
  414.2 6.4 copy.203
  420.7 23.7 %fusion.67 = f32[4096,1024]{0,1:T(8,128)} fusion(bf16[4096,2048]{1,0:T(8,128)(2,1)} %all-gather.12.cloned.1.call-done, bf16[2048,1024]{1,0:T(8,128)(2,1)} %bitcast.149), kind=kOutput, calls=%fused_computation.145 | convolution fusion | flops 17179869184 | bytes 37748736 | tf_op jit(solution)/shard_map/dot_general | solution.py:45
  444.3 91.5 %all-gather.14.cloned.1.call-done = bf16[4096,2048]{1,0:T(8,128)(2,1)} async-done(((bf16[128,2048]{1,0:T(8,128)(2,1)}), bf16[4096,2048]{1,0:T(8,128)(2,1)}) %all-gather.14.cloned.1.call-update) | async-done | bytes 16777232 | tf_op jit(solution)/shard_map/all_gather | solution.py:68
  535.9 21.5 %bitcast_reduce_fusion = (f32[4096,4]{0,1:T(4,128)}, bf16[4096,512]{0,1:T(8,128)(2,1)}, f32[4096,512]{0,1:T(8,128)}) fusion(f32[4096,1024]{0,1:T(8,128)} %fusion.67, bf16[4096,2048]{1,0:T(8,128)(2,1)} %all-gather.14.cloned.1.call-done, bf16[512,2048]{1,0:T(8,128)(2,1)S(1)} %bitcast.157), kind=kOutput, calls=%fused_computation.15 | convolution fusion | flops 8608792576 | bytes 48300032 | tf_op jit(solution)/shard_map/dot_general | solution.py:55
  566.6 9.3 all_to_all.69
  575.9 16.9 %multiply_convert_fusion.2 = (bf16[4096,512]{0,1:T(8,128)(2,1)}, bf16[4096,512]{0,1:T(8,128)(2,1)}, bf16[4096,512]{0,1:T(8,128)(2,1)}) fusion(f32[4096,512]{0,1:T(8,128)} %get-tuple-element.145, f32[4096,1024]{0,1:T(8,128)} %fusion.67, f32[4096,4]{0,1:T(4,128)S(1)} %bitcast.184, bf16[4096,512]{0,1:T(8,128)(2,1)} %get-tuple-element.102), kind=kLoop, calls=%fused_computation.20 | loop fusion | flops 35651584 | bytes 42008576 | tf_op jit(solution)/shard_map/convert.5
  592.8 25.4 %convolution_convert_fusion = bf16[4096,2048]{1,0:T(8,128)(2,1)} fusion(bf16[2048,1024]{1,0:T(8,128)(2,1)} %bitcast.150, bf16[4096,512]{0,1:T(8,128)(2,1)} %get-tuple-element.104, bf16[4096,512]{0,1:T(8,128)(2,1)} %get-tuple-element.103), kind=kOutput, calls=%fused_computation.1 | convolution fusion | flops 17205035008 | bytes 29360128 | tf_op jit(solution)/shard_map/dot_general | solution.py:55
  618.3 14.9 %convolution_convert_fusion.1 = bf16[4096,2048]{1,0:T(8,128)(2,1)} fusion(bf16[4096,512]{0,1:T(8,128)(2,1)} %get-tuple-element.128, bf16[512,2048]{1,0:T(8,128)(2,1)S(1)} %bitcast.158), kind=kOutput, calls=%fused_computation.2 | convolution fusion | flops 8598323200 | bytes 23068672 | tf_op jit(solution)/shard_map/dot_general | solution.py:45
  633.2 168.2 %reduce-scatter.5.cloned.1.call-done = bf16[128,2048]{1,0:T(8,128)(2,1)} async-done(((bf16[4096,2048]{1,0:T(8,128)(2,1)}), bf16[128,2048]{1,0:T(8,128)(2,1)}) %reduce-scatter.5.cloned.1.call-update) | async-done | bytes 524304 | tf_op jit(solution)/shard_map/reduce_scatter | solution.py:72
  804.3 184.0 %reduce-scatter.7.cloned.1.call-done = bf16[128,2048]{1,0:T(8,128)(2,1)} async-done(((bf16[4096,2048]{1,0:T(8,128)(2,1)}), bf16[128,2048]{1,0:T(8,128)(2,1)}) %reduce-scatter.7.cloned.1.call-update) | async-done | bytes 524304 | tf_op jit(solution)/shard_map/reduce_scatter | solution.py:72
  990.7 6.3 convolution_convert_fusion.4
  997.2 16.5 %all_to_all.70 = bf16[8,128,256]{1,2,0:T(8,128)(2,1)S(1)} all-to-all(bf16[8,128,256]{1,2,0:T(8,128)(2,1)S(1)} %bitcast.160), channel_id=1, replica_groups=mesh['dp'=8,'expert'=4] {'dp'}, dimensions={0} | all-to-all | bytes 1048576 | tf_op jit(solution)/shard_map/all_to_all | solution.py:64
  1036.4 8.8 fusion.4
  1050.9 24.3 %fusion.13 = bf16[2048,1024]{1,0:T(8,128)(2,1)} fusion(bf16[4096,2048]{1,0:T(8,128)(2,1)} %all-gather.12.cloned.1.call-done, bf16[4096,512]{0,1:T(8,128)(2,1)} %get-tuple-element.104, bf16[4096,512]{0,1:T(8,128)(2,1)} %get-tuple-element.103), kind=kOutput, calls=%fused_computation.34 | convolution fusion | flops 17198743552 | bytes 29360128 | tf_op jit(solution)/shard_map/dot_general | solution.py:49
  1075.2 7.0 all-to-all-start.11
  1090.2 86.6 %all-to-all-done.11 = bf16[8,256,1024]{2,1,0:T(8,128)(2,1)} async-done(((bf16[8,256,1024]{2,1,0:T(8,128)(2,1)}), bf16[8,256,1024]{2,1,0:T(8,128)(2,1)}, u32[]{:S(2)}, u32[]{:S(2)}) %all-to-all-start.11) | async-done | bytes 4194336 | tf_op jit(solution)/shard_map/all_to_all | solution.py:64
  1184.2 43.6 %all-to-all-done.9 = bf16[4,8,64,768]{3,2,1,0:T(8,128)(2,1)} async-done(((bf16[4,8,64,768]{3,2,1,0:T(8,128)(2,1)}), bf16[4,8,64,768]{3,2,1,0:T(8,128)(2,1)}, u32[]{:S(2)}, u32[]{:S(2)}) %all-to-all-start.9) | async-done | bytes 3145760 | tf_op jit(solution)/shard_map/all_to_all | solution.py:64
  1227.7 9.0 all-to-all-start.8
  1250.2 15.0 %fusion.69 = f32[512,2048]{1,0:T(8,128)} fusion(bf16[4096,512]{0,1:T(8,128)(2,1)} %get-tuple-element.128, bf16[4096,2048]{1,0:T(8,128)(2,1)} %all-gather.14.cloned.1.call-done), kind=kOutput, calls=%fused_computation.147 | convolution fusion | flops 8589934592 | bytes 25165824 | tf_op jit(solution)/shard_map/dot_general | solution.py:49
  1265.3 8.9 reshape.380
  1274.2 8.3 copy.253
  1312.5 24.5 %reduce-scatter.11.cloned.1.call-done = bf16[64,2048]{1,0:T(8,128)(2,1)} async-done(((bf16[2048,2048]{1,0:T(8,128)(2,1)}), bf16[64,2048]{1,0:T(8,128)(2,1)}) %reduce-scatter.11.cloned.1.call-update) | async-done | bytes 262160 | tf_op jit(solution)/shard_map/reduce_scatter | solution.py:72
  (263 shorter events, 172.6 us)
Async XLA Ops:
  7.2 30.5 %copy-start.52 = (f32[64]{0:T(128)S(1)}, f32[64]{0:T(128)}, u32[]{:S(2)}) copy-start(f32[64]{0:T(128)} %param.29) | copy-start | bytes 772
  7.2 30.5 %copy-start.50 = (f32[4]{0:T(128)S(1)}, f32[4]{0:T(128)}, u32[]{:S(2)}) copy-start(f32[4]{0:T(128)} %param.28) | copy-start | bytes 52
  7.2 30.5 %copy-start.51 = (f32[4]{0:T(128)S(1)}, f32[4]{0:T(128)}, u32[]{:S(2)}) copy-start(f32[4]{0:T(128)} %param.27) | copy-start | bytes 52
  7.2 30.5 %copy-start.53 = (f32[64]{0:T(128)S(1)}, f32[64]{0:T(128)}, u32[]{:S(2)}) copy-start(f32[64]{0:T(128)} %param.22) | copy-start | bytes 772
  7.2 38.7 %copy-start.54 = (s32[4]{0:T(128)S(1)}, s32[4]{0:T(128)}, u32[]{:S(2)}) copy-start(s32[4]{0:T(128)} %param.19) | copy-start | bytes 52
  7.2 60.2 %all-gather.8.cloned.1.call-start = ((), (), s32[]{:S(2)}) async-start(), calls=%async_computation.17 | async-start | bytes 3932160 | tf_op jit(solution)/shard_map/all_gather | solution.py:68
  36.1 102.9 %all-gather.6.cloned.1.call-start = ((), (), s32[]{:S(2)}) async-start(), calls=%async_computation.16 | async-start | bytes 4718592 | tf_op jit(solution)/shard_map/all_gather | solution.py:68
  36.9 190.4 %all-gather.10.cloned.1.call-start = ((), (), s32[]{:S(2)}) async-start(), calls=%async_computation.18 | async-start | bytes 8650752 | tf_op jit(solution)/shard_map/all_gather | solution.py:68
  38.4 12.5 all-to-all-start
  49.2 108.2 %copy-start.13 = (f32[1024,64]{1,0:T(8,128)}, f32[1024,64]{1,0:T(8,128)S(1)}, u32[]{:S(2)}) copy-start(f32[1024,64]{1,0:T(8,128)S(1)} %get-tuple-element.137) | copy-start | bytes 786436
  49.2 108.2 %copy-start.15 = (f32[1024,64]{1,0:T(8,128)}, f32[1024,64]{1,0:T(8,128)S(1)}, u32[]{:S(2)}) copy-start(f32[1024,64]{1,0:T(8,128)S(1)} %get-tuple-element.138) | copy-start | bytes 786436
  51.1 105.8 %copy-start.41 = (f32[128]{0:T(128)}, f32[128]{0:T(128)S(1)}, u32[]{:S(2)}) copy-start(f32[128]{0:T(128)S(1)} %mul.447) | copy-start | bytes 1540
  51.2 104.8 %copy-start.39 = (f32[128]{0:T(128)}, f32[128]{0:T(128)S(1)}, u32[]{:S(2)}) copy-start(f32[128]{0:T(128)S(1)} %mul.462) | copy-start | bytes 1540
  51.4 97.3 %copy-start.30 = (f32[2048]{0:T(1024)}, f32[2048]{0:T(1024)S(1)}, u32[]{:S(2)}) copy-start(f32[2048]{0:T(1024)S(1)} %mul.439) | copy-start | bytes 24580
  167.5 59.7 %copy-start.8 = (bf16[128,2048]{1,0:T(8,128)(2,1)S(1)}, bf16[128,2048]{1,0:T(8,128)(2,1)}, u32[]{:S(2)}) copy-start(bf16[128,2048]{1,0:T(8,128)(2,1)} %param.17) | copy-start | bytes 1572868
  172.7 22.5 %all-to-all-start.2 = ((bf16[8,128,256]{1,2,0:T(8,128)(2,1)}), bf16[8,128,256]{1,2,0:T(8,128)(2,1)S(1)}, u32[]{:S(2)}, u32[]{:S(2)}) async-start(bf16[8,128,256]{1,2,0:T(8,128)(2,1)} %copy.198), calls=%async_computation.2 | async-start | bytes 1048576 | tf_op jit(solution)/shard_map/all_to_all | solution.py:64
  179.0 241.7 %all-gather.12.cloned.1.call-start = ((), (), s32[]{:S(2)}) async-start(), calls=%async_computation.19 | async-start | bytes 17301504 | tf_op jit(solution)/shard_map/all_gather | solution.py:68
  179.4 53.1 %copy-start.28 = (f32[2048]{0:T(1024)}, f32[2048]{0:T(1024)S(1)}, u32[]{:S(2)}) copy-start(f32[2048]{0:T(1024)S(1)} %mul.474) | copy-start | bytes 24580
  195.2 36.8 %copy-start.6 = (bf16[8,128,256]{1,2,0:T(8,128)(2,1)}, bf16[8,128,256]{1,2,0:T(8,128)(2,1)S(1)}, u32[]{:S(2)}) copy-start(bf16[8,128,256]{1,2,0:T(8,128)(2,1)S(1)} %all-to-all-done.2) | copy-start | bytes 1572868
  234.0 301.8 %all-gather.14.cloned.1.call-start = ((), (), s32[]{:S(2)}) async-start(), calls=%async_computation.20 | async-start | bytes 17301504 | tf_op jit(solution)/shard_map/all_gather | solution.py:68
  235.4 15.8 %all-to-all-start.3 = ((bf16[32,2,512]{2,1,0:T(2,128)(2,1)}), bf16[32,2,512]{2,1,0:T(2,128)(2,1)S(1)}, u32[]{:S(2)}, u32[]{:S(2)}) async-start(bf16[32,2,512]{2,1,0:T(2,128)(2,1)} %reshape.381), calls=%async_computation.3 | async-start | bytes 131072 | tf_op jit(solution)/shard_map/all_to_all | solution.py:64
  251.2 163.0 %all-to-all-start.5 = ((bf16[8,256,1024]{1,2,0:T(8,128)(2,1)}), bf16[8,256,1024]{1,2,0:T(8,128)(2,1)}, u32[]{:S(2)}, u32[]{:S(2)}) async-start(bf16[8,256,1024]{1,2,0:T(8,128)(2,1)} %bitcast.140), calls=%async_computation.5 | async-start | bytes 8388608 | tf_op jit(solution)/shard_map/all_to_all | solution.py:64
  557.4 9.1 all-to-all-start.6
  561.2 240.2 %reduce-scatter.5.cloned.1.call-start = ((), (), s32[]{:S(2)}) async-start(), calls=%async_computation.21 | async-start | bytes 17301504 | tf_op jit(solution)/shard_map/reduce_scatter | solution.py:72
  618.2 370.1 %reduce-scatter.7.cloned.1.call-start = ((), (), s32[]{:S(2)}) async-start(), calls=%async_computation.22 | async-start | bytes 17301504 | tf_op jit(solution)/shard_map/reduce_scatter | solution.py:72
  802.6 506.3 %reduce-scatter.9.cloned.1.call-start = ((), (), s32[]{:S(2)}) async-start(), calls=%async_computation.23 | async-start | bytes 4718592 | tf_op jit(solution)/shard_map/reduce_scatter | solution.py:72
  1045.2 291.9 %reduce-scatter.11.cloned.1.call-start = ((), (), s32[]{:S(2)}) async-start(), calls=%async_computation.24 | async-start | bytes 8650752 | tf_op jit(solution)/shard_map/reduce_scatter | solution.py:72
  1075.2 101.6 %all-to-all-start.11 = ((bf16[8,256,1024]{2,1,0:T(8,128)(2,1)}), bf16[8,256,1024]{2,1,0:T(8,128)(2,1)}, u32[]{:S(2)}, u32[]{:S(2)}) async-start(bf16[8,256,1024]{2,1,0:T(8,128)(2,1)} %bitcast.151), calls=%async_computation.15 | async-start | bytes 8388608 | tf_op jit(solution)/shard_map/all_to_all | solution.py:64
  1088.3 93.6 %copy-start.11 = (bf16[128,2048]{1,0:T(8,128)(2,1)S(1)}, bf16[128,2048]{1,0:T(8,128)(2,1)}, u32[]{:S(2)}) copy-start(bf16[128,2048]{1,0:T(8,128)(2,1)} %multiply_convert_fusion.4) | copy-start | bytes 1572868
  1176.8 51.0 %all-to-all-start.9 = ((bf16[4,8,64,768]{3,2,1,0:T(8,128)(2,1)}), bf16[4,8,64,768]{3,2,1,0:T(8,128)(2,1)}, u32[]{:S(2)}, u32[]{:S(2)}) async-start(bf16[4,8,64,768]{3,2,1,0:T(8,128)(2,1)} %bitcast.141), calls=%async_computation.12 | async-start | bytes 6291456 | tf_op jit(solution)/shard_map/all_to_all | solution.py:64
  1227.7 16.6 %all-to-all-start.8 = ((f32[32,1,1160]{2,1,0:T(1,128)}), f32[32,1,1160]{2,1,0:T(1,128)S(1)}, u32[]{:S(2)}, u32[]{:S(2)}) async-start(f32[32,1,1160]{2,1,0:T(1,128)} %copy.223), calls=%async_computation.11 | async-start | bytes 327680 | tf_op jit(solution)/shard_map/all_to_all | solution.py:64
  1244.3 54.0 %all-to-all-start.10 = ((bf16[8,64,768]{2,1,0:T(8,128)(2,1)}), bf16[8,64,768]{2,1,0:T(8,128)(2,1)S(1)}, u32[]{:S(2)}, u32[]{:S(2)}) async-start(bf16[8,64,768]{2,1,0:T(8,128)(2,1)} %reduce_sum.248), calls=%async_computation.13 | async-start | bytes 1572864 | tf_op jit(solution)/shard_map/all_to_all | solution.py:64
  (44 other events, 265.0 us)
Sparse Core Ops, SparseCore 0:
  36.2 31.1 all-gather.7
  69.6 69.3 all-gather.5
  142.4 84.7 all-gather.9
  234.2 180.9 all-gather.11
  417.8 117.9 all-gather.13
  618.3 183.0 reduce-scatter.4
  803.7 184.5 reduce-scatter.6
  1045.3 154.3 reduce-scatter.8
  1202.0 134.9 reduce-scatter.10

commit v2 on v1

--- a/solution.py
+++ b/solution.py
@@ -4,9 +4,10 @@
 import jax
 import jax.numpy as jnp
 from jax import lax
+from jax.experimental import pallas as pl
 from jax.sharding import PartitionSpec as P
 
-HEADS = 16
+
 HD = 128
 
 norm_eps = 1e-06
@@ -70,6 +71,205 @@
 
 def scatter(partial_sum, axes):
     return lax.psum_scatter(partial_sum, axes, scatter_dimension=0, tiled=True)
+
+
+def ring_order(size):
+    return list(range(0, size, 2)) + list(range(1, size, 2))[::-1]
+
+
+def ring_perm(n_dp, steps):
+    order = ring_order(n_dp // 2)
+    size = len(order)
+    pairs = []
+    for spot in range(size):
+        for inner in range(2):
+            target = order[(spot + steps) % size]
+            pairs.append((order[spot] * 2 + inner, target * 2 + inner))
+    return pairs
+
+
+def ring_shift(vals, steps):
+    return lax.ppermute(vals, "dp", ring_perm(lax.axis_size("dp"), steps))
+
+
+def flip(vals, axis, bit):
+    size = lax.axis_size(axis)
+    return lax.ppermute(vals, axis, [(i, i ^ bit) for i in range(size)])
+
+
+def core_flip(vals):
+    return flip(vals, "expert", 1)
+
+
+def cross(vals, inner, bits):
+    if inner == 0:
+        return flip(vals, "expert", bits)
+    if bits == 0:
+        return flip(vals, "dp", 1)
+    n_ex = lax.axis_size("expert")
+    size = lax.axis_size("dp") * n_ex
+    pairs = [(i, ((i // n_ex) ^ 1) * n_ex + ((i % n_ex) ^ bits)) for i in range(size)]
+    return lax.ppermute(vals, BOTH, pairs)
+
+
+def peers():
+    size = lax.axis_size("expert")
+    return [(inner, bits) for bits in range(0, size, 2) for inner in range(2)][1:]
+
+
+def ring_blocks(vals):
+    blocks = [vals]
+    for _ in range(1, lax.axis_size("dp") // 2):
+        blocks.append(ring_shift(blocks[-1], 1))
+    return blocks
+
+
+def add(left, right):
+    return (left.astype(F32) + right.astype(F32)).astype(left.dtype)
+
+
+def gather_peers(vals):
+    return jnp.concatenate([vals] + [cross(vals, *peer) for peer in peers()], axis=0)
+
+
+def reduce_peers(vals):
+    total = vals[0].astype(F32)
+    for spot, peer in enumerate(peers()):
+        total = total + cross(vals[spot + 1], *peer).astype(F32)
+    return total.astype(vals.dtype)
+
+
+def walk_tables(n_dp):
+    ring = ring_order(n_dp // 2)
+    size = len(ring)
+    ring_arr = jnp.array(ring, jnp.int32)
+    spot_arr = jnp.array([ring.index(i) for i in range(size)], jnp.int32)
+    member = lax.axis_index("dp")
+    my_spot = spot_arr[member // 2]
+    walk = jnp.arange(n_dp, dtype=jnp.int32)
+    inner = (member % 2) ^ (walk % 2)
+    source = ring_arr[(my_spot - walk // 2) % size] * 2 + inner
+    target = ring_arr[(my_spot + walk // 2) % size] * 2 + inner
+    step_of = ((my_spot - spot_arr[walk // 2]) % size) * 2 + inner
+    return source, target, step_of
+
+
+def walk_perm(n_dp, index):
+    pairs = ring_perm(n_dp, index // 2)
+    return [(src, dst ^ (index % 2)) for src, dst in pairs]
+
+
+def walk_swap(blocks, tables):
+    n_dp = blocks.shape[0]
+    _, target, step_of = tables
+    moved = []
+    for index in range(n_dp):
+        block = lax.dynamic_index_in_dim(blocks, target[index], 0, keepdims=False)
+        if index:
+            block = lax.ppermute(block, "dp", walk_perm(n_dp, index))
+        moved.append(block)
+    return jnp.take(jnp.stack(moved), step_of, axis=0)
+
+
+def home(parts):
+    total = parts[0].astype(F32)
+    for step in range(1, len(parts)):
+        total = total + ring_shift(parts[step], -step).astype(F32)
+    return total
+
+
+def expert_kernel(halves, width, xa, xb, ya, yb, w1, w1t, w2, w2t, pick, place, outs):
+    ma, mb, ra, rb, pre_out, inner_out = outs
+    step = pl.program_id(0)
+    first = step < halves
+    x_all = jnp.where(first, xa[...], xb[...])
+    dy = jnp.where(first, ya[...], yb[...]).reshape(x_all.shape[0], width)
+    x = x_all[:, :width]
+    half = w2.shape[0]
+    gates = dot(x_all[:, width:], pick[...])
+    pre = dot(x, w1[...])
+    gate_val, up_val = pre[:, :half], pre[:, half:]
+    sig = 1.0 / (1.0 + jnp.exp(-gate_val))
+    silu = gate_val * sig
+    inner = (silu * up_val).astype(BF).astype(F32)
+    gated = (gates * inner).astype(BF)
+    inner_out[...] = gated
+    mix = dot(gated, w2[...]).astype(BF)
+    back = dot(dy, w2t[...])
+    prod = inner * back
+    prod_hi = prod.astype(BF)
+    prod_lo = (prod - prod_hi.astype(F32)).astype(BF)
+    gate_grad = (dot(prod_hi, place[...]) + dot(prod_lo, place[...])).astype(BF)
+    inner_grad = gates * back
+    gate_pre = (inner_grad * up_val * sig * (1.0 + gate_val * (1.0 - sig))).astype(BF)
+    up_pre = (inner_grad * silu).astype(BF)
+    pre_out[:, :half] = gate_pre
+    pre_out[:, half:] = up_pre
+    rows = (dot(gate_pre, w1t[:half, :]) + dot(up_pre, w1t[half:, :])).astype(BF)
+
+    @pl.when(first)
+    def _():
+        ma[...] = mix
+        ra[:, :width] = rows
+        ra[:, width:] = gate_grad
+
+    @pl.when(jnp.logical_not(first))
+    def _():
+        mb[...] = mix
+        rb[:, :width] = rows
+        rb[:, width:] = gate_grad
+
+
+def experts(chunk, xa, xb, ya, yb, w1, w1t, w2, w2t, pick, place):
+    count, wide = xa.shape
+    rows, width = ya.shape[2:]
+    half = w2.shape[0]
+    tile = 2 * rows
+    halves = count // tile
+    front = lambda i: (jnp.minimum(i, halves - 1), 0)
+    rear = lambda i: (jnp.maximum(i - halves, 0), 0)
+    whole = lambda arr: pl.BlockSpec(arr.shape, lambda i: (0, 0), pipeline_mode=pl.Buffered(1))
+    back_wide = width + place.shape[1]
+
+    def body(xa, xb, ya, yb, w1, w1t, w2, w2t, pick, place, *outs):
+        expert_kernel(halves, width, xa, xb, ya, yb, w1, w1t, w2, w2t, pick, place, outs)
+
+    flops = 2 * 2 * count * width * half * 6
+    return pl.pallas_call(
+        body,
+        grid=(2 * halves,),
+        in_specs=[
+            pl.BlockSpec((tile, wide), front),
+            pl.BlockSpec((tile, wide), rear),
+            pl.BlockSpec((2, None, rows, width), lambda i: (front(i)[0], chunk, 0, 0)),
+            pl.BlockSpec((2, None, rows, width), lambda i: (rear(i)[0], chunk, 0, 0)),
+        ]
+        + [whole(arr) for arr in (w1, w1t, w2, w2t, pick, place)],
+        out_specs=[
+            pl.BlockSpec((tile, width), front),
+            pl.BlockSpec((tile, width), rear),
+            pl.BlockSpec((tile, back_wide), front),
+            pl.BlockSpec((tile, back_wide), rear),
+            pl.BlockSpec((tile, 2 * half), lambda i: (i, 0)),
+            pl.BlockSpec((tile, half), lambda i: (i, 0)),
+        ],
+        out_shape=[
+            jax.ShapeDtypeStruct((count, width), BF),
+            jax.ShapeDtypeStruct((count, width), BF),
+            jax.ShapeDtypeStruct((count, back_wide), BF),
+            jax.ShapeDtypeStruct((count, back_wide), BF),
+            jax.ShapeDtypeStruct((2 * count, 2 * half), BF),
+            jax.ShapeDtypeStruct((2 * count, half), BF),
+        ],
+        cost_estimate=pl.CostEstimate(
+            flops=flops, transcendentals=2 * count * half, bytes_accessed=20 * count * width
+        ),
+        name="experts",
+    )(xa, xb, ya, yb, w1, w1t, w2, w2t, pick, place)
+
+
+def lanes(count):
+    return -(-count // 128) * 128
 
 
 def on_device(
@@ -112,9 +312,17 @@
     gain_k = gains_all[:, 2 * gw + hw :].reshape(-1)
 
     seq_tokens = gather(tokens, "dp")
+    member = lax.axis_index("dp")
+    tables = walk_tables(n_dp)
+    member_of_walk = tables[0]
     qkv = jnp.stack([w_query, w_key, w_value]).astype(BF).reshape(3, wrows, n_dp, cols)
     qkv = swap(qkv.transpose(2, 1, 0, 3), "dp")
-    qkv = gather(qkv.reshape(1, n_dp, wrows, 3 * cols), "expert")
+    qkv = qkv.reshape(1, n_dp, wrows, 3 * cols)
+    bit = 1
+    while bit < n_ex:
+        qkv = jnp.concatenate([qkv, flip(qkv, "expert", bit)], axis=0)
+        bit *= 2
+    qkv = jnp.take(qkv, seq_id ^ jnp.arange(n_ex, dtype=jnp.int32), axis=0)
     qkv = qkv.transpose(1, 0, 2, 3).reshape(width, 3 * cols)
     wo_all = gather(w_output.astype(BF), BOTH)
     wr_all = swap(
@@ -122,10 +330,14 @@
     )
     wr_all = wr_all.transpose(1, 0, 2).reshape(expert_total, width)
     w1 = jnp.stack([w_gate, w_up]).astype(BF).reshape(2, local_count, cols, n_dp, ff_part)
-    w1 = swap(w1.transpose(3, 2, 0, 1, 4).reshape(n_dp, cols, -1), "dp").reshape(width, -1)
+    w1 = w1.transpose(3, 2, 0, 1, 4).reshape(n_dp, cols, -1)
+    w1 = walk_swap(w1, tables)
+    w1 = w1.reshape(width, -1)
     w2 = w_down.astype(BF).reshape(local_count * ff_part, width)
     half = local_count * ff_part
-    dy_all = gather(cotangent, BOTH)
+    w1t, w2t = w1.T, w2.T
+    dy_near = gather_peers(jnp.stack(ring_blocks(cotangent))[None])
+    dy_far = core_flip(dy_near)
 
     seq_in = seq_tokens.astype(F32)
     normed_one = rms_scale(seq_in, gain_one).astype(BF)
@@ -159,46 +371,79 @@
     routed = jnp.any(routes[:, :, None] == expert_ids[None, None, :], axis=1)
     masked_logits = jnp.where(routed, router_logits, -jnp.inf)
     gates = jax.nn.softmax(masked_logits, axis=-1)
-    gate_blocks = jnp.broadcast_to(
-        gates.T.reshape(1, n_ex, local_count, rows), (n_dp, n_ex, local_count, rows)
-    ).reshape(n_all, local_count, rows)
-    my_gates = swap(gate_blocks, BOTH).transpose(0, 2, 1).reshape(n_all * rows, local_count)
-
-    n2_all = gather(normed_two, BOTH)
-    hidden_pre = dot(n2_all, w1)
-    gate_val = hidden_pre[:, :half]
-    up_val = hidden_pre[:, half:]
-    wide_gates = jnp.repeat(my_gates, ff_part, axis=1)
-    sig = jax.nn.sigmoid(gate_val)
-    silu = gate_val * sig
-    inner = (silu * up_val).astype(BF).astype(F32)
-    gated_inner = (wide_gates * inner).astype(BF)
-    back_inner = dot_t(dy_all, w2)
-    gate_grads = jnp.sum(
-        (inner * back_inner).reshape(-1, local_count, ff_part), axis=-1
-    )
-    inner_grad = wide_gates * back_inner
-    pre_grad = jnp.concatenate(
-        [inner_grad * up_val * sig * (1.0 + gate_val * (1.0 - sig)), inner_grad * silu], axis=1
+    gates_hi = gates.astype(BF)
+    gates_lo = (gates - gates_hi.astype(F32)).astype(BF)
+    spare = lanes(2 * expert_total) - 2 * expert_total
+    payload = jnp.concatenate(
+        [normed_two, gates_hi, gates_lo, jnp.zeros((rows, spare), BF)], axis=1
+    )
+    unit = jnp.arange(half, dtype=jnp.int32) // ff_part + seq_id * local_count
+    gate_col = jnp.arange(lanes(2 * expert_total), dtype=jnp.int32)
+    pick = (
+        (gate_col[:, None] == unit[None, :]) | (gate_col[:, None] == unit[None, :] + expert_total)
     ).astype(BF)
-    row_grads = dot_t(pre_grad, w1).astype(BF)
-    token_grads = scatter(row_grads, BOTH).astype(F32)
-    mixture = dot(gated_inner, w2).astype(BF)
-    mixture, token_grads = lax.optimization_barrier((mixture, token_grads))
-    mixed = scatter(mixture, BOTH).astype(F32)
+    grad_col = jnp.arange(lanes(expert_total * n_dp), dtype=jnp.int32)
+    place = (grad_col[None, :] == (unit * n_dp + member)[:, None]).astype(BF)
+
+    lean = n_all * rows > 4096
+    n2_sets, mix_parts, home_parts, pre_grads, gated_inners = [], [], [], [], []
+    w1_grad, down_grad = 0.0, 0.0
+    near = None
+    for step, block in enumerate(ring_blocks(payload)):
+        if near is not None and not lean:
+            block, near = lax.optimization_barrier((block, near))
+        near = gather_peers(block)
+        far = core_flip(near)
+        ma, mb, ra, rb, pre_grad, gated_inner = experts(
+            step, near, far, dy_near, dy_far, w1, w1t, w2, w2t, pick, place
+        )
+        part = add(ra, core_flip(rb)).reshape(-1, rows, ra.shape[1])
+        home_parts.append(reduce_peers(part))
+        if lean:
+            mix_parts.append(reduce_peers(add(ma, core_flip(mb)).reshape(-1, rows, width)))
+            cut = pre_grad.shape[0] // 2
+            w1_grad = w1_grad + dot_rows(near[:, :width], pre_grad[:cut])
+            w1_grad = w1_grad + dot_rows(far[:, :width], pre_grad[cut:])
+            down_grad = down_grad + dot_rows(gated_inner[:cut], dy_near[:, step].reshape(-1, width))
+            down_grad = down_grad + dot_rows(gated_inner[cut:], dy_far[:, step].reshape(-1, width))
+            w1_grad, down_grad, dy_near, dy_far, mix_parts, home_parts, payload = (
+                lax.optimization_barrier(
+                    (w1_grad, down_grad, dy_near, dy_far, mix_parts, home_parts, payload)
+                )
+            )
+        else:
+            n2_sets += [near, far]
+            mix_parts.append((ma, mb))
+            pre_grads.append(pre_grad)
+            gated_inners.append(gated_inner)
+    returned = home(home_parts)
+    token_grads = returned[:, :width]
+    gg = returned[:, width : width + expert_total * n_dp].reshape(rows, expert_total, n_dp)
+    gg = jnp.sum(gg, axis=-1)
+    if not lean:
+        mix_near = jnp.stack([m[0].reshape(-1, rows, width) for m in mix_parts], axis=1)
+        mix_far = jnp.stack([m[1].reshape(-1, rows, width) for m in mix_parts], axis=1)
+        mix_far, home_parts[-1] = lax.optimization_barrier((mix_far, home_parts[-1]))
+        mix_near = add(mix_near, core_flip(mix_far))
+        mix_parts = list(reduce_peers(mix_near))
+        by_chunk = jnp.stack([g.reshape(2, -1, rows, half) for g in gated_inners], axis=2)
+        by_chunk = by_chunk.reshape(2, -1, half)
+        down_grad = dot_rows(by_chunk[0], dy_near.reshape(-1, width)) + dot_rows(
+            by_chunk[1], dy_far.reshape(-1, width)
+        )
+        n2_all = jnp.concatenate([part[:, :width] for part in n2_sets], axis=0)
+        w1_grad = dot_rows(n2_all, jnp.concatenate(pre_grads, axis=0))
+    mixed = home(mix_parts)
     block_out = (hidden_one + mixed).astype(BF)
-    down_grad = dot_rows(gated_inner, dy_all).reshape(local_count, ff_part, width)
-    w1_grad = dot_rows(n2_all, pre_grad).astype(BF)
-    w1_grad = swap(w1_grad.reshape(n_dp, cols, -1), "dp")
+    down_grad = down_grad.reshape(local_count, ff_part, width)
+    w1_grad = w1_grad.astype(BF)
+    w1_grad = walk_swap(w1_grad.reshape(n_dp, cols, -1), tables)
     w1_grad = (
         w1_grad.reshape(n_dp, cols, 2, local_count, ff_part)
         .transpose(2, 3, 1, 0, 4)
         .reshape(2, local_count, cols, ff)
         .astype(F32)
     )
-
-    gg = swap(gate_grads.reshape(n_all, rows, local_count).transpose(0, 2, 1), BOTH)
-    gg = gg.reshape(n_dp, n_ex, local_count, rows).sum(axis=0).reshape(expert_total, rows).T
     weighted = gates * gg
     logit_bf = (weighted - gates * jnp.sum(weighted, axis=-1, keepdims=True)).astype(BF)
     router_grad = dot_rows(normed_two, logit_bf)
@@ -229,10 +474,17 @@
         [query_flat_grad.astype(BF), key_flat_grad.astype(BF), value_grad.reshape(-1, cols).astype(BF)],
         axis=1,
     )
-    part_grad = dot_t(qkv_grad, qkv)
+    walk_grad = jnp.take(qkv_grad.reshape(n_dp, rows, 3 * cols), member_of_walk, axis=0)
+    part_grad = dot_t(walk_grad.reshape(-1, 3 * cols), qkv)
+    walk_in = jnp.take(seq_tokens.reshape(n_dp, rows, width), member_of_walk, axis=0)
+    seq_in = walk_in.reshape(-1, width).astype(F32)
     seq_scale = lax.rsqrt(jnp.mean(seq_in * seq_in, axis=-1, keepdims=True) + norm_eps)
     norm_one_grad = jnp.sum(part_grad * (seq_in * seq_scale), axis=0)
-    normed_one_grad = scatter(part_grad.astype(BF), "dp").astype(F32)
+    part_bf = part_grad.astype(BF).reshape(n_dp // 2, 2, rows, width)
+    sums = []
+    for step in range(n_dp // 2):
+        sums.append(add(part_bf[step, 0], flip(part_bf[step, 1], "dp", 1)))
+    normed_one_grad = home(sums)
     _, norm_one_back = jax.vjp(lambda v: rms_scale(v, gain_one), inputs)
     (input_part,) = norm_one_back(normed_one_grad)
     grad_tokens = (hidden_grad + input_part).astype(BF)

time: 1370 us -> 1190 us (0.87)
  waiting for transfers between devices: 896 us -> 501 us
  local copies, waits for them, and re-layouts: 83.7 us -> 206 us
  Pallas kernels: 0 us -> 102 us
  matrix products: 190 us -> 99 us
  starting transfers between devices: 54.3 us -> 124 us
  other arithmetic: 57.9 us -> 117 us
  blocking collectives: 48.3 us -> 0 us
  between operations: 15.4 us -> 31.5 us
    ppermute x0 -> x75, waiting for transfers between devices: none -> 452 us  [the longest x36 184 us: flip(): return lax.ppermute(vals, axis, [(i, i ^ bit) for i in range(size)])]
    reduce_scatter x4 -> x1, waiting for transfers between devices: 377 us -> 0.01 us  [scatter(): return lax.psum_scatter(partial_sum, axes, scatter_dimension=0, tiled=True)]
    all_to_all x9 -> x8, waiting for transfers between devices: 310 us -> 48.2 us  [swap(): return lax.all_to_all(blocks, axes, split_axis=0, concat_axis=0, tiled=True)]
    all_gather x5 -> x2, waiting for transfers between devices: 207 us -> 0.02 us  [gather(): return lax.all_gather(shard, axes, axis=0, tiled=True)]
    pallas_call x0 -> x4, Pallas kernels: none -> 102 us  [experts(): pl.pallas_call(body, grid=(2 * halves,), in_specs=[pl.BlockSpec((tile, wi...]
    ppermute x0 -> x75, starting transfers between devices: none -> 75.3 us  [the longest x36 30.1 us: flip(): return lax.ppermute(vals, axis, [(i, i ^ bit) for i in range(size)])]
    unnamed x129 -> x250, local copies, waits for them, and re-layouts: 16.3 us -> 71.5 us
    dot_general x5 -> x3, matrix products: 62.2 us -> 11.2 us  [dot_t(): lax.dot_general(left_mat, right_mat, (((1,), (1,)), ((), ())), preferred_...]
  transfers between devices with their start and end apart: 18 -> 86, of which waited for: 14 -> 38; matrix products, arithmetic and copies ran while one was open for 16% -> 35% of each run, Pallas kernels for 0% -> 9%
where the time goes in v2:
time: 1190 us; the launch traced here: 1180 us
  waiting for transfers between devices  501 us (42%)
  local copies, waits for them, and re-layouts  206 us (17%)
  starting transfers between devices  124 us (10%)
  other arithmetic  117 us (10%)
  Pallas kernels  102 us (9%)
  matrix products  99 us (8%)
  between operations  31.5 us (3%)
    ppermute x36, waiting for transfers between devices, flip(): return lax.ppermute(vals, axis, [(i, i ^ bit) for i in range(size)])  184 us
    ppermute x15, waiting for transfers between devices, ring_shift(): return lax.ppermute(vals, 'dp', ring_perm(lax.axis_size('dp'), steps))  137 us
    pallas_call x4, Pallas kernels, experts(): pl.pallas_call(body, grid=(2 * halves,), in_specs=[pl.BlockSpec((tile, wi...  102 us
    unnamed x250, local copies, waits for them, and re-layouts  71.5 us
    ppermute x14, waiting for transfers between devices, walk_swap(): block = lax.ppermute(block, 'dp', walk_perm(n_dp, index))  67.8 us
    ppermute x10, waiting for transfers between devices, cross(): return lax.ppermute(vals, BOTH, pairs)  63.2 us
    dot_general x6, matrix products, dot_rows(): lax.dot_general(left_mat, right_mat, (((0,), (0,)), ((), ())), preferred_...  52.6 us
    all_to_all x8, starting transfers between devices, swap(): return lax.all_to_all(blocks, axes, split_axis=0, concat_axis=0, tiled=True)  48.5 us
  transfers between devices with their start and end apart: 86, of which 38 were waited for; matrix products, arithmetic and copies ran while one was open for 35% of the time, Pallas kernels for 9%

profile of v2, /device:TPU:13, one launch (start us, length us, event | category | flops | bytes accessed | tf_op | source)
XLA Modules:
  0.0 1179.3 jit_solution(5939086611575098889)
XLA Ops:
  76.2 10.9 all-to-all-done.1
  130.7 12.3 %collective-permute-done.7 = bf16[128,2048]{1,0:T(8,128)(2,1)} collective-permute-done((bf16[128,2048]{1,0:T(8,128)(2,1)}, bf16[128,2048]{1,0:T(8,128)(2,1)}, u32[]{:S(2)}, u32[]{:S(2)}) %collective-permute-start.7) | collective-permute-done | bytes 524320 | tf_op jit(solution)/shard_map/ppermute | solution.py:92
  144.9 32.8 %collective-permute-done.16 = bf16[256,1024]{1,0:T(8,128)(2,1)S(1)} collective-permute-done((bf16[256,1024]{1,0:T(8,128)(2,1)}, bf16[256,1024]{1,0:T(8,128)(2,1)S(1)}, u32[]{:S(2)}, u32[]{:S(2)}) %collective-permute-start.16) | collective-permute-done | bytes 524320 | tf_op jit(solution)/shard_map/ppermute | solution.py:169
  178.7 34.5 %collective-permute-done.17 = bf16[256,1024]{1,0:T(8,128)(2,1)S(1)} collective-permute-done((bf16[256,1024]{1,0:T(8,128)(2,1)}, bf16[256,1024]{1,0:T(8,128)(2,1)S(1)}, u32[]{:S(2)}, u32[]{:S(2)}) %collective-permute-start.17) | collective-permute-done | bytes 524320 | tf_op jit(solution)/shard_map/ppermute | solution.py:169
  244.3 8.0 fusion.114
  265.5 58.7 %collective-permute-done.10 = bf16[1,4,128,2048]{3,2,1,0:T(8,128)(2,1)} collective-permute-done((bf16[1,4,128,2048]{3,2,1,0:T(8,128)(2,1)}, bf16[1,4,128,2048]{3,2,1,0:T(8,128)(2,1)}, u32[]{:S(2)}, u32[]{:S(2)}) %collective-permute-start.10) | collective-permute-done | bytes 2097184 | tf_op jit(solution)/shard_map/ppermute | solution.py:97
  378.6 7.9 collective-permute-done.21
  389.4 11.3 collective-permute-done.23
  420.0 11.3 collective-permute-done.28
  452.3 9.9 collective-permute-done.33
  465.4 25.4 %experts.4 = (bf16[512,2048]{1,0:T(8,128)(2,1)}, bf16[512,2048]{1,0:T(8,128)(2,1)}, bf16[512,2176]{1,0:T(8,128)(2,1)}, bf16[512,2176]{1,0:T(8,128)(2,1)}, bf16[1...) custom-call(bf16[512,2176]{1,0:T(8,128)(2,1)} %copy-done.11, bf16[512,2176]{1,0:T(8,128)(2,1)} %copy-done.49, ...), custom_call_target="tpu_custom_call" | custom-call | flops 12884901888 | bytes 20971520 | tf_op jit(solution)/shard_map/experts/pallas_call | solution.py:238
  497.3 25.4 %experts.5 = (bf16[512,2048]{1,0:T(8,128)(2,1)}, bf16[512,2048]{1,0:T(8,128)(2,1)}, bf16[512,2176]{1,0:T(8,128)(2,1)}, bf16[512,2176]{1,0:T(8,128)(2,1)}, bf16[1...) custom-call(bf16[512,2176]{1,0:T(8,128)(2,1)} %constant_dynamic-update-slice_fusion.1.xa, ...), custom_call_target="tpu_custom_call" | custom-call | flops 12884901888 | bytes 20971520 | tf_op jit(solution)/shard_map/experts/pallas_call | solution.py:238
  529.7 25.6 %experts.7 = (bf16[512,2048]{1,0:T(8,128)(2,1)}, bf16[512,2048]{1,0:T(8,128)(2,1)}, bf16[512,2176]{1,0:T(8,128)(2,1)}, bf16[512,2176]{1,0:T(8,128)(2,1)}, bf16[1...) custom-call(bf16[512,2176]{1,0:T(8,128)(2,1)} %constant_dynamic-update-slice_fusion.9.xa, ...), custom_call_target="tpu_custom_call" | custom-call | flops 12884901888 | bytes 20971520 | tf_op jit(solution)/shard_map/experts/pallas_call | solution.py:238
  561.7 25.4 %experts.6 = (bf16[512,2048]{1,0:T(8,128)(2,1)}, bf16[512,2048]{1,0:T(8,128)(2,1)}, bf16[512,2176]{1,0:T(8,128)(2,1)}, bf16[512,2176]{1,0:T(8,128)(2,1)}, bf16[1...) custom-call(bf16[512,2176]{1,0:T(8,128)(2,1)} %constant_dynamic-update-slice_fusion.5.xa, ...), custom_call_target="tpu_custom_call" | custom-call | flops 12884901888 | bytes 20971520 | tf_op jit(solution)/shard_map/experts/pallas_call | solution.py:238
  607.2 9.4 collective-permute-done.37
  619.3 22.8 %fusion.19 = bf16[2048,1024]{1,0:T(8,128)(2,1)S(1)} fusion(bf16[4096,2048]{1,0:T(8,128)(2,1)} %slice_dynamic-update-slice_fusion, bf16[1024,1024]{1,0:T(8,128)(2,1)S(1)} %copy-done.100, bf16[1024,1024]{1,0:T(8,128)(2,1)} %get-tuple-element.65, bf16[1024,1024]{1,0:T(8,128)(2,1)S(1)} %copy-done.99, bf16[1024,1024]{1,0:T(8,128)(2,1)S(1)} %copy-done.98), kind=kOutput, calls=%fused_computation.51 | convolution fusion | flops 17215520768 | bytes 29360128 | tf_op jit(solution)/shard_map/dot_general | solution.py:50
  658.1 16.5 %collective-permute-done.53 = bf16[128,2176]{1,0:T(8,128)(2,1)S(1)} collective-permute-done((bf16[128,2176]{1,0:T(8,128)(2,1)S(1)}, bf16[128,2176]{1,0:T(8,128)(2,1)S(1)}, u32[]{:S(2)}, u32[]{:S(2)}) %collective-permute-start.53) | collective-permute-done | bytes 557088 | tf_op jit(solution)/shard_map/ppermute | solution.py:112
  675.8 10.5 collective-permute-done.52
  712.6 9.6 collective-permute-done.57
  725.5 45.2 %collective-permute-done.47 = bf16[128,2176]{1,0:T(8,128)(2,1)S(1)} collective-permute-done((bf16[128,2176]{1,0:T(8,128)(2,1)S(1)}, bf16[128,2176]{1,0:T(8,128)(2,1)S(1)}, u32[]{:S(2)}, u32[]{:S(2)}) %collective-permute-start.47) | collective-permute-done | bytes 557088 | tf_op jit(solution)/shard_map/ppermute | solution.py:97
  777.8 30.9 %collective-permute-done.59 = bf16[128,2176]{1,0:T(8,128)(2,1)S(1)} collective-permute-done((bf16[128,2176]{1,0:T(8,128)(2,1)S(1)}, bf16[128,2176]{1,0:T(8,128)(2,1)S(1)}, u32[]{:S(2)}, u32[]{:S(2)}) %collective-permute-start.59) | collective-permute-done | bytes 557088 | tf_op jit(solution)/shard_map/ppermute | solution.py:92
  831.8 31.7 %collective-permute-done.44 = bf16[128,2048]{1,0:T(8,128)(2,1)S(1)} collective-permute-done((bf16[128,2048]{1,0:T(8,128)(2,1)S(1)}, bf16[128,2048]{1,0:T(8,128)(2,1)S(1)}, u32[]{:S(2)}, u32[]{:S(2)}) %collective-permute-start.44) | collective-permute-done | bytes 524320 | tf_op jit(solution)/shard_map/ppermute | solution.py:92
  863.5 26.1 %collective-permute-done.43 = bf16[128,2048]{1,0:T(8,128)(2,1)S(1)} collective-permute-done((bf16[128,2048]{1,0:T(8,128)(2,1)S(1)}, bf16[128,2048]{1,0:T(8,128)(2,1)S(1)}, u32[]{:S(2)}, u32[]{:S(2)}) %collective-permute-start.43) | collective-permute-done | bytes 524320 | tf_op jit(solution)/shard_map/ppermute | solution.py:92
  905.9 9.8 convolution_add_fusion
  940.7 31.8 %all-to-all-done.4 = bf16[8,128,256]{1,2,0:T(8,128)(2,1)S(1)} async-done(((bf16[8,128,256]{1,2,0:T(8,128)(2,1)}), bf16[8,128,256]{1,2,0:T(8,128)(2,1)S(1)}, u32[]{:S(2)}, u32[]{:S(2)}) %all-to-all-start.4) | async-done | bytes 524320 | tf_op jit(solution)/shard_map/all_to_all | solution.py:65
  1015.5 7.9 multiply_reduce_fusion
  1024.7 13.1 %all-to-all-start.5 = ((f32[32,1,1160]{2,1,0:T(1,128)}), f32[32,1,1160]{2,1,0:T(1,128)S(1)}, u32[]{:S(2)}, u32[]{:S(2)}) async-start(f32[32,1,1160]{2,1,0:T(1,128)} %copy.436), calls=%async_computation.5 | async-start | bytes 327680 | tf_op jit(solution)/shard_map/all_to_all | solution.py:65
  1067.5 10.5 reshape.738
  1078.1 8.3 copy.481
  1086.8 10.4 collective-permute-done.64
  1127.7 10.9 collective-permute-done.65
  1138.6 17.6 %collective-permute-done.63 = bf16[128,2048]{1,0:T(8,128)(2,1)} collective-permute-done((bf16[128,2048]{1,0:T(8,128)(2,1)}, bf16[128,2048]{1,0:T(8,128)(2,1)}, u32[]{:S(2)}, u32[]{:S(2)}) %collective-permute-start.63) | collective-permute-done | bytes 524320 | tf_op jit(solution)/shard_map/ppermute | solution.py:92
  (598 shorter events, 525.5 us)
Async XLA Ops:
  7.2 219.4 %all-gather.3.cloned.1.call-start = ((), (), s32[]{:S(2)}) async-start(), calls=%async_computation.9 | async-start | bytes 4718592 | tf_op jit(solution)/shard_map/all_gather | solution.py:69
  7.9 329.6 %all-gather.5.cloned.1.call-start = ((), (), s32[]{:S(2)}) async-start(), calls=%async_computation.10 | async-start | bytes 8650752 | tf_op jit(solution)/shard_map/all_gather | solution.py:69
  13.4 73.6 %all-to-all-start.1 = ((bf16[8,64,3,256]{3,1,2,0:T(8,128)(2,1)}), bf16[8,64,3,256]{3,1,2,0:T(8,128)(2,1)S(1)}, u32[]{:S(2)}, u32[]{:S(2)}) async-start(bf16[8,64,3,256]{3,1,2,0:T(8,128)(2,1)} %copy.381), calls=%async_computation.1 | async-start | bytes 1572864 | tf_op jit(solution)/shard_map/all_to_all | solution.py:65
  19.1 96.6 %collective-permute-start.6 = (bf16[128,2048]{1,0:T(8,128)(2,1)S(1)}, bf16[128,2048]{1,0:T(8,128)(2,1)}, u32[]{:S(2)}, u32[]{:S(2)}) collective-permute-start(bf16[128,2048]{1,0:T(8,128)(2,1)S(1)} %copy-done.47), channel_id=1, source_target_pairs={{0,16},{4,20},{16,24},{20,28},{24,8},{28,12},{8,0},{12,4},{1,17},{... | collective-permute-start | bytes 1572872 | tf_op jit(solution)/shard_map/ppermute | solution.py:92
  55.5 66.9 %collective-permute-start.13 = (bf16[256,1024]{1,0:T(8,128)(2,1)}, bf16[256,1024]{1,0:T(8,128)(2,1)}, u32[]{:S(2)}, u32[]{:S(2)}) collective-permute-start(bf16[256,1024]{1,0:T(8,128)(2,1)} %bitcast.356), channel_id=1, source_target_pairs={{0,4},{4,0},{16,20},{20,16},{24,28},{28,24},{8,12},{12,8},{1,5},{5... | collective-permute-start | bytes 1572872 | tf_op jit(solution)/shard_map/ppermute | solution.py:169
  57.6 67.2 %collective-permute-start.14 = (bf16[256,1024]{1,0:T(8,128)(2,1)}, bf16[256,1024]{1,0:T(8,128)(2,1)}, u32[]{:S(2)}, u32[]{:S(2)}) collective-permute-start(bf16[256,1024]{1,0:T(8,128)(2,1)} %bitcast.355), channel_id=1, source_target_pairs={{0,16},{4,20},{16,24},{20,28},{24,8},{28,12},{8,0},{12,4},{1,17},{... | collective-permute-start | bytes 1572872 | tf_op jit(solution)/shard_map/ppermute | solution.py:169
  60.9 67.6 %collective-permute-start.15 = (bf16[256,1024]{1,0:T(8,128)(2,1)}, bf16[256,1024]{1,0:T(8,128)(2,1)}, u32[]{:S(2)}, u32[]{:S(2)}) collective-permute-start(bf16[256,1024]{1,0:T(8,128)(2,1)} %bitcast.354), channel_id=1, source_target_pairs={{0,20},{4,16},{16,28},{20,24},{24,12},{28,8},{8,4},{12,0},{1,21},{... | collective-permute-start | bytes 1572872 | tf_op jit(solution)/shard_map/ppermute | solution.py:169
  118.4 100.5 %collective-permute-start.1 = (bf16[2,8,64,768]{3,2,1,0:T(8,128)(2,1)}, bf16[2,8,64,768]{3,2,1,0:T(8,128)(2,1)}, u32[]{:S(2)}, u32[]{:S(2)}) collective-permute-start(bf16[2,8,64,768]{3,2,1,0:T(8,128)(2,1)} %pad_maximum_fusion.5), channel_id=1, source_target_pairs={{0,2},{1,3},{2,0},{3,1},{4,6},{5,7},{6,4},{7,5},{8,10},{9,11},{10,... | collective-permute-start | bytes 4718600 | tf_op jit(solution)/shard_map/ppermute | solution.py:97
  124.8 88.4 %collective-permute-start.17 = (bf16[256,1024]{1,0:T(8,128)(2,1)}, bf16[256,1024]{1,0:T(8,128)(2,1)S(1)}, u32[]{:S(2)}, u32[]{:S(2)}) collective-permute-start(bf16[256,1024]{1,0:T(8,128)(2,1)} %bitcast.357), channel_id=1, source_target_pairs={{0,28},{4,24},{16,12},{20,8},{24,4},{28,0},{8,20},{12,16},{1,29},{... | collective-permute-start | bytes 1572872 | tf_op jit(solution)/shard_map/ppermute | solution.py:169
  128.5 132.8 %collective-permute-start.18 = (bf16[256,1024]{1,0:T(8,128)(2,1)}, bf16[256,1024]{1,0:T(8,128)(2,1)}, u32[]{:S(2)}, u32[]{:S(2)}) collective-permute-start(bf16[256,1024]{1,0:T(8,128)(2,1)} %bitcast.353), channel_id=1, source_target_pairs={{0,8},{4,12},{16,0},{20,4},{24,16},{28,20},{8,24},{12,28},{1,9},{5... | collective-permute-start | bytes 1572872 | tf_op jit(solution)/shard_map/ppermute | solution.py:169
  143.0 71.0 %collective-permute-start.8 = (bf16[128,2048]{1,0:T(8,128)(2,1)}, bf16[128,2048]{1,0:T(8,128)(2,1)S(1)}, u32[]{:S(2)}, u32[]{:S(2)}) collective-permute-start(bf16[128,2048]{1,0:T(8,128)(2,1)} %collective-permute-done.7), channel_id=1, source_target_pairs={{0,16},{4,20},{16,24},{20,28},{24,8},{28,12},{8,0},{12,4},{1,17},{... | collective-permute-start | bytes 1572872 | tf_op jit(solution)/shard_map/ppermute | solution.py:92
  177.7 168.5 %collective-permute-start.19 = (bf16[256,1024]{1,0:T(8,128)(2,1)}, bf16[256,1024]{1,0:T(8,128)(2,1)}, u32[]{:S(2)}, u32[]{:S(2)}) collective-permute-start(bf16[256,1024]{1,0:T(8,128)(2,1)} %bitcast.352), channel_id=1, source_target_pairs={{0,12},{4,8},{16,4},{20,0},{24,20},{28,16},{8,28},{12,24},{1,13},{... | collective-permute-start | bytes 1572872 | tf_op jit(solution)/shard_map/ppermute | solution.py:169
  218.9 105.3 %collective-permute-start.10 = (bf16[1,4,128,2048]{3,2,1,0:T(8,128)(2,1)}, bf16[1,4,128,2048]{3,2,1,0:T(8,128)(2,1)}, u32[]{:S(2)}, u32[]{:S(2)}) collective-permute-start(bf16[1,4,128,2048]{3,2,1,0:T(8,128)(2,1)} %maximum_bitcast_fusion.1), channel_id=1, source_target_pairs={{0,2},{1,3},{2,0},{3,1},{4,6},{5,7},{6,4},{7,5},{8,10},{9,11},{10,... | collective-permute-start | bytes 6291464 | tf_op jit(solution)/shard_map/ppermute | solution.py:97
  218.9 110.7 %collective-permute-start.9 = (bf16[1,4,128,2048]{3,2,1,0:T(8,128)(2,1)}, bf16[1,4,128,2048]{3,2,1,0:T(8,128)(2,1)}, u32[]{:S(2)}, u32[]{:S(2)}) collective-permute-start(bf16[1,4,128,2048]{3,2,1,0:T(8,128)(2,1)} %maximum_bitcast_fusion.1), channel_id=1, source_target_pairs={{0,4},{4,0},{8,12},{12,8},{16,20},{20,16},{24,28},{28,24},{1,5},{5... | collective-permute-start | bytes 6291464 | tf_op jit(solution)/shard_map/ppermute | solution.py:97
  257.7 79.8 %all-to-all-start.2 = ((bf16[8,128,256]{1,2,0:T(8,128)(2,1)}), bf16[8,128,256]{1,2,0:T(8,128)(2,1)S(1)}, u32[]{:S(2)}, u32[]{:S(2)}) async-start(bf16[8,128,256]{1,2,0:T(8,128)(2,1)} %copy.387), calls=%async_computation.2 | async-start | bytes 1048576 | tf_op jit(solution)/shard_map/all_to_all | solution.py:65
  261.3 909.4 %reduce-scatter.2.cloned.1.call-start = ((), (), s32[]{:S(2)}) async-start(), calls=%async_computation.11 | async-start | bytes 8650752 | tf_op jit(solution)/shard_map/reduce_scatter | solution.py:73
  336.9 127.1 %collective-permute-start.12 = (bf16[4,4,128,2048]{3,2,1,0:T(8,128)(2,1)}, bf16[4,4,128,2048]{3,2,1,0:T(8,128)(2,1)}, u32[]{:S(2)}, u32[]{:S(2)}) collective-permute-start(bf16[4,4,128,2048]{3,2,1,0:T(8,128)(2,1)} %pad_maximum_fusion.ya), channel_id=1, source_target_pairs={{0,1},{1,0},{2,3},{3,2},{4,5},{5,4},{6,7},{7,6},{8,9},{9,8},{10,11... | collective-permute-start | bytes 25165832 | tf_op jit(solution)/shard_map/ppermute | solution.py:97
  450.1 105.3 %collective-permute-start.29 = (bf16[512,2176]{1,0:T(8,128)(2,1)}, bf16[512,2176]{1,0:T(8,128)(2,1)}, u32[]{:S(2)}, u32[]{:S(2)}) collective-permute-start(bf16[512,2176]{1,0:T(8,128)(2,1)} %constant_dynamic-update-slice_fusion.5.xa), channel_id=1, source_target_pairs={{0,1},{1,0},{2,3},{3,2},{4,5},{5,4},{6,7},{7,6},{8,9},{9,8},{10,11... | collective-permute-start | bytes 6684680 | tf_op jit(solution)/shard_map/ppermute | solution.py:97
  490.7 152.1 %collective-permute-start.46 = (bf16[512,2176]{1,0:T(8,128)(2,1)}, bf16[512,2176]{1,0:T(8,128)(2,1)}, u32[]{:S(2)}, u32[]{:S(2)}) collective-permute-start(bf16[512,2176]{1,0:T(8,128)(2,1)} %get-tuple-element.58), channel_id=1, source_target_pairs={{0,1},{1,0},{2,3},{3,2},{4,5},{5,4},{6,7},{7,6},{8,9},{9,8},{10,11... | collective-permute-start | bytes 6684680 | tf_op jit(solution)/shard_map/ppermute | solution.py:97
  522.7 126.7 %collective-permute-start.50 = (bf16[512,2176]{1,0:T(8,128)(2,1)}, bf16[512,2176]{1,0:T(8,128)(2,1)}, u32[]{:S(2)}, u32[]{:S(2)}) collective-permute-start(bf16[512,2176]{1,0:T(8,128)(2,1)} %get-tuple-element.60), channel_id=1, source_target_pairs={{0,1},{1,0},{2,3},{3,2},{4,5},{5,4},{6,7},{7,6},{8,9},{9,8},{10,11... | collective-permute-start | bytes 6684680 | tf_op jit(solution)/shard_map/ppermute | solution.py:97
  618.8 70.4 %collective-permute-start.39 = (bf16[4,4,128,2048]{3,2,1,0:T(8,128)(2,1)}, bf16[4,4,128,2048]{3,2,1,0:T(8,128)(2,1)}, u32[]{:S(2)}, u32[]{:S(2)}) collective-permute-start(bf16[4,4,128,2048]{3,2,1,0:T(8,128)(2,1)} %pad_maximum_fusion.1), channel_id=1, source_target_pairs={{0,1},{1,0},{2,3},{3,2},{4,5},{5,4},{6,7},{7,6},{8,9},{9,8},{10,11... | collective-permute-start | bytes 25165832 | tf_op jit(solution)/shard_map/ppermute | solution.py:97
  701.7 69.1 %collective-permute-start.47 = (bf16[128,2176]{1,0:T(8,128)(2,1)S(1)}, bf16[128,2176]{1,0:T(8,128)(2,1)S(1)}, u32[]{:S(2)}, u32[]{:S(2)}) collective-permute-start(bf16[128,2176]{1,0:T(8,128)(2,1)S(1)} %copy-done.54), channel_id=1, source_target_pairs={{0,4},{4,0},{8,12},{12,8},{16,20},{20,16},{24,28},{28,24},{1,5},{5... | collective-permute-start | bytes 1671176 | tf_op jit(solution)/shard_map/ppermute | solution.py:97
  702.0 68.7 %collective-permute-start.54 = (bf16[128,2176]{1,0:T(8,128)(2,1)}, bf16[128,2176]{1,0:T(8,128)(2,1)S(1)}, u32[]{:S(2)}, u32[]{:S(2)}) collective-permute-start(bf16[128,2176]{1,0:T(8,128)(2,1)} %add_convert_fusion.6), channel_id=1, source_target_pairs={{0,8},{4,12},{16,0},{20,4},{24,16},{28,20},{8,24},{12,28},{1,9},{5... | collective-permute-start | bytes 1671176 | tf_op jit(solution)/shard_map/ppermute | solution.py:92
  710.5 101.6 %collective-permute-start.42 = (bf16[4,128,2048]{2,1,0:T(8,128)(2,1)}, bf16[4,128,2048]{2,1,0:T(8,128)(2,1)}, u32[]{:S(2)}, u32[]{:S(2)}) collective-permute-start(bf16[4,128,2048]{2,1,0:T(8,128)(2,1)} %get-tuple-element.172), channel_id=1, source_target_pairs={{0,6},{1,7},{2,4},{3,5},{4,2},{5,3},{6,0},{7,1},{8,14},{9,15},{10,... | collective-permute-start | bytes 6291464 | tf_op jit(solution)/shard_map/ppermute | solution.py:112
  722.3 89.9 %collective-permute-start.41 = (bf16[4,128,2048]{2,1,0:T(8,128)(2,1)}, bf16[4,128,2048]{2,1,0:T(8,128)(2,1)}, u32[]{:S(2)}, u32[]{:S(2)}) collective-permute-start(bf16[4,128,2048]{2,1,0:T(8,128)(2,1)} %get-tuple-element.173), channel_id=1, source_target_pairs={{0,2},{1,3},{2,0},{3,1},{4,6},{5,7},{6,4},{7,5},{8,10},{9,11},{10,... | collective-permute-start | bytes 6291464 | tf_op jit(solution)/shard_map/ppermute | solution.py:97
  723.7 92.0 %collective-permute-start.40 = (bf16[4,128,2048]{2,1,0:T(8,128)(2,1)}, bf16[4,128,2048]{2,1,0:T(8,128)(2,1)}, u32[]{:S(2)}, u32[]{:S(2)}) collective-permute-start(bf16[4,128,2048]{2,1,0:T(8,128)(2,1)} %get-tuple-element.171), channel_id=1, source_target_pairs={{0,4},{4,0},{8,12},{12,8},{16,20},{20,16},{24,28},{28,24},{1,5},{5... | collective-permute-start | bytes 6291464 | tf_op jit(solution)/shard_map/ppermute | solution.py:97
  808.8 106.9 %collective-permute-start.68 = (bf16[256,1024]{1,0:T(8,128)(2,1)}, bf16[256,1024]{1,0:T(8,128)(2,1)}, u32[]{:S(2)}, u32[]{:S(2)}) collective-permute-start(bf16[256,1024]{1,0:T(8,128)(2,1)} %get-tuple-element.182), channel_id=1, source_target_pairs={{0,4},{4,0},{16,20},{20,16},{24,28},{28,24},{8,12},{12,8},{1,5},{5... | collective-permute-start | bytes 1572872 | tf_op jit(solution)/shard_map/ppermute | solution.py:169
  810.2 111.4 %collective-permute-start.69 = (bf16[256,1024]{1,0:T(8,128)(2,1)}, bf16[256,1024]{1,0:T(8,128)(2,1)}, u32[]{:S(2)}, u32[]{:S(2)}) collective-permute-start(bf16[256,1024]{1,0:T(8,128)(2,1)} %get-tuple-element.181), channel_id=1, source_target_pairs={{0,16},{4,20},{16,24},{20,28},{24,8},{28,12},{8,0},{12,4},{1,17},{... | collective-permute-start | bytes 1572872 | tf_op jit(solution)/shard_map/ppermute | solution.py:169
  831.8 93.4 %collective-permute-start.70 = (bf16[256,1024]{1,0:T(8,128)(2,1)}, bf16[256,1024]{1,0:T(8,128)(2,1)}, u32[]{:S(2)}, u32[]{:S(2)}) collective-permute-start(bf16[256,1024]{1,0:T(8,128)(2,1)} %get-tuple-element.180), channel_id=1, source_target_pairs={{0,20},{4,16},{16,28},{20,24},{24,12},{28,8},{8,4},{12,0},{1,21},{... | collective-permute-start | bytes 1572872 | tf_op jit(solution)/shard_map/ppermute | solution.py:169
  863.5 72.0 %collective-permute-start.71 = (bf16[256,1024]{1,0:T(8,128)(2,1)}, bf16[256,1024]{1,0:T(8,128)(2,1)S(1)}, u32[]{:S(2)}, u32[]{:S(2)}) collective-permute-start(bf16[256,1024]{1,0:T(8,128)(2,1)} %get-tuple-element.179), channel_id=1, source_target_pairs={{0,24},{4,28},{16,8},{20,12},{24,0},{28,4},{8,16},{12,20},{1,25},{... | collective-permute-start | bytes 1572872 | tf_op jit(solution)/shard_map/ppermute | solution.py:169
  921.6 129.4 %collective-permute-start.74 = (bf16[256,1024]{1,0:T(8,128)(2,1)}, bf16[256,1024]{1,0:T(8,128)(2,1)}, u32[]{:S(2)}, u32[]{:S(2)}) collective-permute-start(bf16[256,1024]{1,0:T(8,128)(2,1)} %get-tuple-element.176), channel_id=1, source_target_pairs={{0,12},{4,8},{16,4},{20,0},{24,20},{28,16},{8,28},{12,24},{1,13},{... | collective-permute-start | bytes 1572872 | tf_op jit(solution)/shard_map/ppermute | solution.py:169
  1045.8 72.5 %all-to-all-start.6 = ((bf16[4,8,64,768]{3,2,1,0:T(8,128)(2,1)}), bf16[4,8,64,768]{3,2,1,0:T(8,128)(2,1)}, u32[]{:S(2)}, u32[]{:S(2)}) async-start(bf16[4,8,64,768]{3,2,1,0:T(8,128)(2,1)} %bitcast.292), calls=%async_computation.6 | async-start | bytes 6291456 | tf_op jit(solution)/shard_map/all_to_all | solution.py:65
  (157 other events, 3907.2 us)
Sparse Core Ops, SparseCore 0:
  10.1 159.7 all-gather.2
  172.7 150.1 all-gather.4
  898.2 141.0 reduce-scatter.1

commit v3 on v2

--- a/solution.py
+++ b/solution.py
@@ -5,6 +5,7 @@
 import jax.numpy as jnp
 from jax import lax
 from jax.experimental import pallas as pl
+from jax.experimental.pallas import tpu as pltpu
 from jax.sharding import PartitionSpec as P
 
 
@@ -268,6 +269,86 @@
     )(xa, xb, ya, yb, w1, w1t, w2, w2t, pick, place)
 
 
+def attend_kernel(scale, q, k, v, bias, out):
+    scores = dot_t(q[...], k[...]) * scale + bias[...]
+    weights = jnp.exp(scores - jnp.max(scores, axis=-1, keepdims=True))
+    probs = (weights / jnp.sum(weights, axis=-1, keepdims=True)).astype(BF)
+    out[...] = dot(probs, v[...]).astype(BF)
+
+
+def attend(q, k, v, bias, scale):
+    count, cols = q.shape
+    tile = min(256, count)
+    mine = pl.BlockSpec((tile, HD), lambda h, i: (i, h))
+    full = pl.BlockSpec((count, HD), lambda h, i: (0, h))
+    return pl.pallas_call(
+        partial(attend_kernel, scale),
+        grid=(cols // HD, count // tile),
+        in_specs=[mine, full, full, pl.BlockSpec((1, count), lambda h, i: (0, 0))],
+        out_specs=mine,
+        out_shape=jax.ShapeDtypeStruct((count, cols), BF),
+        cost_estimate=pl.CostEstimate(
+            flops=4 * count * count * cols,
+            transcendentals=count * count * cols // HD,
+            bytes_accessed=8 * count * cols,
+        ),
+        name="attend",
+    )(q, k, v, bias)
+
+
+def attend_back_kernel(scale, q, k, v, bias, grad, dq, dk, dv, dk_sum, dv_sum):
+    step = pl.program_id(1)
+    scores = dot_t(q[...], k[...]) * scale + bias[...]
+    weights = jnp.exp(scores - jnp.max(scores, axis=-1, keepdims=True))
+    probs = weights / jnp.sum(weights, axis=-1, keepdims=True)
+    prob_grad = dot_t(grad[...], v[...])
+    mean = jnp.sum(probs * prob_grad, axis=-1, keepdims=True)
+    score_grad = (probs * (prob_grad - mean)).astype(BF)
+    dq[...] = dot(score_grad, k[...]) * scale
+    dk_part = dot_rows(score_grad, q[...]) * scale
+    dv_part = dot_rows(probs.astype(BF), grad[...])
+
+    @pl.when(step == 0)
+    def _():
+        dk_sum[...] = dk_part
+        dv_sum[...] = dv_part
+
+    @pl.when(step > 0)
+    def _():
+        dk_sum[...] += dk_part
+        dv_sum[...] += dv_part
+
+    @pl.when(step == pl.num_programs(1) - 1)
+    def _():
+        dk[...] = dk_sum[...]
+        dv[...] = dv_sum[...].astype(BF)
+
+
+def attend_back(q, k, v, bias, grad, scale):
+    count, cols = q.shape
+    tile = min(256, count)
+    mine = pl.BlockSpec((tile, HD), lambda h, i: (i, h))
+    full = pl.BlockSpec((count, HD), lambda h, i: (0, h))
+    return pl.pallas_call(
+        partial(attend_back_kernel, scale),
+        grid=(cols // HD, count // tile),
+        in_specs=[mine, full, full, pl.BlockSpec((1, count), lambda h, i: (0, 0)), mine],
+        out_specs=[mine, full, full],
+        out_shape=[
+            jax.ShapeDtypeStruct((count, cols), F32),
+            jax.ShapeDtypeStruct((count, cols), F32),
+            jax.ShapeDtypeStruct((count, cols), BF),
+        ],
+        scratch_shapes=[pltpu.VMEM((count, HD), F32), pltpu.VMEM((count, HD), F32)],
+        cost_estimate=pl.CostEstimate(
+            flops=10 * count * count * cols,
+            transcendentals=count * count * cols // HD,
+            bytes_accessed=20 * count * cols,
+        ),
+        name="attend_back",
+    )(q, k, v, bias, grad)
+
+
 def lanes(count):
     return -(-count // 128) * 128
 
@@ -331,12 +412,14 @@
     wr_all = wr_all.transpose(1, 0, 2).reshape(expert_total, width)
     w1 = jnp.stack([w_gate, w_up]).astype(BF).reshape(2, local_count, cols, n_dp, ff_part)
     w1 = w1.transpose(3, 2, 0, 1, 4).reshape(n_dp, cols, -1)
+    dy_ring = jnp.stack(ring_blocks(cotangent))[None]
+    w1, dy_ring = lax.optimization_barrier((w1, dy_ring))
     w1 = walk_swap(w1, tables)
     w1 = w1.reshape(width, -1)
     w2 = w_down.astype(BF).reshape(local_count * ff_part, width)
     half = local_count * ff_part
     w1t, w2t = w1.T, w2.T
-    dy_near = gather_peers(jnp.stack(ring_blocks(cotangent))[None])
+    dy_near = gather_peers(dy_ring)
     dy_far = core_flip(dy_near)
 
     seq_in = seq_tokens.astype(F32)
@@ -350,18 +433,14 @@
     angles = position.astype(F32)[:, None] * frequency[None, :]
     query_rot, query_back = jax.vjp(partial(head_piece, angles), qkv_flat[:, :cols], gain_q)
     key_rot, key_back = jax.vjp(partial(head_piece, angles), qkv_flat[:, cols : 2 * cols], gain_k)
-    query_bf = query_rot.astype(BF)
-    key_bf = key_rot.astype(BF)
-    value_bf = qkv_flat[:, 2 * cols :].astype(BF).reshape(-1, cols // HD, HD)
-    scores = (
-        jnp.einsum("qhd,khd->hqk", query_bf, key_bf, preferred_element_type=F32) * score_scale
-    )
-    scores = jnp.where(visible[None, None, :], scores, -jnp.inf)
-    probs = jax.nn.softmax(scores, axis=-1)
-    probs_bf = probs.astype(BF)
-    attended = jnp.einsum("hqk,khd->qhd", probs_bf, value_bf, preferred_element_type=F32)
-    attended = swap(attended.astype(BF).reshape(n_dp, rows, cols), "dp")
+    query_bf = query_rot.astype(BF).reshape(-1, cols)
+    key_bf = key_rot.astype(BF).reshape(-1, cols)
+    value_bf = qkv_flat[:, 2 * cols :].astype(BF)
+    bias = jnp.where(visible, 0.0, -jnp.inf).astype(F32)[None, :]
+    attended = attend(query_bf, key_bf, value_bf, bias, score_scale)
+    attended = swap(attended.reshape(n_dp, rows, cols), "dp")
     attended = attended.transpose(1, 0, 2).reshape(rows, width)
+    attended, w1, w1t, w2t = lax.optimization_barrier((attended, w1, w1t, w2t))
 
     inputs = tokens.astype(F32)
     hidden_one = inputs + dot(attended, wo_all)
@@ -417,13 +496,10 @@
             pre_grads.append(pre_grad)
             gated_inners.append(gated_inner)
     returned = home(home_parts)
-    token_grads = returned[:, :width]
-    gg = returned[:, width : width + expert_total * n_dp].reshape(rows, expert_total, n_dp)
-    gg = jnp.sum(gg, axis=-1)
     if not lean:
         mix_near = jnp.stack([m[0].reshape(-1, rows, width) for m in mix_parts], axis=1)
         mix_far = jnp.stack([m[1].reshape(-1, rows, width) for m in mix_parts], axis=1)
-        mix_far, home_parts[-1] = lax.optimization_barrier((mix_far, home_parts[-1]))
+        mix_far, returned = lax.optimization_barrier((mix_far, returned))
         mix_near = add(mix_near, core_flip(mix_far))
         mix_parts = list(reduce_peers(mix_near))
         by_chunk = jnp.stack([g.reshape(2, -1, rows, half) for g in gated_inners], axis=2)
@@ -432,11 +508,15 @@
             by_chunk[1], dy_far.reshape(-1, width)
         )
         n2_all = jnp.concatenate([part[:, :width] for part in n2_sets], axis=0)
-        w1_grad = dot_rows(n2_all, jnp.concatenate(pre_grads, axis=0))
+        pre_all = jnp.concatenate(pre_grads, axis=0)
+        w1_grad = dot_rows(n2_all, pre_all)
+    w1_grad = w1_grad.astype(BF)
+    w1_grad, returned = lax.optimization_barrier((w1_grad, returned))
+    token_grads = returned[:, :width]
+    gg = returned[:, width : width + expert_total * n_dp].reshape(rows, expert_total, n_dp)
+    gg = jnp.sum(gg, axis=-1)
     mixed = home(mix_parts)
-    block_out = (hidden_one + mixed).astype(BF)
     down_grad = down_grad.reshape(local_count, ff_part, width)
-    w1_grad = w1_grad.astype(BF)
     w1_grad = walk_swap(w1_grad.reshape(n_dp, cols, -1), tables)
     w1_grad = (
         w1_grad.reshape(n_dp, cols, 2, local_count, ff_part)
@@ -455,23 +535,19 @@
     output_grad = scatter(dot_rows(attended, attn_grad_bf).astype(BF), BOTH).astype(F32)
     attended_grad = dot_t(attn_grad_bf, wo_all).astype(BF)
     attended_grad = swap(attended_grad.reshape(rows, n_dp, cols).transpose(1, 0, 2), "dp")
-    attended_grad = attended_grad.reshape(-1, cols // HD, HD)
-
-    prob_grad = jnp.einsum("qhd,khd->hqk", attended_grad, value_bf, preferred_element_type=F32)
-    score_grad = (
-        probs * (prob_grad - jnp.sum(probs * prob_grad, axis=-1, keepdims=True))
-    ).astype(BF)
-    query_grad = (
-        jnp.einsum("hqk,khd->qhd", score_grad, key_bf, preferred_element_type=F32) * score_scale
-    )
-    key_grad = (
-        jnp.einsum("hqk,qhd->khd", score_grad, query_bf, preferred_element_type=F32) * score_scale
-    )
-    value_grad = jnp.einsum("hqk,qhd->khd", probs_bf, attended_grad, preferred_element_type=F32)
+    attended_grad = attended_grad.reshape(-1, cols)
+
+    query_grad, key_grad, value_grad = attend_back(
+        query_bf, key_bf, value_bf, bias, attended_grad, score_scale
+    )
+    hidden_late, query_grad = lax.optimization_barrier((hidden_one, query_grad))
+    block_out = (hidden_late + mixed).astype(BF)
+    query_grad = query_grad.reshape(-1, cols // HD, HD)
+    key_grad = key_grad.reshape(-1, cols // HD, HD)
     query_flat_grad, query_gain_grad = query_back(query_grad)
     key_flat_grad, key_gain_grad = key_back(key_grad)
     qkv_grad = jnp.concatenate(
-        [query_flat_grad.astype(BF), key_flat_grad.astype(BF), value_grad.reshape(-1, cols).astype(BF)],
+        [query_flat_grad.astype(BF), key_flat_grad.astype(BF), value_grad],
         axis=1,
     )
     walk_grad = jnp.take(qkv_grad.reshape(n_dp, rows, 3 * cols), member_of_walk, axis=0)

time: 1190 us -> 1270 us (1.067)
  starting transfers between devices: 124 us -> 167 us
  local copies, waits for them, and re-layouts: 206 us -> 241 us
  other arithmetic: 117 us -> 89.1 us
  waiting for transfers between devices: 501 us -> 523 us
  Pallas kernels: 102 us -> 123 us
  matrix products: 99 us -> 79 us
    ppermute x14, waiting for transfers between devices: 67.8 us -> 196 us  [walk_swap(): block = lax.ppermute(block, 'dp', walk_perm(n_dp, index))]
    ppermute x10, waiting for transfers between devices: 63.2 us -> 11.6 us  [cross(): return lax.ppermute(vals, BOTH, pairs)]
    all_to_all x8, waiting for transfers between devices: 48.2 us -> 0.02 us  [swap(): return lax.all_to_all(blocks, axes, split_axis=0, concat_axis=0, tiled=True)]
    all_to_all x8, starting transfers between devices: 48.5 us -> 74.7 us  [swap(): return lax.all_to_all(blocks, axes, split_axis=0, concat_axis=0, tiled=True)]
    pallas_call x0 -> x2, Pallas kernels: none -> 21.6 us  [the longest x1 13.1 us: attend_back(): pl.pallas_call(partial(attend_back_kernel, scale), grid=(cols // HD, coun...]
    ppermute x15, waiting for transfers between devices: 137 us -> 117 us  [ring_shift(): return lax.ppermute(vals, 'dp', ring_perm(lax.axis_size('dp'), steps))]
    dot_general x5 -> x0, matrix products: 18 us -> none  [the longest x1 5.21 us: on_device(): jnp.einsum('hqk,qhd->khd', probs_bf, attended_grad, preferred_element_typ...]
    ppermute x36, waiting for transfers between devices: 184 us -> 198 us  [flip(): return lax.ppermute(vals, axis, [(i, i ^ bit) for i in range(size)])]
  transfers between devices with their start and end apart: 86 -> 86, of which waited for: 38 -> 35; matrix products, arithmetic and copies ran while one was open for 35% -> 31% of each run, Pallas kernels for 9% -> 10%
where the time goes in v3:
time: 1270 us; the launch traced here: 1250 us
  waiting for transfers between devices  523 us (41%)
  local copies, waits for them, and re-layouts  241 us (19%)
  starting transfers between devices  167 us (13%)
  Pallas kernels  123 us (10%)
  other arithmetic  89.1 us (7%)
  matrix products  79 us (6%)
  between operations  30.9 us (2%)
    ppermute x36, waiting for transfers between devices, flip(): return lax.ppermute(vals, axis, [(i, i ^ bit) for i in range(size)])  198 us
    ppermute x14, waiting for transfers between devices, walk_swap(): block = lax.ppermute(block, 'dp', walk_perm(n_dp, index))  196 us
    ppermute x15, waiting for transfers between devices, ring_shift(): return lax.ppermute(vals, 'dp', ring_perm(lax.axis_size('dp'), steps))  117 us
    pallas_call x4, Pallas kernels, experts(): pl.pallas_call(body, grid=(2 * halves,), in_specs=[pl.BlockSpec((tile, wi...  102 us
    unnamed x225, local copies, waits for them, and re-layouts  78.8 us
    all_to_all x8, starting transfers between devices, swap(): return lax.all_to_all(blocks, axes, split_axis=0, concat_axis=0, tiled=True)  74.7 us
    dot_general x6, matrix products, dot_rows(): lax.dot_general(left_mat, right_mat, (((0,), (0,)), ((), ())), preferred_...  59 us
    ppermute x36, starting transfers between devices, flip(): return lax.ppermute(vals, axis, [(i, i ^ bit) for i in range(size)])  32 us
  transfers between devices with their start and end apart: 86, of which 35 were waited for; matrix products, arithmetic and copies ran while one was open for 31% of the time, Pallas kernels for 10%

profile of v3, /device:TPU:13, one launch (start us, length us, event | category | flops | bytes accessed | tf_op | source)
XLA Modules:
  0.0 1253.4 jit_solution(14087944065591018427)
XLA Ops:
  73.5 28.1 %collective-permute-done.3 = bf16[128,2048]{1,0:T(8,128)(2,1)} collective-permute-done((bf16[128,2048]{1,0:T(8,128)(2,1)S(1)}, bf16[128,2048]{1,0:T(8,128)(2,1)}, u32[]{:S(2)}, u32[]{:S(2)}) %collective-permute-start.3) | collective-permute-done | bytes 524320 | tf_op jit(solution)/shard_map/ppermute | solution.py:93
  165.8 14.4 %collective-permute-done.7 = bf16[256,1024]{1,0:T(8,128)(2,1)S(1)} collective-permute-done((bf16[256,1024]{1,0:T(8,128)(2,1)}, bf16[256,1024]{1,0:T(8,128)(2,1)S(1)}, u32[]{:S(2)}, u32[]{:S(2)}) %collective-permute-start.7) | collective-permute-done | bytes 524320 | tf_op jit(solution)/shard_map/ppermute | solution.py:170
  186.2 33.6 %collective-permute-done.8 = bf16[256,1024]{1,0:T(8,128)(2,1)S(1)} collective-permute-done((bf16[256,1024]{1,0:T(8,128)(2,1)}, bf16[256,1024]{1,0:T(8,128)(2,1)S(1)}, u32[]{:S(2)}, u32[]{:S(2)}) %collective-permute-start.8) | collective-permute-done | bytes 524320 | tf_op jit(solution)/shard_map/ppermute | solution.py:170
  220.9 21.7 %collective-permute-done.9 = bf16[256,1024]{1,0:T(8,128)(2,1)S(1)} collective-permute-done((bf16[256,1024]{1,0:T(8,128)(2,1)}, bf16[256,1024]{1,0:T(8,128)(2,1)S(1)}, u32[]{:S(2)}, u32[]{:S(2)}) %collective-permute-start.9) | collective-permute-done | bytes 524320 | tf_op jit(solution)/shard_map/ppermute | solution.py:170
  244.4 10.0 collective-permute-done.10
  256.2 16.8 %collective-permute-done.11 = bf16[256,1024]{1,0:T(8,128)(2,1)S(1)} collective-permute-done((bf16[256,1024]{1,0:T(8,128)(2,1)S(1)}, bf16[256,1024]{1,0:T(8,128)(2,1)S(1)}, u32[]{:S(2)}, u32[]{:S(2)}) %collective-permute-start.11) | collective-permute-done | bytes 524320 | tf_op jit(solution)/shard_map/ppermute | solution.py:170
  322.6 10.6 all-to-all-start.2
  376.5 12.0 collective-permute-done.13
  400.3 17.0 %collective-permute-done.17 = bf16[128,2176]{1,0:T(8,128)(2,1)S(1)} collective-permute-done((bf16[128,2176]{1,0:T(8,128)(2,1)S(1)}, bf16[128,2176]{1,0:T(8,128)(2,1)S(1)}, u32[]{:S(2)}, u32[]{:S(2)}) %collective-permute-start.17) | collective-permute-done | bytes 557088 | tf_op jit(solution)/shard_map/ppermute | solution.py:98
  439.9 18.0 %collective-permute-done.23 = bf16[128,2176]{1,0:T(8,128)(2,1)S(1)} collective-permute-done((bf16[128,2176]{1,0:T(8,128)(2,1)S(1)}, bf16[128,2176]{1,0:T(8,128)(2,1)S(1)}, u32[]{:S(2)}, u32[]{:S(2)}) %collective-permute-start.23) | collective-permute-done | bytes 557088 | tf_op jit(solution)/shard_map/ppermute | solution.py:98
  480.5 10.7 collective-permute-done.29
  492.9 25.3 %experts.4 = (bf16[512,2048]{1,0:T(8,128)(2,1)}, bf16[512,2048]{1,0:T(8,128)(2,1)}, bf16[512,2176]{1,0:T(8,128)(2,1)}, bf16[512,2176]{1,0:T(8,128)(2,1)}, bf16[1...) custom-call(bf16[512,2176]{1,0:T(8,128)(2,1)} %pad_maximum_fusion.3.xa, bf16[512,2176]{1,0:T(8,128)(2,1)} %collective-permute-done.15.xb, ...), custom_call_target="tpu_custom_call" | custom-call | flops 12884901888 | bytes 20971520 | tf_op jit(solution)/shard_map/experts/pallas_call | solution.py:239
  524.8 25.3 %experts.5 = (bf16[512,2048]{1,0:T(8,128)(2,1)}, bf16[512,2048]{1,0:T(8,128)(2,1)}, bf16[512,2176]{1,0:T(8,128)(2,1)}, bf16[512,2176]{1,0:T(8,128)(2,1)}, bf16[1...) custom-call(bf16[512,2176]{1,0:T(8,128)(2,1)} %constant_dynamic-update-slice_fusion.xa, ...), custom_call_target="tpu_custom_call" | custom-call | flops 12884901888 | bytes 20971520 | tf_op jit(solution)/shard_map/experts/pallas_call | solution.py:239
  557.1 25.6 %experts.6 = (bf16[512,2048]{1,0:T(8,128)(2,1)}, bf16[512,2048]{1,0:T(8,128)(2,1)}, bf16[512,2176]{1,0:T(8,128)(2,1)}, bf16[512,2176]{1,0:T(8,128)(2,1)}, bf16[1...) custom-call(bf16[512,2176]{1,0:T(8,128)(2,1)} %constant_dynamic-update-slice_fusion.4.xa, ...), custom_call_target="tpu_custom_call" | custom-call | flops 12884901888 | bytes 20971520 | tf_op jit(solution)/shard_map/experts/pallas_call | solution.py:239
  589.1 25.4 %experts.7 = (bf16[512,2048]{1,0:T(8,128)(2,1)}, bf16[512,2048]{1,0:T(8,128)(2,1)}, bf16[512,2176]{1,0:T(8,128)(2,1)}, bf16[512,2176]{1,0:T(8,128)(2,1)}, bf16[1...) custom-call(bf16[512,2176]{1,0:T(8,128)(2,1)} %constant_dynamic-update-slice_fusion.8.xa, ...), custom_call_target="tpu_custom_call" | custom-call | flops 12884901888 | bytes 20971520 | tf_op jit(solution)/shard_map/experts/pallas_call | solution.py:239
  618.6 27.5 %fusion.14 = bf16[2048,1024]{1,0:T(8,128)(2,1)} fusion(bf16[4096,2048]{1,0:T(8,128)(2,1)} %slice_dynamic-update-slice_fusion, bf16[1024,1024]{1,0:T(8,128)(2,1)} %get-tuple-element.69, bf16[1024,1024]{1,0:T(8,128)(2,1)} %get-tuple-element.68, bf16[1024,1024]{1,0:T(8,128)(2,1)S(1)} %copy-done.87, bf16[1024,1024]{1,0:T(8,128)(2,1)S(1)} %copy-done.86), kind=kOutput, calls=%fused_computation.40 | convolution fusion | flops 17215520768 | bytes 29360128 | tf_op jit(solution)/shard_map/dot_general | solution.py:51
  659.6 29.5 %collective-permute-done.40 = bf16[128,2176]{1,0:T(8,128)(2,1)S(1)} collective-permute-done((bf16[128,2176]{1,0:T(8,128)(2,1)S(1)}, bf16[128,2176]{1,0:T(8,128)(2,1)S(1)}, u32[]{:S(2)}, u32[]{:S(2)}) %collective-permute-start.40) | collective-permute-done | bytes 557088 | tf_op jit(solution)/shard_map/ppermute | solution.py:98
  693.0 34.1 %collective-permute-done.45 = bf16[128,2176]{1,0:T(8,128)(2,1)S(1)} collective-permute-done((bf16[128,2176]{1,0:T(8,128)(2,1)S(1)}, bf16[128,2176]{1,0:T(8,128)(2,1)S(1)}, u32[]{:S(2)}, u32[]{:S(2)}) %collective-permute-start.45) | collective-permute-done | bytes 557088 | tf_op jit(solution)/shard_map/ppermute | solution.py:98
  730.1 22.0 %collective-permute-done.50 = bf16[128,2176]{1,0:T(8,128)(2,1)S(1)} collective-permute-done((bf16[128,2176]{1,0:T(8,128)(2,1)S(1)}, bf16[128,2176]{1,0:T(8,128)(2,1)S(1)}, u32[]{:S(2)}, u32[]{:S(2)}) %collective-permute-start.50) | collective-permute-done | bytes 557088 | tf_op jit(solution)/shard_map/ppermute | solution.py:98
  770.0 34.5 %collective-permute-done.48 = bf16[128,2176]{1,0:T(8,128)(2,1)S(1)} collective-permute-done((bf16[128,2176]{1,0:T(8,128)(2,1)S(1)}, bf16[128,2176]{1,0:T(8,128)(2,1)S(1)}, u32[]{:S(2)}, u32[]{:S(2)}) %collective-permute-start.48) | collective-permute-done | bytes 557088 | tf_op jit(solution)/shard_map/ppermute | solution.py:93
  823.8 9.7 convolution_add_fusion
  851.6 37.7 %collective-permute-done.68 = bf16[256,1024]{1,0:T(8,128)(2,1)} collective-permute-done((bf16[256,1024]{1,0:T(8,128)(2,1)}, bf16[256,1024]{1,0:T(8,128)(2,1)}, u32[]{:S(2)}, u32[]{:S(2)}) %collective-permute-start.68) | collective-permute-done | bytes 524320 | tf_op jit(solution)/shard_map/ppermute | solution.py:170
  897.6 27.6 %collective-permute-done.71 = bf16[256,1024]{1,0:T(8,128)(2,1)S(1)} collective-permute-done((bf16[256,1024]{1,0:T(8,128)(2,1)}, bf16[256,1024]{1,0:T(8,128)(2,1)S(1)}, u32[]{:S(2)}, u32[]{:S(2)}) %collective-permute-start.71) | collective-permute-done | bytes 524320 | tf_op jit(solution)/shard_map/ppermute | solution.py:170
  925.9 28.2 %collective-permute-done.72 = bf16[256,1024]{1,0:T(8,128)(2,1)S(1)} collective-permute-done((bf16[256,1024]{1,0:T(8,128)(2,1)}, bf16[256,1024]{1,0:T(8,128)(2,1)S(1)}, u32[]{:S(2)}, u32[]{:S(2)}) %collective-permute-start.72) | collective-permute-done | bytes 524320 | tf_op jit(solution)/shard_map/ppermute | solution.py:170
  962.6 13.1 %attend_back.1 = (f32[1024,256]{1,0:T(8,128)}, f32[1024,256]{1,0:T(8,128)}, bf16[1024,256]{1,0:T(8,128)(2,1)}) custom-call(bf16[1024,256]{1,0:T(8,128)(2,1)} %copy.351.q, bf16[1024,256]{1,0:T(8,128)(2,1)} %copy.352.k, bf16[1024,256]{1,0:T(8,128)(2,1)} %copy.360.v, f32[1,1024]{1,0:T(1,128)} %bitcast.356, bf16[1024,256]{1,0:T(8,128)(2,1)} %bitcast.341), custom_call_target="tpu_custom_call" | custom-call | flops 2684354560 | bytes 5242880 | tf_op jit(solution)/shard_map/attend_back/pallas_call | solution.py:332
  1008.4 31.8 %all-to-all-start.5 = ((f32[32,1,1160]{2,1,0:T(1,128)}), f32[32,1,1160]{2,1,0:T(1,128)S(1)}, u32[]{:S(2)}, u32[]{:S(2)}) async-start(f32[32,1,1160]{2,1,0:T(1,128)} %copy.338), calls=%async_computation.5 | async-start | bytes 327680 | tf_op jit(solution)/shard_map/all_to_all | solution.py:66
  1069.3 9.9 collective-permute-done.64
  1080.2 10.3 collective-permute-done.62
  1099.8 10.5 reshape.754
  1135.0 19.5 %collective-permute-done.65 = bf16[128,2048]{1,0:T(8,128)(2,1)} collective-permute-done((bf16[128,2048]{1,0:T(8,128)(2,1)}, bf16[128,2048]{1,0:T(8,128)(2,1)}, u32[]{:S(2)}, u32[]{:S(2)}) %collective-permute-start.65) | collective-permute-done | bytes 524320 | tf_op jit(solution)/shard_map/ppermute | solution.py:93
  1163.2 23.5 %collective-permute-done.55 = bf16[4,128,2048]{2,1,0:T(8,128)(2,1)} collective-permute-done((bf16[4,128,2048]{2,1,0:T(8,128)(2,1)}, bf16[4,128,2048]{2,1,0:T(8,128)(2,1)}, u32[]{:S(2)}, u32[]{:S(2)}) %collective-permute-start.55) | collective-permute-done | bytes 2097184 | tf_op jit(solution)/shard_map/ppermute | solution.py:98
  1221.0 21.5 %collective-permute-done.59 = bf16[128,2048]{1,0:T(8,128)(2,1)} collective-permute-done((bf16[128,2048]{1,0:T(8,128)(2,1)}, bf16[128,2048]{1,0:T(8,128)(2,1)}, u32[]{:S(2)}, u32[]{:S(2)}) %collective-permute-start.59) | collective-permute-done | bytes 524320 | tf_op jit(solution)/shard_map/ppermute | solution.py:93
  (565 shorter events, 536.9 us)
Async XLA Ops:
  7.2 283.2 %all-gather.3.cloned.1.call-start = ((), (), s32[]{:S(2)}) async-start(), calls=%async_computation.9 | async-start | bytes 4718592 | tf_op jit(solution)/shard_map/all_gather | solution.py:70
  8.0 343.6 %all-gather.5.cloned.1.call-start = ((), (), s32[]{:S(2)}) async-start(), calls=%async_computation.10 | async-start | bytes 8650752 | tf_op jit(solution)/shard_map/all_gather | solution.py:70
  39.9 67.5 %all-to-all-start.1 = ((bf16[8,64,3,256]{3,1,2,0:T(8,128)(2,1)}), bf16[8,64,3,256]{3,1,2,0:T(8,128)(2,1)S(1)}, u32[]{:S(2)}, u32[]{:S(2)}) async-start(bf16[8,64,3,256]{3,1,2,0:T(8,128)(2,1)} %copy.296), calls=%async_computation.1 | async-start | bytes 1572864 | tf_op jit(solution)/shard_map/all_to_all | solution.py:66
  127.8 151.1 %collective-permute-start.31 = (bf16[1,4,128,2048]{3,2,1,0:T(8,128)(2,1)}, bf16[1,4,128,2048]{3,2,1,0:T(8,128)(2,1)}, u32[]{:S(2)}, u32[]{:S(2)}) collective-permute-start(bf16[1,4,128,2048]{3,2,1,0:T(8,128)(2,1)} %maximum_bitcast_fusion.1), channel_id=1, source_target_pairs={{0,4},{4,0},{8,12},{12,8},{16,20},{20,16},{24,28},{28,24},{1,5},{5... | collective-permute-start | bytes 6291464 | tf_op jit(solution)/shard_map/ppermute | solution.py:98
  153.1 66.7 %collective-permute-start.8 = (bf16[256,1024]{1,0:T(8,128)(2,1)}, bf16[256,1024]{1,0:T(8,128)(2,1)S(1)}, u32[]{:S(2)}, u32[]{:S(2)}) collective-permute-start(bf16[256,1024]{1,0:T(8,128)(2,1)} %bitcast.347), channel_id=1, source_target_pairs={{0,24},{4,28},{16,8},{20,12},{24,0},{28,4},{8,16},{12,20},{1,25},{... | collective-permute-start | bytes 1572872 | tf_op jit(solution)/shard_map/ppermute | solution.py:170
  155.8 86.8 %collective-permute-start.9 = (bf16[256,1024]{1,0:T(8,128)(2,1)}, bf16[256,1024]{1,0:T(8,128)(2,1)S(1)}, u32[]{:S(2)}, u32[]{:S(2)}) collective-permute-start(bf16[256,1024]{1,0:T(8,128)(2,1)} %bitcast.343), channel_id=1, source_target_pairs={{0,28},{4,24},{16,12},{20,8},{24,4},{28,0},{8,20},{12,16},{1,29},{... | collective-permute-start | bytes 1572872 | tf_op jit(solution)/shard_map/ppermute | solution.py:170
  163.8 118.3 %collective-permute-start.1 = (bf16[2,8,64,768]{3,2,1,0:T(8,128)(2,1)}, bf16[2,8,64,768]{3,2,1,0:T(8,128)(2,1)}, u32[]{:S(2)}, u32[]{:S(2)}) collective-permute-start(bf16[2,8,64,768]{3,2,1,0:T(8,128)(2,1)} %pad_maximum_fusion.4), channel_id=1, source_target_pairs={{0,2},{1,3},{2,0},{3,1},{4,6},{5,7},{6,4},{7,5},{8,10},{9,11},{10,... | collective-permute-start | bytes 4718600 | tf_op jit(solution)/shard_map/ppermute | solution.py:98
  180.2 74.2 %collective-permute-start.10 = (bf16[256,1024]{1,0:T(8,128)(2,1)S(1)}, bf16[256,1024]{1,0:T(8,128)(2,1)S(1)}, u32[]{:S(2)}, u32[]{:S(2)}) collective-permute-start(bf16[256,1024]{1,0:T(8,128)(2,1)S(1)} %bitcast.342), channel_id=1, source_target_pairs={{0,8},{4,12},{16,0},{20,4},{24,16},{28,20},{8,24},{12,28},{1,9},{5... | collective-permute-start | bytes 1572872 | tf_op jit(solution)/shard_map/ppermute | solution.py:170
  242.7 94.8 %collective-permute-start.33 = (bf16[1,4,128,2048]{3,2,1,0:T(8,128)(2,1)}, bf16[1,4,128,2048]{3,2,1,0:T(8,128)(2,1)}, u32[]{:S(2)}, u32[]{:S(2)}) collective-permute-start(bf16[1,4,128,2048]{3,2,1,0:T(8,128)(2,1)} %maximum_bitcast_fusion.1), channel_id=1, source_target_pairs={{0,6},{1,7},{2,4},{3,5},{4,2},{5,3},{6,0},{7,1},{8,14},{9,15},{10,... | collective-permute-start | bytes 6291464 | tf_op jit(solution)/shard_map/ppermute | solution.py:113
  254.4 79.8 %collective-permute-start.32 = (bf16[1,4,128,2048]{3,2,1,0:T(8,128)(2,1)}, bf16[1,4,128,2048]{3,2,1,0:T(8,128)(2,1)}, u32[]{:S(2)}, u32[]{:S(2)}) collective-permute-start(bf16[1,4,128,2048]{3,2,1,0:T(8,128)(2,1)} %maximum_bitcast_fusion.1), channel_id=1, source_target_pairs={{0,2},{1,3},{2,0},{3,1},{4,6},{5,7},{6,4},{7,5},{8,10},{9,11},{10,... | collective-permute-start | bytes 6291464 | tf_op jit(solution)/shard_map/ppermute | solution.py:98
  333.3 911.6 %reduce-scatter.2.cloned.1.call-start = ((), (), s32[]{:S(2)}) async-start(), calls=%async_computation.11 | async-start | bytes 8650752 | tf_op jit(solution)/shard_map/reduce_scatter | solution.py:74
  340.8 152.1 %collective-permute-start.34 = (bf16[4,4,128,2048]{3,2,1,0:T(8,128)(2,1)}, bf16[4,4,128,2048]{3,2,1,0:T(8,128)(2,1)}, u32[]{:S(2)}, u32[]{:S(2)}) collective-permute-start(bf16[4,4,128,2048]{3,2,1,0:T(8,128)(2,1)} %constant_dynamic-update-slice_fusion.12.ya), channel_id=1, source_target_pairs={{0,1},{1,0},{2,3},{3,2},{4,5},{5,4},{6,7},{7,6},{8,9},{9,8},{10,11... | collective-permute-start | bytes 25165832 | tf_op jit(solution)/shard_map/ppermute | solution.py:98
  430.0 62.9 %collective-permute-start.15 = (bf16[512,2176]{1,0:T(8,128)(2,1)S(1)}, bf16[512,2176]{1,0:T(8,128)(2,1)}, u32[]{:S(2)}, u32[]{:S(2)}) collective-permute-start(bf16[512,2176]{1,0:T(8,128)(2,1)S(1)} %copy-done.15), channel_id=1, source_target_pairs={{0,1},{1,0},{2,3},{3,2},{4,5},{5,4},{6,7},{7,6},{8,9},{9,8},{10,11... | collective-permute-start | bytes 6684680 | tf_op jit(solution)/shard_map/ppermute | solution.py:98
  462.5 62.3 %collective-permute-start.20 = (bf16[512,2176]{1,0:T(8,128)(2,1)}, bf16[512,2176]{1,0:T(8,128)(2,1)}, u32[]{:S(2)}, u32[]{:S(2)}) collective-permute-start(bf16[512,2176]{1,0:T(8,128)(2,1)} %constant_dynamic-update-slice_fusion.xa), channel_id=1, source_target_pairs={{0,1},{1,0},{2,3},{3,2},{4,5},{5,4},{6,7},{7,6},{8,9},{9,8},{10,11... | collective-permute-start | bytes 6684680 | tf_op jit(solution)/shard_map/ppermute | solution.py:98
  478.3 78.8 %collective-permute-start.25 = (bf16[512,2176]{1,0:T(8,128)(2,1)}, bf16[512,2176]{1,0:T(8,128)(2,1)}, u32[]{:S(2)}, u32[]{:S(2)}) collective-permute-start(bf16[512,2176]{1,0:T(8,128)(2,1)} %constant_dynamic-update-slice_fusion.4.xa), channel_id=1, source_target_pairs={{0,1},{1,0},{2,3},{3,2},{4,5},{5,4},{6,7},{7,6},{8,9},{9,8},{10,11... | collective-permute-start | bytes 6684680 | tf_op jit(solution)/shard_map/ppermute | solution.py:98
  492.0 97.1 %collective-permute-start.30 = (bf16[512,2176]{1,0:T(8,128)(2,1)}, bf16[512,2176]{1,0:T(8,128)(2,1)}, u32[]{:S(2)}, u32[]{:S(2)}) collective-permute-start(bf16[512,2176]{1,0:T(8,128)(2,1)} %constant_dynamic-update-slice_fusion.8.xa), channel_id=1, source_target_pairs={{0,1},{1,0},{2,3},{3,2},{4,5},{5,4},{6,7},{7,6},{8,9},{9,8},{10,11... | collective-permute-start | bytes 6684680 | tf_op jit(solution)/shard_map/ppermute | solution.py:98
  518.3 131.9 %collective-permute-start.35 = (bf16[512,2176]{1,0:T(8,128)(2,1)}, bf16[512,2176]{1,0:T(8,128)(2,1)S(1)}, u32[]{:S(2)}, u32[]{:S(2)}) collective-permute-start(bf16[512,2176]{1,0:T(8,128)(2,1)} %get-tuple-element.75), channel_id=1, source_target_pairs={{0,1},{1,0},{2,3},{3,2},{4,5},{5,4},{6,7},{7,6},{8,9},{9,8},{10,11... | collective-permute-start | bytes 6684680 | tf_op jit(solution)/shard_map/ppermute | solution.py:98
  550.1 100.9 %collective-permute-start.39 = (bf16[512,2176]{1,0:T(8,128)(2,1)}, bf16[512,2176]{1,0:T(8,128)(2,1)}, u32[]{:S(2)}, u32[]{:S(2)}) collective-permute-start(bf16[512,2176]{1,0:T(8,128)(2,1)} %get-tuple-element.77), channel_id=1, source_target_pairs={{0,1},{1,0},{2,3},{3,2},{4,5},{5,4},{6,7},{7,6},{8,9},{9,8},{10,11... | collective-permute-start | bytes 6684680 | tf_op jit(solution)/shard_map/ppermute | solution.py:98
  582.7 73.4 %collective-permute-start.44 = (bf16[512,2176]{1,0:T(8,128)(2,1)}, bf16[512,2176]{1,0:T(8,128)(2,1)}, u32[]{:S(2)}, u32[]{:S(2)}) collective-permute-start(bf16[512,2176]{1,0:T(8,128)(2,1)} %get-tuple-element.79), channel_id=1, source_target_pairs={{0,1},{1,0},{2,3},{3,2},{4,5},{5,4},{6,7},{7,6},{8,9},{9,8},{10,11... | collective-permute-start | bytes 6684680 | tf_op jit(solution)/shard_map/ppermute | solution.py:98
  614.5 77.4 %collective-permute-start.49 = (bf16[512,2176]{1,0:T(8,128)(2,1)}, bf16[512,2176]{1,0:T(8,128)(2,1)S(1)}, u32[]{:S(2)}, u32[]{:S(2)}) collective-permute-start(bf16[512,2176]{1,0:T(8,128)(2,1)} %get-tuple-element.81), channel_id=1, source_target_pairs={{0,1},{1,0},{2,3},{3,2},{4,5},{5,4},{6,7},{7,6},{8,9},{9,8},{10,11... | collective-permute-start | bytes 6684680 | tf_op jit(solution)/shard_map/ppermute | solution.py:98
  650.8 107.7 %collective-permute-start.36 = (bf16[128,2176]{1,0:T(8,128)(2,1)S(1)}, bf16[128,2176]{1,0:T(8,128)(2,1)S(1)}, u32[]{:S(2)}, u32[]{:S(2)}) collective-permute-start(bf16[128,2176]{1,0:T(8,128)(2,1)S(1)} %get-tuple-element.232), channel_id=1, source_target_pairs={{0,4},{4,0},{8,12},{12,8},{16,20},{20,16},{24,28},{28,24},{1,5},{5... | collective-permute-start | bytes 1671176 | tf_op jit(solution)/shard_map/ppermute | solution.py:98
  689.0 73.8 %collective-permute-start.38 = (bf16[128,2176]{1,0:T(8,128)(2,1)S(1)}, bf16[128,2176]{1,0:T(8,128)(2,1)S(1)}, u32[]{:S(2)}, u32[]{:S(2)}) collective-permute-start(bf16[128,2176]{1,0:T(8,128)(2,1)S(1)} %get-tuple-element.233), channel_id=1, source_target_pairs={{0,6},{1,7},{2,4},{3,5},{4,2},{5,3},{6,0},{7,1},{8,14},{9,15},{10,... | collective-permute-start | bytes 1671176 | tf_op jit(solution)/shard_map/ppermute | solution.py:113
  821.3 224.9 %collective-permute-start.54 = (bf16[4,4,128,2048]{3,2,1,0:T(8,128)(2,1)}, bf16[4,4,128,2048]{3,2,1,0:T(8,128)(2,1)}, u32[]{:S(2)}, u32[]{:S(2)}) collective-permute-start(bf16[4,4,128,2048]{3,2,1,0:T(8,128)(2,1)} %pad_maximum_fusion), channel_id=1, source_target_pairs={{0,1},{1,0},{2,3},{3,2},{4,5},{5,4},{6,7},{7,6},{8,9},{9,8},{10,11... | collective-permute-start | bytes 25165832 | tf_op jit(solution)/shard_map/ppermute | solution.py:98
  835.5 61.2 %collective-permute-start.70 = (bf16[256,1024]{1,0:T(8,128)(2,1)}, bf16[256,1024]{1,0:T(8,128)(2,1)S(1)}, u32[]{:S(2)}, u32[]{:S(2)}) collective-permute-start(bf16[256,1024]{1,0:T(8,128)(2,1)} %get-tuple-element.208), channel_id=1, source_target_pairs={{0,20},{4,16},{16,28},{20,24},{24,12},{28,8},{8,4},{12,0},{1,21},{... | collective-permute-start | bytes 1572872 | tf_op jit(solution)/shard_map/ppermute | solution.py:170
  845.0 116.9 %all-to-all-start.4 = ((bf16[8,128,256]{2,1,0:T(8,128)(2,1)}), bf16[8,128,256]{2,1,0:T(8,128)(2,1)S(1)}, u32[]{:S(2)}, u32[]{:S(2)}) async-start(bf16[8,128,256]{2,1,0:T(8,128)(2,1)} %bitcast.269), calls=%async_computation.4 | async-start | bytes 1048576 | tf_op jit(solution)/shard_map/all_to_all | solution.py:66
  849.2 106.6 %collective-permute-start.74 = (bf16[256,1024]{1,0:T(8,128)(2,1)S(1)}, bf16[256,1024]{1,0:T(8,128)(2,1)S(1)}, u32[]{:S(2)}, u32[]{:S(2)}) collective-permute-start(bf16[256,1024]{1,0:T(8,128)(2,1)S(1)} %copy-done.57), channel_id=1, source_target_pairs={{0,12},{4,8},{16,4},{20,0},{24,20},{28,16},{8,28},{12,24},{1,13},{... | collective-permute-start | bytes 1572872 | tf_op jit(solution)/shard_map/ppermute | solution.py:170
  891.2 63.0 %collective-permute-start.72 = (bf16[256,1024]{1,0:T(8,128)(2,1)}, bf16[256,1024]{1,0:T(8,128)(2,1)S(1)}, u32[]{:S(2)}, u32[]{:S(2)}) collective-permute-start(bf16[256,1024]{1,0:T(8,128)(2,1)} %get-tuple-element.206), channel_id=1, source_target_pairs={{0,28},{4,24},{16,12},{20,8},{24,4},{28,0},{8,20},{12,16},{1,29},{... | collective-permute-start | bytes 1572872 | tf_op jit(solution)/shard_map/ppermute | solution.py:170
  1043.2 75.4 %collective-permute-start.61 = (bf16[128,2048]{1,0:T(8,128)(2,1)}, bf16[128,2048]{1,0:T(8,128)(2,1)}, u32[]{:S(2)}, u32[]{:S(2)}) collective-permute-start(bf16[128,2048]{1,0:T(8,128)(2,1)} %get-tuple-element.212), channel_id=1, source_target_pairs={{0,4},{4,0},{8,12},{12,8},{16,20},{20,16},{24,28},{28,24},{1,5},{5... | collective-permute-start | bytes 1572872 | tf_op jit(solution)/shard_map/ppermute | solution.py:98
  1057.8 128.9 %collective-permute-start.55 = (bf16[4,128,2048]{2,1,0:T(8,128)(2,1)}, bf16[4,128,2048]{2,1,0:T(8,128)(2,1)}, u32[]{:S(2)}, u32[]{:S(2)}) collective-permute-start(bf16[4,128,2048]{2,1,0:T(8,128)(2,1)} %get-tuple-element.199), channel_id=1, source_target_pairs={{0,4},{4,0},{8,12},{12,8},{16,20},{20,16},{24,28},{28,24},{1,5},{5... | collective-permute-start | bytes 6291464 | tf_op jit(solution)/shard_map/ppermute | solution.py:98
  1058.1 98.9 %all-to-all-start.6 = ((bf16[4,8,64,768]{3,2,1,0:T(8,128)(2,1)}), bf16[4,8,64,768]{3,2,1,0:T(8,128)(2,1)S(1)}, u32[]{:S(2)}, u32[]{:S(2)}) async-start(bf16[4,8,64,768]{3,2,1,0:T(8,128)(2,1)} %bitcast.267), calls=%async_computation.6 | async-start | bytes 6291456 | tf_op jit(solution)/shard_map/all_to_all | solution.py:66
  1068.0 118.7 %collective-permute-start.57 = (bf16[4,128,2048]{2,1,0:T(8,128)(2,1)}, bf16[4,128,2048]{2,1,0:T(8,128)(2,1)}, u32[]{:S(2)}, u32[]{:S(2)}) collective-permute-start(bf16[4,128,2048]{2,1,0:T(8,128)(2,1)} %get-tuple-element.200), channel_id=1, source_target_pairs={{0,6},{1,7},{2,4},{3,5},{4,2},{5,3},{6,0},{7,1},{8,14},{9,15},{10,... | collective-permute-start | bytes 6291464 | tf_op jit(solution)/shard_map/ppermute | solution.py:113
  1079.3 110.2 %collective-permute-start.56 = (bf16[4,128,2048]{2,1,0:T(8,128)(2,1)}, bf16[4,128,2048]{2,1,0:T(8,128)(2,1)}, u32[]{:S(2)}, u32[]{:S(2)}) collective-permute-start(bf16[4,128,2048]{2,1,0:T(8,128)(2,1)} %get-tuple-element.201), channel_id=1, source_target_pairs={{0,2},{1,3},{2,0},{3,1},{4,6},{5,7},{6,4},{7,5},{8,10},{9,11},{10,... | collective-permute-start | bytes 6291464 | tf_op jit(solution)/shard_map/ppermute | solution.py:98
  (144 other events, 4573.1 us)
Sparse Core Ops, SparseCore 0:
  10.2 112.7 all-gather.2
  125.8 185.2 all-gather.4
  813.6 180.4 reduce-scatter.1

commit v4 on v3

--- a/solution.py
+++ b/solution.py
@@ -120,20 +120,65 @@
 
 def ring_blocks(vals):
     blocks = [vals]
-    for _ in range(1, lax.axis_size("dp") // 2):
-        blocks.append(ring_shift(blocks[-1], 1))
+    for step in range(1, lax.axis_size("dp") // 2):
+        blocks.append(ring_shift(vals, step))
     return blocks
+
+
+def pick_rows(vals, index):
+    return vals.at[index].get(mode="promise_in_bounds")
+
+
+def add32(left, right):
+    return left.astype(F32) + right.astype(F32)
 
 
 def add(left, right):
     return (left.astype(F32) + right.astype(F32)).astype(left.dtype)
 
 
+def x_flip(vals):
+    return flip(vals, "expert", 2)
+
+
+def y_flip(vals):
+    return flip(vals, "dp", 1)
+
+
+def split_at(width):
+    return width // 256 * 128
+
+
 def gather_peers(vals):
-    return jnp.concatenate([vals] + [cross(vals, *peer) for peer in peers()], axis=0)
+    if lax.axis_size("expert") != 4:
+        return jnp.stack([vals] + [cross(vals, *peer) for peer in peers()])
+    cut = split_at(vals.shape[-1])
+    left, right = vals[..., :cut], vals[..., cut:]
+    left_y, right_x = y_flip(left), x_flip(right)
+    left_pair, right_pair = jnp.stack([left, left_y]), jnp.stack([right, right_x])
+    left_far, right_far = x_flip(left_pair), y_flip(right_pair)
+    return jnp.stack(
+        [
+            vals,
+            jnp.concatenate([left_y, right_far[0]], axis=-1),
+            jnp.concatenate([left_far[0], right_x], axis=-1),
+            jnp.concatenate([left_far[1], right_far[1]], axis=-1),
+        ]
+    )
 
 
 def reduce_peers(vals):
+    if lax.axis_size("expert") == 4:
+        cut = split_at(vals.shape[-1])
+        own, at_y, at_x, at_xy = vals[0], vals[1], vals[2], vals[3]
+        left = x_flip(jnp.stack([at_x[..., :cut], at_xy[..., :cut]]))
+        right = y_flip(jnp.stack([at_y[..., cut:], at_xy[..., cut:]]))
+        left_y = add(at_y[..., :cut], left[1])
+        right_x = add(at_x[..., cut:], right[1])
+        left_y, right_x = y_flip(left_y), x_flip(right_x)
+        left = add(add32(own[..., :cut], left[0]), left_y).astype(vals.dtype)
+        right = add(add32(own[..., cut:], right[0]), right_x).astype(vals.dtype)
+        return jnp.concatenate([left, right], axis=-1)
     total = vals[0].astype(F32)
     for spot, peer in enumerate(peers()):
         total = total + cross(vals[spot + 1], *peer).astype(F32)
@@ -169,7 +214,7 @@
         if index:
             block = lax.ppermute(block, "dp", walk_perm(n_dp, index))
         moved.append(block)
-    return jnp.take(jnp.stack(moved), step_of, axis=0)
+    return pick_rows(jnp.stack(moved), step_of)
 
 
 def home(parts):
@@ -384,13 +429,17 @@
     wrows = w_query.shape[0]
     score_scale = 1.0 / math.sqrt(HD)
 
-    gains = jnp.concatenate([attn_gain, moe_gain, query_gain, key_gain])
+    gains = jnp.concatenate(
+        [attn_gain, moe_gain, query_gain, key_gain, w_router.T.reshape(-1)]
+    )
     gains_all = swap(jnp.broadcast_to(gains, (n_all, gains.shape[0])), BOTH)
     gw, hw = attn_gain.shape[0], query_gain.shape[0]
     gain_one = gains_all[:, :gw].reshape(-1)
     gain_two = gains_all[:, gw : 2 * gw].reshape(-1)
     gain_q = gains_all[:, 2 * gw : 2 * gw + hw].reshape(-1)
-    gain_k = gains_all[:, 2 * gw + hw :].reshape(-1)
+    gain_k = gains_all[:, 2 * gw + hw : 2 * gw + 2 * hw].reshape(-1)
+    wr_all = gains_all[:, 2 * gw + 2 * hw :].reshape(n_all, expert_total, wrows)
+    wr_all = wr_all.transpose(1, 0, 2).reshape(expert_total, width).astype(BF)
 
     seq_tokens = gather(tokens, "dp")
     member = lax.axis_index("dp")
@@ -403,17 +452,12 @@
     while bit < n_ex:
         qkv = jnp.concatenate([qkv, flip(qkv, "expert", bit)], axis=0)
         bit *= 2
-    qkv = jnp.take(qkv, seq_id ^ jnp.arange(n_ex, dtype=jnp.int32), axis=0)
+    qkv = pick_rows(qkv, seq_id ^ jnp.arange(n_ex, dtype=jnp.int32))
     qkv = qkv.transpose(1, 0, 2, 3).reshape(width, 3 * cols)
     wo_all = gather(w_output.astype(BF), BOTH)
-    wr_all = swap(
-        jnp.broadcast_to(w_router.astype(BF).T, (n_all, expert_total, wrows)), BOTH
-    )
-    wr_all = wr_all.transpose(1, 0, 2).reshape(expert_total, width)
     w1 = jnp.stack([w_gate, w_up]).astype(BF).reshape(2, local_count, cols, n_dp, ff_part)
     w1 = w1.transpose(3, 2, 0, 1, 4).reshape(n_dp, cols, -1)
-    dy_ring = jnp.stack(ring_blocks(cotangent))[None]
-    w1, dy_ring = lax.optimization_barrier((w1, dy_ring))
+    dy_ring = jnp.stack(ring_blocks(cotangent))
     w1 = walk_swap(w1, tables)
     w1 = w1.reshape(width, -1)
     w2 = w_down.astype(BF).reshape(local_count * ff_part, width)
@@ -467,11 +511,8 @@
     lean = n_all * rows > 4096
     n2_sets, mix_parts, home_parts, pre_grads, gated_inners = [], [], [], [], []
     w1_grad, down_grad = 0.0, 0.0
-    near = None
     for step, block in enumerate(ring_blocks(payload)):
-        if near is not None and not lean:
-            block, near = lax.optimization_barrier((block, near))
-        near = gather_peers(block)
+        near = gather_peers(block).reshape(-1, block.shape[-1])
         far = core_flip(near)
         ma, mb, ra, rb, pre_grad, gated_inner = experts(
             step, near, far, dy_near, dy_far, w1, w1t, w2, w2t, pick, place
@@ -550,9 +591,9 @@
         [query_flat_grad.astype(BF), key_flat_grad.astype(BF), value_grad],
         axis=1,
     )
-    walk_grad = jnp.take(qkv_grad.reshape(n_dp, rows, 3 * cols), member_of_walk, axis=0)
+    walk_grad = pick_rows(qkv_grad.reshape(n_dp, rows, 3 * cols), member_of_walk)
     part_grad = dot_t(walk_grad.reshape(-1, 3 * cols), qkv)
-    walk_in = jnp.take(seq_tokens.reshape(n_dp, rows, width), member_of_walk, axis=0)
+    walk_in = pick_rows(seq_tokens.reshape(n_dp, rows, width), member_of_walk)
     seq_in = walk_in.reshape(-1, width).astype(F32)
     seq_scale = lax.rsqrt(jnp.mean(seq_in * seq_in, axis=-1, keepdims=True) + norm_eps)
     norm_one_grad = jnp.sum(part_grad * (seq_in * seq_scale), axis=0)

time: 1270 us -> 1290 us (1.016)
  waiting for transfers between devices: 523 us -> 557 us
  other arithmetic: 89.1 us -> 114 us
  local copies, waits for them, and re-layouts: 241 us -> 219 us
    ppermute x15, waiting for transfers between devices: 117 us -> 177 us  [ring_shift(): return lax.ppermute(vals, 'dp', ring_perm(lax.axis_size('dp'), steps))]
    ppermute x14, waiting for transfers between devices: 196 us -> 153 us  [walk_swap(): block = lax.ppermute(block, 'dp', walk_perm(n_dp, index))]
    another operation x4 -> x46, other arithmetic: 1.24 us -> 34.6 us  [the longest x21 23 us: gather_peers(): jnp.stack([vals, jnp.concatenate([left_y, right_far[0]], axis=-1), jnp.co...]
    all_to_all x8 -> x7, waiting for transfers between devices: 0.02 us -> 28.1 us  [swap(): return lax.all_to_all(blocks, axes, split_axis=0, concat_axis=0, tiled=True)]
    ppermute x36 -> x56, starting transfers between devices: 32 us -> 50 us  [flip(): return lax.ppermute(vals, axis, [(i, i ^ bit) for i in range(size)])]
    unnamed x225 -> x202, local copies, waits for them, and re-layouts: 78.8 us -> 64.5 us
    ppermute x10 -> x0, starting transfers between devices: 13.1 us -> none  [cross(): return lax.ppermute(vals, BOTH, pairs)]
    all_to_all x8 -> x7, starting transfers between devices: 74.7 us -> 65.9 us  [swap(): return lax.all_to_all(blocks, axes, split_axis=0, concat_axis=0, tiled=True)]
  transfers between devices with their start and end apart: 86 -> 95, of which waited for: 35 -> 40; matrix products, arithmetic and copies ran while one was open for 31% -> 31% of each run, Pallas kernels for 10% -> 10%
where the time goes in v4:
time: 1290 us; the launch traced here: 1280 us
  waiting for transfers between devices  557 us (43%)
  local copies, waits for them, and re-layouts  219 us (17%)
  starting transfers between devices  157 us (12%)
  Pallas kernels  124 us (10%)
  other arithmetic  114 us (9%)
  matrix products  77.4 us (6%)
  between operations  31.4 us (2%)
    ppermute x56, waiting for transfers between devices, flip(): return lax.ppermute(vals, axis, [(i, i ^ bit) for i in range(size)])  198 us
    ppermute x15, waiting for transfers between devices, ring_shift(): return lax.ppermute(vals, 'dp', ring_perm(lax.axis_size('dp'), steps))  177 us
    ppermute x14, waiting for transfers between devices, walk_swap(): block = lax.ppermute(block, 'dp', walk_perm(n_dp, index))  153 us
    pallas_call x4, Pallas kernels, experts(): pl.pallas_call(body, grid=(2 * halves,), in_specs=[pl.BlockSpec((tile, wi...  102 us
    all_to_all x7, starting transfers between devices, swap(): return lax.all_to_all(blocks, axes, split_axis=0, concat_axis=0, tiled=True)  65.9 us
    unnamed x202, local copies, waits for them, and re-layouts  64.5 us
    dot_general x6, matrix products, dot_rows(): lax.dot_general(left_mat, right_mat, (((0,), (0,)), ((), ())), preferred_...  53.9 us
    ppermute x56, starting transfers between devices, flip(): return lax.ppermute(vals, axis, [(i, i ^ bit) for i in range(size)])  50 us
  transfers between devices with their start and end apart: 95, of which 40 were waited for; matrix products, arithmetic and copies ran while one was open for 31% of the time, Pallas kernels for 10%

profile of v4, /device:TPU:13, one launch (start us, length us, event | category | flops | bytes accessed | tf_op | source)
XLA Modules:
  0.0 1280.1 jit_solution(15598830988639574698)
XLA Ops:
  69.7 51.5 %collective-permute-done.33 = bf16[128,2048]{1,0:T(8,128)(2,1)} collective-permute-done((bf16[128,2048]{1,0:T(8,128)(2,1)}, bf16[128,2048]{1,0:T(8,128)(2,1)}, u32[]{:S(2)}, u32[]{:S(2)}) %collective-permute-start.33) | collective-permute-done | bytes 524320 | tf_op jit(solution)/shard_map/ppermute | solution.py:93
  168.9 24.8 %all-to-all-done.1 = bf16[8,64,3,256]{3,1,2,0:T(8,128)(2,1)} async-done(((bf16[8,64,3,256]{3,1,2,0:T(8,128)(2,1)}), bf16[8,64,3,256]{3,1,2,0:T(8,128)(2,1)}, u32[]{:S(2)}, u32[]{:S(2)}) %all-to-all-start.1) | async-done | bytes 786464 | tf_op jit(solution)/shard_map/all_to_all | solution.py:66
  199.7 16.8 %collective-permute-done.5 = bf16[256,1024]{1,0:T(8,128)(2,1)} collective-permute-done((bf16[256,1024]{1,0:T(8,128)(2,1)}, bf16[256,1024]{1,0:T(8,128)(2,1)}, u32[]{:S(2)}, u32[]{:S(2)}) %collective-permute-start.5) | collective-permute-done | bytes 524320 | tf_op jit(solution)/shard_map/ppermute | solution.py:215
  223.1 12.9 %collective-permute-done.6 = bf16[256,1024]{1,0:T(8,128)(2,1)} collective-permute-done((bf16[256,1024]{1,0:T(8,128)(2,1)}, bf16[256,1024]{1,0:T(8,128)(2,1)}, u32[]{:S(2)}, u32[]{:S(2)}) %collective-permute-start.6) | collective-permute-done | bytes 524320 | tf_op jit(solution)/shard_map/ppermute | solution.py:215
  238.1 23.2 %collective-permute-done.7 = bf16[256,1024]{1,0:T(8,128)(2,1)S(1)} collective-permute-done((bf16[256,1024]{1,0:T(8,128)(2,1)}, bf16[256,1024]{1,0:T(8,128)(2,1)S(1)}, u32[]{:S(2)}, u32[]{:S(2)}) %collective-permute-start.7) | collective-permute-done | bytes 524320 | tf_op jit(solution)/shard_map/ppermute | solution.py:215
  387.0 34.2 %collective-permute-done.20 = bf16[128,2176]{1,0:T(8,128)(2,1)S(1)} collective-permute-done((bf16[128,2176]{1,0:T(8,128)(2,1)S(1)}, bf16[128,2176]{1,0:T(8,128)(2,1)S(1)}, u32[]{:S(2)}, u32[]{:S(2)}) %collective-permute-start.20) | collective-permute-done | bytes 557088 | tf_op jit(solution)/shard_map/ppermute | solution.py:93
  453.0 29.1 %collective-permute-done.18 = bf16[2,128,1024]{2,1,0:T(8,128)(2,1)S(1)} collective-permute-done((bf16[2,128,1024]{2,1,0:T(8,128)(2,1)S(1)}, bf16[2,128,1024]{2,1,0:T(8,128)(2,1)S(1)}, u32[]{:S(2)}, u32[]{:S(2)}) %collective-permute-start.18) | collective-permute-done | bytes 524320 | tf_op jit(solution)/shard_map/ppermute | solution.py:98
  487.0 20.0 %collective-permute-done.17 = bf16[2,128,1152]{2,1,0:T(8,128)(2,1)S(1)} collective-permute-done((bf16[2,128,1152]{2,1,0:T(8,128)(2,1)S(1)}, bf16[2,128,1152]{2,1,0:T(8,128)(2,1)S(1)}, u32[]{:S(2)}, u32[]{:S(2)}) %collective-permute-start.17) | collective-permute-done | bytes 589856 | tf_op jit(solution)/shard_map/ppermute | solution.py:98
  516.9 25.9 %experts.4 = (bf16[512,2048]{1,0:T(8,128)(2,1)}, bf16[512,2048]{1,0:T(8,128)(2,1)}, bf16[512,2176]{1,0:T(8,128)(2,1)}, bf16[512,2176]{1,0:T(8,128)(2,1)}, bf16[1...) custom-call(bf16[512,2176]{1,0:T(8,128)(2,1)} %bitcast.537, bf16[512,2176]{1,0:T(8,128)(2,1)} %collective-permute-done.13.xb, ...), custom_call_target="tpu_custom_call" | custom-call | flops 12884901888 | bytes 20971520 | tf_op jit(solution)/shard_map/experts/pallas_call | solution.py:284
  549.8 25.4 %experts.7 = (bf16[512,2048]{1,0:T(8,128)(2,1)}, bf16[512,2048]{1,0:T(8,128)(2,1)}, bf16[512,2176]{1,0:T(8,128)(2,1)}, bf16[512,2176]{1,0:T(8,128)(2,1)}, bf16[1...) custom-call(bf16[512,2176]{1,0:T(8,128)(2,1)} %bitcast.103.xa, bf16[512,2176]{1,0:T(8,128)(2,1)} %collective-permute-done.31.xb, ...), custom_call_target="tpu_custom_call" | custom-call | flops 12884901888 | bytes 20971520 | tf_op jit(solution)/shard_map/experts/pallas_call | solution.py:284
  575.3 25.5 %experts.6 = (bf16[512,2048]{1,0:T(8,128)(2,1)}, bf16[512,2048]{1,0:T(8,128)(2,1)}, bf16[512,2176]{1,0:T(8,128)(2,1)}, bf16[512,2176]{1,0:T(8,128)(2,1)}, bf16[1...) custom-call(bf16[512,2176]{1,0:T(8,128)(2,1)} %bitcast.90.xa, bf16[512,2176]{1,0:T(8,128)(2,1)} %collective-permute-done.25.xb, ...), custom_call_target="tpu_custom_call" | custom-call | flops 12884901888 | bytes 20971520 | tf_op jit(solution)/shard_map/experts/pallas_call | solution.py:284
  601.4 25.4 %experts.5 = (bf16[512,2048]{1,0:T(8,128)(2,1)}, bf16[512,2048]{1,0:T(8,128)(2,1)}, bf16[512,2176]{1,0:T(8,128)(2,1)}, bf16[512,2176]{1,0:T(8,128)(2,1)}, bf16[1...) custom-call(bf16[512,2176]{1,0:T(8,128)(2,1)} %bitcast.77.xa, bf16[512,2176]{1,0:T(8,128)(2,1)} %collective-permute-done.19.xb, ...), custom_call_target="tpu_custom_call" | custom-call | flops 12884901888 | bytes 20971520 | tf_op jit(solution)/shard_map/experts/pallas_call | solution.py:284
  652.0 24.8 %fusion.13 = bf16[2048,1024]{1,0:T(8,128)(2,1)} fusion(bf16[4096,2048]{1,0:T(8,128)(2,1)} %slice_dynamic-update-slice_fusion, bf16[1024,1024]{1,0:T(8,128)(2,1)S(1)} %copy-done.82, bf16[1024,1024]{1,0:T(8,128)(2,1)} %get-tuple-element.57, bf16[1024,1024]{1,0:T(8,128)(2,1)} %get-tuple-element.56, bf16[1024,1024]{1,0:T(8,128)(2,1)S(1)} %copy-done.81), kind=kOutput, calls=%fused_computation.36 | convolution fusion | flops 17215520768 | bytes 29360128 | tf_op jit(solution)/shard_map/dot_general | solution.py:51
  680.6 11.6 collective-permute-done.41
  708.2 10.8 collective-permute-done.52
  719.4 10.8 collective-permute-done.46
  770.6 25.7 %collective-permute-done.56 = bf16[128,2176]{1,0:T(8,128)(2,1)S(1)} collective-permute-done((bf16[128,2176]{1,0:T(8,128)(2,1)S(1)}, bf16[128,2176]{1,0:T(8,128)(2,1)S(1)}, u32[]{:S(2)}, u32[]{:S(2)}) %collective-permute-start.56) | collective-permute-done | bytes 557088 | tf_op jit(solution)/shard_map/ppermute | solution.py:93
  796.3 10.5 collective-permute-done.50
  823.8 9.7 convolution_add_fusion
  853.3 37.5 %collective-permute-done.78 = bf16[256,1024]{1,0:T(8,128)(2,1)} collective-permute-done((bf16[256,1024]{1,0:T(8,128)(2,1)}, bf16[256,1024]{1,0:T(8,128)(2,1)}, u32[]{:S(2)}, u32[]{:S(2)}) %collective-permute-start.78) | collective-permute-done | bytes 524320 | tf_op jit(solution)/shard_map/ppermute | solution.py:215
  900.2 27.3 %collective-permute-done.81 = bf16[256,1024]{1,0:T(8,128)(2,1)S(1)} collective-permute-done((bf16[256,1024]{1,0:T(8,128)(2,1)}, bf16[256,1024]{1,0:T(8,128)(2,1)S(1)}, u32[]{:S(2)}, u32[]{:S(2)}) %collective-permute-start.81) | collective-permute-done | bytes 524320 | tf_op jit(solution)/shard_map/ppermute | solution.py:215
  928.3 26.8 %collective-permute-done.82 = bf16[256,1024]{1,0:T(8,128)(2,1)S(1)} collective-permute-done((bf16[256,1024]{1,0:T(8,128)(2,1)}, bf16[256,1024]{1,0:T(8,128)(2,1)S(1)}, u32[]{:S(2)}, u32[]{:S(2)}) %collective-permute-start.82) | collective-permute-done | bytes 524320 | tf_op jit(solution)/shard_map/ppermute | solution.py:215
  971.8 11.7 copy.374
  983.4 13.5 %attend_back.1 = (f32[1024,256]{1,0:T(8,128)}, f32[1024,256]{1,0:T(8,128)}, bf16[1024,256]{1,0:T(8,128)(2,1)}) custom-call(bf16[1024,256]{1,0:T(8,128)(2,1)} %copy.352.q, bf16[1024,256]{1,0:T(8,128)(2,1)} %copy.353.k, bf16[1024,256]{1,0:T(8,128)(2,1)} %copy.362.v, f32[1,1024]{1,0:T(1,128)} %bitcast.622, bf16[1024,256]{1,0:T(8,128)(2,1)} %bitcast.158.grad), custom_call_target="tpu_custom_call" | custom-call | flops 2684354560 | bytes 5242880 | tf_op jit(solution)/shard_map/attend_back/pallas_call | solution.py:377
  1013.2 9.1 fusion.12
  1023.6 29.8 %all-to-all-start.4 = ((f32[32,1,1160]{2,1,0:T(1,128)}), f32[32,1,1160]{2,1,0:T(1,128)S(1)}, u32[]{:S(2)}, u32[]{:S(2)}) async-start(f32[32,1,1160]{2,1,0:T(1,128)} %copy.339), calls=%async_computation.4 | async-start | bytes 327680 | tf_op jit(solution)/shard_map/all_to_all | solution.py:66
  1085.8 38.6 %collective-permute-done.76 = bf16[128,2048]{1,0:T(8,128)(2,1)S(1)} collective-permute-done((bf16[128,2048]{1,0:T(8,128)(2,1)}, bf16[128,2048]{1,0:T(8,128)(2,1)S(1)}, u32[]{:S(2)}, u32[]{:S(2)}) %collective-permute-start.76) | collective-permute-done | bytes 524320 | tf_op jit(solution)/shard_map/ppermute | solution.py:98
  1124.7 11.0 collective-permute-done.74
  1135.6 11.2 collective-permute-done.72
  1179.0 16.5 %collective-permute-done.75 = bf16[128,2048]{1,0:T(8,128)(2,1)} collective-permute-done((bf16[128,2048]{1,0:T(8,128)(2,1)}, bf16[128,2048]{1,0:T(8,128)(2,1)}, u32[]{:S(2)}, u32[]{:S(2)}) %collective-permute-start.75) | collective-permute-done | bytes 524320 | tf_op jit(solution)/shard_map/ppermute | solution.py:93
  1234.4 22.6 %collective-permute-done.68 = bf16[128,2048]{1,0:T(8,128)(2,1)} collective-permute-done((bf16[128,2048]{1,0:T(8,128)(2,1)}, bf16[128,2048]{1,0:T(8,128)(2,1)}, u32[]{:S(2)}, u32[]{:S(2)}) %collective-permute-start.68) | collective-permute-done | bytes 524320 | tf_op jit(solution)/shard_map/ppermute | solution.py:93
  1257.0 12.1 collective-permute-done.69
  (632 shorter events, 562.4 us)
Async XLA Ops:
  7.2 299.9 %all-gather.3.cloned.1.call-start = ((), (), s32[]{:S(2)}) async-start(), calls=%async_computation.8 | async-start | bytes 4718592 | tf_op jit(solution)/shard_map/all_gather | solution.py:70
  7.9 356.0 %all-gather.5.cloned.1.call-start = ((), (), s32[]{:S(2)}) async-start(), calls=%async_computation.9 | async-start | bytes 8650752 | tf_op jit(solution)/shard_map/all_gather | solution.py:70
  12.2 108.9 %collective-permute-start.33 = (bf16[128,2048]{1,0:T(8,128)(2,1)}, bf16[128,2048]{1,0:T(8,128)(2,1)}, u32[]{:S(2)}, u32[]{:S(2)}) collective-permute-start(bf16[128,2048]{1,0:T(8,128)(2,1)} %param.20), channel_id=1, source_target_pairs={{0,24},{4,28},{16,8},{20,12},{24,0},{28,4},{8,16},{12,20},{1,25},{... | collective-permute-start | bytes 1572872 | tf_op jit(solution)/shard_map/ppermute | solution.py:93
  15.8 126.8 %all-to-all-start = ((f32[32,1,1160]{2,1,0:T(1,128)}), f32[32,1,1160]{2,1,0:T(1,128)}, u32[]{:S(2)}, u32[]{:S(2)}) async-start(f32[32,1,1160]{2,1,0:T(1,128)} %broadcast_in_dim.23), calls=%async_computation | async-start | bytes 327680 | tf_op jit(solution)/shard_map/all_to_all | solution.py:66
  56.8 107.2 %collective-permute-start.2 = (bf16[256,1024]{1,0:T(8,128)(2,1)}, bf16[256,1024]{1,0:T(8,128)(2,1)}, u32[]{:S(2)}, u32[]{:S(2)}) collective-permute-start(bf16[256,1024]{1,0:T(8,128)(2,1)} %bitcast.611), channel_id=1, source_target_pairs={{0,4},{4,0},{16,20},{20,16},{24,28},{28,24},{8,12},{12,8},{1,5},{5... | collective-permute-start | bytes 1572872 | tf_op jit(solution)/shard_map/ppermute | solution.py:215
  58.0 107.8 %collective-permute-start.3 = (bf16[256,1024]{1,0:T(8,128)(2,1)}, bf16[256,1024]{1,0:T(8,128)(2,1)}, u32[]{:S(2)}, u32[]{:S(2)}) collective-permute-start(bf16[256,1024]{1,0:T(8,128)(2,1)} %bitcast.27), channel_id=1, source_target_pairs={{0,16},{4,20},{16,24},{20,28},{24,8},{28,12},{8,0},{12,4},{1,17},{... | collective-permute-start | bytes 1572872 | tf_op jit(solution)/shard_map/ppermute | solution.py:215
  66.4 130.1 %collective-permute-start.4 = (bf16[256,1024]{1,0:T(8,128)(2,1)}, bf16[256,1024]{1,0:T(8,128)(2,1)}, u32[]{:S(2)}, u32[]{:S(2)}) collective-permute-start(bf16[256,1024]{1,0:T(8,128)(2,1)} %bitcast.30), channel_id=1, source_target_pairs={{0,20},{4,16},{16,28},{20,24},{24,12},{28,8},{8,4},{12,0},{1,21},{... | collective-permute-start | bytes 1572872 | tf_op jit(solution)/shard_map/ppermute | solution.py:215
  152.2 132.6 %collective-permute-start.38 = (bf16[2,4,128,1024]{3,2,1,0:T(8,128)(2,1)}, bf16[2,4,128,1024]{3,2,1,0:T(8,128)(2,1)}, u32[]{:S(2)}, u32[]{:S(2)}) collective-permute-start(bf16[2,4,128,1024]{3,2,1,0:T(8,128)(2,1)} %pad_maximum_fusion.10), channel_id=1, source_target_pairs={{0,2},{1,3},{2,0},{3,1},{4,6},{5,7},{6,4},{7,5},{8,10},{9,11},{10,... | collective-permute-start | bytes 6291464 | tf_op jit(solution)/shard_map/ppermute | solution.py:98
  164.0 122.5 %collective-permute-start.37 = (bf16[2,4,128,1024]{3,2,1,0:T(8,128)(2,1)}, bf16[2,4,128,1024]{3,2,1,0:T(8,128)(2,1)}, u32[]{:S(2)}, u32[]{:S(2)}) collective-permute-start(bf16[2,4,128,1024]{3,2,1,0:T(8,128)(2,1)} %pad_maximum_fusion.9), channel_id=1, source_target_pairs={{0,4},{4,0},{8,12},{12,8},{16,20},{20,16},{24,28},{28,24},{1,5},{5... | collective-permute-start | bytes 6291464 | tf_op jit(solution)/shard_map/ppermute | solution.py:98
  165.9 70.1 %collective-permute-start.6 = (bf16[256,1024]{1,0:T(8,128)(2,1)}, bf16[256,1024]{1,0:T(8,128)(2,1)}, u32[]{:S(2)}, u32[]{:S(2)}) collective-permute-start(bf16[256,1024]{1,0:T(8,128)(2,1)} %bitcast.36), channel_id=1, source_target_pairs={{0,28},{4,24},{16,12},{20,8},{24,4},{28,0},{8,20},{12,16},{1,29},{... | collective-permute-start | bytes 1572872 | tf_op jit(solution)/shard_map/ppermute | solution.py:215
  196.5 64.8 %collective-permute-start.7 = (bf16[256,1024]{1,0:T(8,128)(2,1)}, bf16[256,1024]{1,0:T(8,128)(2,1)S(1)}, u32[]{:S(2)}, u32[]{:S(2)}) collective-permute-start(bf16[256,1024]{1,0:T(8,128)(2,1)} %bitcast.613), channel_id=1, source_target_pairs={{0,8},{4,12},{16,0},{20,4},{24,16},{28,20},{8,24},{12,28},{1,9},{5... | collective-permute-start | bytes 1572872 | tf_op jit(solution)/shard_map/ppermute | solution.py:215
  345.4 926.2 %reduce-scatter.2.cloned.1.call-start = ((), (), s32[]{:S(2)}) async-start(), calls=%async_computation.10 | async-start | bytes 8650752 | tf_op jit(solution)/shard_map/reduce_scatter | solution.py:74
  352.9 164.1 %collective-permute-start.39 = (bf16[4,4,128,2048]{3,2,1,0:T(8,128)(2,1)}, bf16[4,4,128,2048]{3,2,1,0:T(8,128)(2,1)}, u32[]{:S(2)}, u32[]{:S(2)}) collective-permute-start(bf16[4,4,128,2048]{3,2,1,0:T(8,128)(2,1)} %pad_maximum_fusion.ya), channel_id=1, source_target_pairs={{0,1},{1,0},{2,3},{3,2},{4,5},{5,4},{6,7},{7,6},{8,9},{9,8},{10,11... | collective-permute-start | bytes 25165832 | tf_op jit(solution)/shard_map/ppermute | solution.py:98
  385.8 62.6 %collective-permute-start.11 = (bf16[2,128,1152]{2,1,0:T(8,128)(2,1)S(1)}, bf16[2,128,1152]{2,1,0:T(8,128)(2,1)S(1)}, u32[]{:S(2)}, u32[]{:S(2)}) collective-permute-start(bf16[2,128,1152]{2,1,0:T(8,128)(2,1)S(1)} %pad_maximum_fusion.15), channel_id=1, source_target_pairs={{0,4},{4,0},{8,12},{12,8},{16,20},{20,16},{24,28},{28,24},{1,5},{5... | collective-permute-start | bytes 1769480 | tf_op jit(solution)/shard_map/ppermute | solution.py:98
  448.4 65.7 %collective-permute-start.29 = (bf16[2,128,1152]{2,1,0:T(8,128)(2,1)S(1)}, bf16[2,128,1152]{2,1,0:T(8,128)(2,1)S(1)}, u32[]{:S(2)}, u32[]{:S(2)}) collective-permute-start(bf16[2,128,1152]{2,1,0:T(8,128)(2,1)S(1)} %pad_maximum_fusion.18), channel_id=1, source_target_pairs={{0,4},{4,0},{8,12},{12,8},{16,20},{20,16},{24,28},{28,24},{1,5},{5... | collective-permute-start | bytes 1769480 | tf_op jit(solution)/shard_map/ppermute | solution.py:98
  508.9 92.5 %collective-permute-start.19 = (bf16[512,2176]{1,0:T(8,128)(2,1)}, bf16[512,2176]{1,0:T(8,128)(2,1)}, u32[]{:S(2)}, u32[]{:S(2)}) collective-permute-start(bf16[512,2176]{1,0:T(8,128)(2,1)} %bitcast.77.xa), channel_id=1, source_target_pairs={{0,1},{1,0},{2,3},{3,2},{4,5},{5,4},{6,7},{7,6},{8,9},{9,8},{10,11... | collective-permute-start | bytes 6684680 | tf_op jit(solution)/shard_map/ppermute | solution.py:98
  514.1 61.2 %collective-permute-start.25 = (bf16[512,2176]{1,0:T(8,128)(2,1)}, bf16[512,2176]{1,0:T(8,128)(2,1)}, u32[]{:S(2)}, u32[]{:S(2)}) collective-permute-start(bf16[512,2176]{1,0:T(8,128)(2,1)} %bitcast.90.xa), channel_id=1, source_target_pairs={{0,1},{1,0},{2,3},{3,2},{4,5},{5,4},{6,7},{7,6},{8,9},{9,8},{10,11... | collective-permute-start | bytes 6684680 | tf_op jit(solution)/shard_map/ppermute | solution.py:98
  542.8 134.0 %collective-permute-start.40 = (bf16[512,2176]{1,0:T(8,128)(2,1)}, bf16[512,2176]{1,0:T(8,128)(2,1)}, u32[]{:S(2)}, u32[]{:S(2)}) collective-permute-start(bf16[512,2176]{1,0:T(8,128)(2,1)} %get-tuple-element.64), channel_id=1, source_target_pairs={{0,1},{1,0},{2,3},{3,2},{4,5},{5,4},{6,7},{7,6},{8,9},{9,8},{10,11... | collective-permute-start | bytes 6684680 | tf_op jit(solution)/shard_map/ppermute | solution.py:98
  575.2 118.2 %collective-permute-start.57 = (bf16[512,2176]{1,0:T(8,128)(2,1)}, bf16[512,2176]{1,0:T(8,128)(2,1)}, u32[]{:S(2)}, u32[]{:S(2)}) collective-permute-start(bf16[512,2176]{1,0:T(8,128)(2,1)} %get-tuple-element.70), channel_id=1, source_target_pairs={{0,1},{1,0},{2,3},{3,2},{4,5},{5,4},{6,7},{7,6},{8,9},{9,8},{10,11... | collective-permute-start | bytes 6684680 | tf_op jit(solution)/shard_map/ppermute | solution.py:98
  600.8 95.3 %collective-permute-start.51 = (bf16[512,2176]{1,0:T(8,128)(2,1)}, bf16[512,2176]{1,0:T(8,128)(2,1)S(1)}, u32[]{:S(2)}, u32[]{:S(2)}) collective-permute-start(bf16[512,2176]{1,0:T(8,128)(2,1)} %get-tuple-element.68), channel_id=1, source_target_pairs={{0,1},{1,0},{2,3},{3,2},{4,5},{5,4},{6,7},{7,6},{8,9},{9,8},{10,11... | collective-permute-start | bytes 6684680 | tf_op jit(solution)/shard_map/ppermute | solution.py:98
  631.8 66.2 %collective-permute-start.45 = (bf16[512,2176]{1,0:T(8,128)(2,1)S(1)}, bf16[512,2176]{1,0:T(8,128)(2,1)S(1)}, u32[]{:S(2)}, u32[]{:S(2)}) collective-permute-start(bf16[512,2176]{1,0:T(8,128)(2,1)S(1)} %copy-done.79), channel_id=1, source_target_pairs={{0,1},{1,0},{2,3},{3,2},{4,5},{5,4},{6,7},{7,6},{8,9},{9,8},{10,11... | collective-permute-start | bytes 6684680 | tf_op jit(solution)/shard_map/ppermute | solution.py:98
  692.3 74.8 %collective-permute-start.42 = (bf16[128,1024]{1,0:T(8,128)(2,1)S(1)}, bf16[128,1024]{1,0:T(8,128)(2,1)S(1)}, u32[]{:S(2)}, u32[]{:S(2)}) collective-permute-start(bf16[128,1024]{1,0:T(8,128)(2,1)S(1)} %fusion.68), channel_id=1, source_target_pairs={{0,4},{4,0},{8,12},{12,8},{16,20},{20,16},{24,28},{28,24},{1,5},{5... | collective-permute-start | bytes 786440 | tf_op jit(solution)/shard_map/ppermute | solution.py:98
  807.1 246.3 %collective-permute-start.63 = (bf16[4,4,128,2048]{3,2,1,0:T(8,128)(2,1)}, bf16[4,4,128,2048]{3,2,1,0:T(8,128)(2,1)}, u32[]{:S(2)}, u32[]{:S(2)}) collective-permute-start(bf16[4,4,128,2048]{3,2,1,0:T(8,128)(2,1)} %pad_maximum_fusion.1), channel_id=1, source_target_pairs={{0,1},{1,0},{2,3},{3,2},{4,5},{5,4},{6,7},{7,6},{8,9},{9,8},{10,11... | collective-permute-start | bytes 25165832 | tf_op jit(solution)/shard_map/ppermute | solution.py:98
  835.5 62.8 %collective-permute-start.80 = (bf16[256,1024]{1,0:T(8,128)(2,1)}, bf16[256,1024]{1,0:T(8,128)(2,1)}, u32[]{:S(2)}, u32[]{:S(2)}) collective-permute-start(bf16[256,1024]{1,0:T(8,128)(2,1)} %get-tuple-element.196), channel_id=1, source_target_pairs={{0,20},{4,16},{16,28},{20,24},{24,12},{28,8},{8,4},{12,0},{1,21},{... | collective-permute-start | bytes 1572872 | tf_op jit(solution)/shard_map/ppermute | solution.py:215
  843.6 139.8 %all-to-all-start.3 = ((bf16[8,128,256]{2,1,0:T(8,128)(2,1)}), bf16[8,128,256]{2,1,0:T(8,128)(2,1)}, u32[]{:S(2)}, u32[]{:S(2)}) async-start(bf16[8,128,256]{2,1,0:T(8,128)(2,1)} %bitcast.577), calls=%async_computation.3 | async-start | bytes 1048576 | tf_op jit(solution)/shard_map/all_to_all | solution.py:66
  851.2 105.5 %collective-permute-start.84 = (bf16[256,1024]{1,0:T(8,128)(2,1)}, bf16[256,1024]{1,0:T(8,128)(2,1)S(1)}, u32[]{:S(2)}, u32[]{:S(2)}) collective-permute-start(bf16[256,1024]{1,0:T(8,128)(2,1)} %get-tuple-element.192), channel_id=1, source_target_pairs={{0,12},{4,8},{16,4},{20,0},{24,20},{28,16},{8,28},{12,24},{1,13},{... | collective-permute-start | bytes 1572872 | tf_op jit(solution)/shard_map/ppermute | solution.py:215
  892.8 62.3 %collective-permute-start.82 = (bf16[256,1024]{1,0:T(8,128)(2,1)}, bf16[256,1024]{1,0:T(8,128)(2,1)S(1)}, u32[]{:S(2)}, u32[]{:S(2)}) collective-permute-start(bf16[256,1024]{1,0:T(8,128)(2,1)} %get-tuple-element.194), channel_id=1, source_target_pairs={{0,28},{4,24},{16,12},{20,8},{24,4},{28,0},{8,20},{12,16},{1,29},{... | collective-permute-start | bytes 1572872 | tf_op jit(solution)/shard_map/ppermute | solution.py:215
  1066.0 86.3 %collective-permute-start.66 = (bf16[2,4,128,1024]{3,2,1,0:T(8,128)(2,1)}, bf16[2,4,128,1024]{3,2,1,0:T(8,128)(2,1)}, u32[]{:S(2)}, u32[]{:S(2)}) collective-permute-start(bf16[2,4,128,1024]{3,2,1,0:T(8,128)(2,1)} %pad_maximum_fusion.12), channel_id=1, source_target_pairs={{0,4},{4,0},{8,12},{12,8},{16,20},{20,16},{24,28},{28,24},{1,5},{5... | collective-permute-start | bytes 6291464 | tf_op jit(solution)/shard_map/ppermute | solution.py:98
  1067.9 87.6 %collective-permute-start.64 = (bf16[2,4,128,1024]{3,2,1,0:T(8,128)(2,1)}, bf16[2,4,128,1024]{3,2,1,0:T(8,128)(2,1)}, u32[]{:S(2)}, u32[]{:S(2)}) collective-permute-start(bf16[2,4,128,1024]{3,2,1,0:T(8,128)(2,1)} %pad_maximum_fusion.11), channel_id=1, source_target_pairs={{0,2},{1,3},{2,0},{3,1},{4,6},{5,7},{6,4},{7,5},{8,10},{9,11},{10,... | collective-permute-start | bytes 6291464 | tf_op jit(solution)/shard_map/ppermute | solution.py:98
  1071.9 63.7 %collective-permute-start.74 = (bf16[128,2048]{1,0:T(8,128)(2,1)}, bf16[128,2048]{1,0:T(8,128)(2,1)}, u32[]{:S(2)}, u32[]{:S(2)}) collective-permute-start(bf16[128,2048]{1,0:T(8,128)(2,1)} %get-tuple-element.202), channel_id=1, source_target_pairs={{0,4},{4,0},{8,12},{12,8},{16,20},{20,16},{24,28},{28,24},{1,5},{5... | collective-permute-start | bytes 1572872 | tf_op jit(solution)/shard_map/ppermute | solution.py:98
  1072.2 74.6 %collective-permute-start.72 = (bf16[128,2048]{1,0:T(8,128)(2,1)}, bf16[128,2048]{1,0:T(8,128)(2,1)}, u32[]{:S(2)}, u32[]{:S(2)}) collective-permute-start(bf16[128,2048]{1,0:T(8,128)(2,1)} %get-tuple-element.203), channel_id=1, source_target_pairs={{0,4},{4,0},{8,12},{12,8},{16,20},{20,16},{24,28},{28,24},{1,5},{5... | collective-permute-start | bytes 1572872 | tf_op jit(solution)/shard_map/ppermute | solution.py:98
  1079.6 118.0 %all-to-all-start.5 = ((bf16[4,8,64,768]{3,2,1,0:T(8,128)(2,1)}), bf16[4,8,64,768]{3,2,1,0:T(8,128)(2,1)}, u32[]{:S(2)}, u32[]{:S(2)}) async-start(bf16[4,8,64,768]{3,2,1,0:T(8,128)(2,1)} %bitcast.532), calls=%async_computation.5 | async-start | bytes 6291456 | tf_op jit(solution)/shard_map/all_to_all | solution.py:66
  (148 other events, 3812.8 us)
Sparse Core Ops, SparseCore 0:
  10.1 125.0 all-gather.2
  138.0 136.8 all-gather.4
  815.9 177.9 reduce-scatter.1

commit v5 on v4

--- a/solution.py
+++ b/solution.py
@@ -121,8 +121,12 @@
 def ring_blocks(vals):
     blocks = [vals]
     for step in range(1, lax.axis_size("dp") // 2):
-        blocks.append(ring_shift(vals, step))
+        blocks.append(ring_shift(after(vals, blocks[1]) if step == 2 else vals, step))
     return blocks
+
+
+def after(vals, *others):
+    return lax.optimization_barrier((vals,) + others)[0]
 
 
 def pick_rows(vals, index):
@@ -205,7 +209,7 @@
     return [(src, dst ^ (index % 2)) for src, dst in pairs]
 
 
-def walk_swap(blocks, tables):
+def walk_swap(blocks, tables, wait_for=None):
     n_dp = blocks.shape[0]
     _, target, step_of = tables
     moved = []
@@ -214,6 +218,8 @@
         if index:
             block = lax.ppermute(block, "dp", walk_perm(n_dp, index))
         moved.append(block)
+    if wait_for is not None:
+        moved = [after(block, wait_for) for block in moved]
     return pick_rows(jnp.stack(moved), step_of)
 
 
@@ -429,9 +435,16 @@
     wrows = w_query.shape[0]
     score_scale = 1.0 / math.sqrt(HD)
 
+    seq_tokens = gather(tokens, "dp")
+    member = lax.axis_index("dp")
+    tables = walk_tables(n_dp)
+    member_of_walk = tables[0]
+    qkv = jnp.stack([w_query, w_key, w_value]).astype(BF).reshape(3, wrows, n_dp, cols)
+    qkv = swap(qkv.transpose(2, 1, 0, 3), "dp")
     gains = jnp.concatenate(
         [attn_gain, moe_gain, query_gain, key_gain, w_router.T.reshape(-1)]
     )
+    gains = after(gains, qkv)
     gains_all = swap(jnp.broadcast_to(gains, (n_all, gains.shape[0])), BOTH)
     gw, hw = attn_gain.shape[0], query_gain.shape[0]
     gain_one = gains_all[:, :gw].reshape(-1)
@@ -441,12 +454,6 @@
     wr_all = gains_all[:, 2 * gw + 2 * hw :].reshape(n_all, expert_total, wrows)
     wr_all = wr_all.transpose(1, 0, 2).reshape(expert_total, width).astype(BF)
 
-    seq_tokens = gather(tokens, "dp")
-    member = lax.axis_index("dp")
-    tables = walk_tables(n_dp)
-    member_of_walk = tables[0]
-    qkv = jnp.stack([w_query, w_key, w_value]).astype(BF).reshape(3, wrows, n_dp, cols)
-    qkv = swap(qkv.transpose(2, 1, 0, 3), "dp")
     qkv = qkv.reshape(1, n_dp, wrows, 3 * cols)
     bit = 1
     while bit < n_ex:
@@ -457,7 +464,8 @@
     wo_all = gather(w_output.astype(BF), BOTH)
     w1 = jnp.stack([w_gate, w_up]).astype(BF).reshape(2, local_count, cols, n_dp, ff_part)
     w1 = w1.transpose(3, 2, 0, 1, 4).reshape(n_dp, cols, -1)
-    dy_ring = jnp.stack(ring_blocks(cotangent))
+    w1 = after(w1, gains_all)
+    dy_ring = jnp.stack(ring_blocks(after(cotangent, gains_all)))
     w1 = walk_swap(w1, tables)
     w1 = w1.reshape(width, -1)
     w2 = w_down.astype(BF).reshape(local_count * ff_part, width)
@@ -540,7 +548,7 @@
     if not lean:
         mix_near = jnp.stack([m[0].reshape(-1, rows, width) for m in mix_parts], axis=1)
         mix_far = jnp.stack([m[1].reshape(-1, rows, width) for m in mix_parts], axis=1)
-        mix_far, returned = lax.optimization_barrier((mix_far, returned))
+        mix_far = after(mix_far, returned)
         mix_near = add(mix_near, core_flip(mix_far))
         mix_parts = list(reduce_peers(mix_near))
         by_chunk = jnp.stack([g.reshape(2, -1, rows, half) for g in gated_inners], axis=2)
@@ -552,19 +560,12 @@
         pre_all = jnp.concatenate(pre_grads, axis=0)
         w1_grad = dot_rows(n2_all, pre_all)
     w1_grad = w1_grad.astype(BF)
-    w1_grad, returned = lax.optimization_barrier((w1_grad, returned))
+    w1_grad = after(w1_grad, returned)
     token_grads = returned[:, :width]
     gg = returned[:, width : width + expert_total * n_dp].reshape(rows, expert_total, n_dp)
     gg = jnp.sum(gg, axis=-1)
     mixed = home(mix_parts)
     down_grad = down_grad.reshape(local_count, ff_part, width)
-    w1_grad = walk_swap(w1_grad.reshape(n_dp, cols, -1), tables)
-    w1_grad = (
-        w1_grad.reshape(n_dp, cols, 2, local_count, ff_part)
-        .transpose(2, 3, 1, 0, 4)
-        .reshape(2, local_count, cols, ff)
-        .astype(F32)
-    )
     weighted = gates * gg
     logit_bf = (weighted - gates * jnp.sum(weighted, axis=-1, keepdims=True)).astype(BF)
     router_grad = dot_rows(normed_two, logit_bf)
@@ -581,8 +582,7 @@
     query_grad, key_grad, value_grad = attend_back(
         query_bf, key_bf, value_bf, bias, attended_grad, score_scale
     )
-    hidden_late, query_grad = lax.optimization_barrier((hidden_one, query_grad))
-    block_out = (hidden_late + mixed).astype(BF)
+    block_out = (after(hidden_one, query_grad) + mixed).astype(BF)
     query_grad = query_grad.reshape(-1, cols // HD, HD)
     key_grad = key_grad.reshape(-1, cols // HD, HD)
     query_flat_grad, query_gain_grad = query_back(query_grad)
@@ -602,6 +602,13 @@
     for step in range(n_dp // 2):
         sums.append(add(part_bf[step, 0], flip(part_bf[step, 1], "dp", 1)))
     normed_one_grad = home(sums)
+    w1_grad = walk_swap(w1_grad.reshape(n_dp, cols, -1), tables, sums[-1])
+
+    def unpack(blocks):
+        blocks = blocks.reshape(n_dp, cols, local_count, ff_part).transpose(2, 1, 0, 3)
+        return blocks.reshape(local_count, cols, ff).astype(F32)
+
+    gate_w_grad, up_w_grad = unpack(w1_grad[:, :, :half]), unpack(w1_grad[:, :, half:])
     _, norm_one_back = jax.vjp(lambda v: rms_scale(v, gain_one), inputs)
     (input_part,) = norm_one_back(normed_one_grad)
     grad_tokens = (hidden_grad + input_part).astype(BF)
@@ -634,8 +641,8 @@
         small[2 * gw + hw : 2 * gw + 2 * hw],
         small[gw : 2 * gw],
         small[2 * gw + 2 * hw :].reshape(wrows, expert_total),
-        w1_grad[0],
-        w1_grad[1],
+        gate_w_grad,
+        up_w_grad,
         down_grad,
     )
 

time: 1290 us -> 1190 us (0.922)
  waiting for transfers between devices: 557 us -> 471 us
  starting transfers between devices: 157 us -> 116 us
    ppermute x14, waiting for transfers between devices: 153 us -> 78.4 us  [walk_swap(): block = lax.ppermute(block, 'dp', walk_perm(n_dp, index))]
    ppermute x15, waiting for transfers between devices: 177 us -> 133 us  [ring_shift(): return lax.ppermute(vals, 'dp', ring_perm(lax.axis_size('dp'), steps))]
    all_to_all x7, waiting for transfers between devices: 28.1 us -> 56 us  [swap(): return lax.all_to_all(blocks, axes, split_axis=0, concat_axis=0, tiled=True)]
    all_to_all x7, starting transfers between devices: 65.9 us -> 41.3 us  [swap(): return lax.all_to_all(blocks, axes, split_axis=0, concat_axis=0, tiled=True)]
    unnamed x202 -> x210, local copies, waits for them, and re-layouts: 64.5 us -> 76.1 us
  transfers between devices with their start and end apart: 95 -> 95, of which waited for: 40 -> 41; matrix products, arithmetic and copies ran while one was open for 31% -> 36% of each run, Pallas kernels for 10% -> 11%
where the time goes in v5:
time: 1190 us; the launch traced here: 1170 us
  waiting for transfers between devices  471 us (40%)
  local copies, waits for them, and re-layouts  228 us (19%)
  Pallas kernels  124 us (10%)
  starting transfers between devices  116 us (10%)
  other arithmetic  116 us (10%)
  matrix products  87.3 us (7%)
  between operations  31.7 us (3%)
    ppermute x56, waiting for transfers between devices, flip(): return lax.ppermute(vals, axis, [(i, i ^ bit) for i in range(size)])  203 us
    ppermute x15, waiting for transfers between devices, ring_shift(): return lax.ppermute(vals, 'dp', ring_perm(lax.axis_size('dp'), steps))  133 us
    pallas_call x4, Pallas kernels, experts(): pl.pallas_call(body, grid=(2 * halves,), in_specs=[pl.BlockSpec((tile, wi...  102 us
    ppermute x14, waiting for transfers between devices, walk_swap(): block = lax.ppermute(block, 'dp', walk_perm(n_dp, index))  78.4 us
    unnamed x210, local copies, waits for them, and re-layouts  76.1 us
    dot_general x6, matrix products, dot_rows(): lax.dot_general(left_mat, right_mat, (((0,), (0,)), ((), ())), preferred_...  60.3 us
    all_to_all x7, waiting for transfers between devices, swap(): return lax.all_to_all(blocks, axes, split_axis=0, concat_axis=0, tiled=True)  56 us
    ppermute x56, starting transfers between devices, flip(): return lax.ppermute(vals, axis, [(i, i ^ bit) for i in range(size)])  47 us
  transfers between devices with their start and end apart: 95, of which 41 were waited for; matrix products, arithmetic and copies ran while one was open for 36% of the time, Pallas kernels for 11%

profile of v5, /device:TPU:13, one launch (start us, length us, event | category | flops | bytes accessed | tf_op | source)
XLA Modules:
  0.0 1174.7 jit_solution(4267532608532172740)
XLA Ops:
  39.3 12.9 %all-to-all-done = bf16[8,64,3,256]{3,1,2,0:T(8,128)(2,1)S(1)} async-done(((bf16[8,64,3,256]{3,1,2,0:T(8,128)(2,1)}), bf16[8,64,3,256]{3,1,2,0:T(8,128)(2,1)S(1)}, u32[]{:S(2)}, u32[]{:S(2)}) %all-to-all-start) | async-done | bytes 786464 | tf_op jit(solution)/shard_map/all_to_all | solution.py:66
  60.7 10.1 all-to-all-done.1
  75.3 37.0 %collective-permute-done.14 = bf16[128,2048]{1,0:T(8,128)(2,1)S(1)} collective-permute-done((bf16[128,2048]{1,0:T(8,128)(2,1)}, bf16[128,2048]{1,0:T(8,128)(2,1)S(1)}, u32[]{:S(2)}, u32[]{:S(2)}) %collective-permute-start.14) | collective-permute-done | bytes 524320 | tf_op jit(solution)/shard_map/ppermute | solution.py:93
  121.1 23.1 %collective-permute-done.15 = bf16[128,2048]{1,0:T(8,128)(2,1)} collective-permute-done((bf16[128,2048]{1,0:T(8,128)(2,1)}, bf16[128,2048]{1,0:T(8,128)(2,1)}, u32[]{:S(2)}, u32[]{:S(2)}) %collective-permute-start.15) | collective-permute-done | bytes 524320 | tf_op jit(solution)/shard_map/ppermute | solution.py:93
  212.1 26.8 %collective-permute-done.2 = bf16[256,1024]{1,0:T(8,128)(2,1)} collective-permute-done((bf16[256,1024]{1,0:T(8,128)(2,1)}, bf16[256,1024]{1,0:T(8,128)(2,1)}, u32[]{:S(2)}, u32[]{:S(2)}) %collective-permute-start.2) | collective-permute-done | bytes 524320 | tf_op jit(solution)/shard_map/ppermute | solution.py:219
  244.6 24.5 %collective-permute-done.5 = bf16[256,1024]{1,0:T(8,128)(2,1)S(1)} collective-permute-done((bf16[256,1024]{1,0:T(8,128)(2,1)S(1)}, bf16[256,1024]{1,0:T(8,128)(2,1)S(1)}, u32[]{:S(2)}, u32[]{:S(2)}) %collective-permute-start.5) | collective-permute-done | bytes 524320 | tf_op jit(solution)/shard_map/ppermute | solution.py:219
  270.9 9.2 collective-permute-done.6
  290.2 10.4 collective-permute-done.8
  409.6 12.2 %collective-permute-done.51 = bf16[128,2176]{1,0:T(8,128)(2,1)S(1)} collective-permute-done((bf16[128,2176]{1,0:T(8,128)(2,1)}, bf16[128,2176]{1,0:T(8,128)(2,1)S(1)}, u32[]{:S(2)}, u32[]{:S(2)}) %collective-permute-start.51) | collective-permute-done | bytes 557088 | tf_op jit(solution)/shard_map/ppermute | solution.py:93
  455.2 9.2 collective-permute-done.31
  464.5 9.2 collective-permute-done.40
  495.4 25.8 %experts.4 = (bf16[512,2048]{1,0:T(8,128)(2,1)}, bf16[512,2048]{1,0:T(8,128)(2,1)}, bf16[512,2176]{1,0:T(8,128)(2,1)}, bf16[512,2176]{1,0:T(8,128)(2,1)}, bf16[1...) custom-call(bf16[512,2176]{1,0:T(8,128)(2,1)} %bitcast.544, bf16[512,2176]{1,0:T(8,128)(2,1)} %collective-permute-done.13.xb, ...), custom_call_target="tpu_custom_call" | custom-call | flops 12884901888 | bytes 20971520 | tf_op jit(solution)/shard_map/experts/pallas_call | solution.py:290
  527.7 25.4 %experts.7 = (bf16[512,2048]{1,0:T(8,128)(2,1)}, bf16[512,2048]{1,0:T(8,128)(2,1)}, bf16[512,2176]{1,0:T(8,128)(2,1)}, bf16[512,2176]{1,0:T(8,128)(2,1)}, bf16[1...) custom-call(bf16[512,2176]{1,0:T(8,128)(2,1)} %bitcast.143.xa, bf16[512,2176]{1,0:T(8,128)(2,1)} %collective-permute-done.56.xb, ...), custom_call_target="tpu_custom_call" | custom-call | flops 12884901888 | bytes 20971520 | tf_op jit(solution)/shard_map/experts/pallas_call | solution.py:290
  553.6 25.6 %experts.5 = (bf16[512,2048]{1,0:T(8,128)(2,1)}, bf16[512,2048]{1,0:T(8,128)(2,1)}, bf16[512,2176]{1,0:T(8,128)(2,1)}, bf16[512,2176]{1,0:T(8,128)(2,1)}, bf16[1...) custom-call(bf16[512,2176]{1,0:T(8,128)(2,1)} %bitcast.101.xa, bf16[512,2176]{1,0:T(8,128)(2,1)} %collective-permute-done.32.xb, ...), custom_call_target="tpu_custom_call" | custom-call | flops 12884901888 | bytes 20971520 | tf_op jit(solution)/shard_map/experts/pallas_call | solution.py:290
  585.7 25.5 %experts.6 = (bf16[512,2048]{1,0:T(8,128)(2,1)}, bf16[512,2048]{1,0:T(8,128)(2,1)}, bf16[512,2176]{1,0:T(8,128)(2,1)}, bf16[512,2176]{1,0:T(8,128)(2,1)}, bf16[1...) custom-call(bf16[512,2176]{1,0:T(8,128)(2,1)} %bitcast.122.xa, bf16[512,2176]{1,0:T(8,128)(2,1)} %collective-permute-done.44.xb, ...), custom_call_target="tpu_custom_call" | custom-call | flops 12884901888 | bytes 20971520 | tf_op jit(solution)/shard_map/experts/pallas_call | solution.py:290
  631.3 23.4 %fusion.13 = bf16[2048,1024]{1,0:T(8,128)(2,1)} fusion(bf16[4096,2048]{1,0:T(8,128)(2,1)} %slice_dynamic-update-slice_fusion, bf16[1024,1024]{1,0:T(8,128)(2,1)S(1)} %copy-done.85, bf16[1024,1024]{1,0:T(8,128)(2,1)S(1)} %copy-done.87, bf16[1024,1024]{1,0:T(8,128)(2,1)S(1)} %copy-done.86, bf16[1024,1024]{1,0:T(8,128)(2,1)S(1)} %copy-done.84), kind=kOutput, calls=%fused_computation.35 | convolution fusion | flops 17215520768 | bytes 29360128 | tf_op jit(solution)/shard_map/dot_general | solution.py:51
  657.7 12.7 %collective-permute-done.23 = bf16[2,128,1024]{2,1,0:T(8,128)(2,1)S(1)} collective-permute-done((bf16[2,128,1024]{2,1,0:T(8,128)(2,1)S(1)}, bf16[2,128,1024]{2,1,0:T(8,128)(2,1)S(1)}, u32[]{:S(2)}, u32[]{:S(2)}) %collective-permute-start.23) | collective-permute-done | bytes 524320 | tf_op jit(solution)/shard_map/ppermute | solution.py:98
  677.0 9.6 collective-permute-done.58
  686.8 11.1 collective-permute-done.34
  714.8 18.2 %collective-permute-done.37 = bf16[128,1152]{1,0:T(8,128)(2,1)S(1)} collective-permute-done((bf16[128,1152]{1,0:T(8,128)(2,1)S(1)}, bf16[128,1152]{1,0:T(8,128)(2,1)S(1)}, u32[]{:S(2)}, u32[]{:S(2)}) %collective-permute-start.37) | collective-permute-done | bytes 294944 | tf_op jit(solution)/shard_map/ppermute | solution.py:98
  746.6 11.8 %collective-permute-done.38 = bf16[128,2176]{1,0:T(8,128)(2,1)S(1)} collective-permute-done((bf16[128,2176]{1,0:T(8,128)(2,1)S(1)}, bf16[128,2176]{1,0:T(8,128)(2,1)S(1)}, u32[]{:S(2)}, u32[]{:S(2)}) %collective-permute-start.38) | collective-permute-done | bytes 557088 | tf_op jit(solution)/shard_map/ppermute | solution.py:93
  758.4 26.0 %collective-permute-done.50 = bf16[128,2176]{1,0:T(8,128)(2,1)S(1)} collective-permute-done((bf16[128,2176]{1,0:T(8,128)(2,1)S(1)}, bf16[128,2176]{1,0:T(8,128)(2,1)S(1)}, u32[]{:S(2)}, u32[]{:S(2)}) %collective-permute-start.50) | collective-permute-done | bytes 557088 | tf_op jit(solution)/shard_map/ppermute | solution.py:93
  795.4 10.6 fusion.121
  817.0 12.0 %convolution_add_fusion = f32[512,2048]{1,0:T(8,128)} fusion(f32[512,2048]{1,0:T(8,128)} %fusion.121, bf16[2048,512]{1,0:T(8,128)(2,1)} %bitcast.541, bf16[2048,2048]{1,0:T(8,128)(2,1)} %bitcast.236), kind=kOutput, calls=%fused_computation.39 | convolution fusion | flops 4296015872 | bytes 18874368 | tf_op jit(solution)/shard_map/dot_general | solution.py:51
  841.2 13.1 %attend_back.1 = (f32[1024,256]{1,0:T(8,128)}, f32[1024,256]{1,0:T(8,128)}, bf16[1024,256]{1,0:T(8,128)(2,1)}) custom-call(bf16[1024,256]{1,0:T(8,128)(2,1)} %copy.375.q, bf16[1024,256]{1,0:T(8,128)(2,1)} %copy.376.k, bf16[1024,256]{1,0:T(8,128)(2,1)} %copy.384.v, f32[1,1024]{1,0:T(1,128)} %bitcast.632, bf16[1024,256]{1,0:T(8,128)(2,1)} %bitcast.624), custom_call_target="tpu_custom_call" | custom-call | flops 2684354560 | bytes 5242880 | tf_op jit(solution)/shard_map/attend_back/pallas_call | solution.py:383
  870.5 9.2 fusion.12
  899.0 9.0 all-to-all-done.4
  934.5 41.8 %collective-permute-done.76 = bf16[128,2048]{1,0:T(8,128)(2,1)S(1)} collective-permute-done((bf16[128,2048]{1,0:T(8,128)(2,1)}, bf16[128,2048]{1,0:T(8,128)(2,1)S(1)}, u32[]{:S(2)}, u32[]{:S(2)}) %collective-permute-start.76) | collective-permute-done | bytes 524320 | tf_op jit(solution)/shard_map/ppermute | solution.py:98
  1004.1 21.3 %collective-permute-done.64 = bf16[2,4,128,1024]{3,2,1,0:T(8,128)(2,1)S(1)} collective-permute-done((bf16[2,4,128,1024]{3,2,1,0:T(8,128)(2,1)S(1)}, bf16[2,4,128,1024]{3,2,1,0:T(8,128)(2,1)S(1)}, u32[]{:S(2)}, u32[]{:S(2)}) %collective-permute-start.64) | collective-permute-done | bytes 2097184 | tf_op jit(solution)/shard_map/ppermute | solution.py:98
  1035.6 9.4 collective-permute-done.71
  1116.1 24.0 %all-to-all-done.6 = bf16[8,64,768]{2,1,0:T(8,128)(2,1)} async-done(((bf16[8,64,768]{2,1,0:T(8,128)(2,1)}), bf16[8,64,768]{2,1,0:T(8,128)(2,1)}, u32[]{:S(2)}, u32[]{:S(2)}) %all-to-all-start.6) | async-done | bytes 786464 | tf_op jit(solution)/shard_map/all_to_all | solution.py:66
  1153.1 10.3 collective-permute-done.68
  (640 shorter events, 582.7 us)
Async XLA Ops:
  7.2 323.6 %all-gather.3.cloned.1.call-start = ((), (), s32[]{:S(2)}) async-start(), calls=%async_computation.8 | async-start | bytes 4718592 | tf_op jit(solution)/shard_map/all_gather | solution.py:70
  7.9 379.8 %all-gather.5.cloned.1.call-start = ((), (), s32[]{:S(2)}) async-start(), calls=%async_computation.9 | async-start | bytes 8650752 | tf_op jit(solution)/shard_map/all_gather | solution.py:70
  116.4 72.2 %collective-permute-start = (bf16[1,8,64,768]{3,2,1,0:T(8,128)(2,1)S(1)}, bf16[1,8,64,768]{3,2,1,0:T(8,128)(2,1)}, u32[]{:S(2)}, u32[]{:S(2)}) collective-permute-start(bf16[1,8,64,768]{3,2,1,0:T(8,128)(2,1)S(1)} %reshape.783), channel_id=1, source_target_pairs={{0,1},{1,0},{2,3},{3,2},{4,5},{5,4},{6,7},{7,6},{8,9},{9,8},{10,11... | collective-permute-start | bytes 2359304 | tf_op jit(solution)/shard_map/ppermute | solution.py:98
  183.2 55.8 %collective-permute-start.2 = (bf16[256,1024]{1,0:T(8,128)(2,1)}, bf16[256,1024]{1,0:T(8,128)(2,1)}, u32[]{:S(2)}, u32[]{:S(2)}) collective-permute-start(bf16[256,1024]{1,0:T(8,128)(2,1)} %bitcast.622), channel_id=1, source_target_pairs={{0,4},{4,0},{16,20},{20,16},{24,28},{28,24},{8,12},{12,8},{1,5},{5... | collective-permute-start | bytes 1572872 | tf_op jit(solution)/shard_map/ppermute | solution.py:219
  201.5 67.6 %collective-permute-start.5 = (bf16[256,1024]{1,0:T(8,128)(2,1)S(1)}, bf16[256,1024]{1,0:T(8,128)(2,1)S(1)}, u32[]{:S(2)}, u32[]{:S(2)}) collective-permute-start(bf16[256,1024]{1,0:T(8,128)(2,1)S(1)} %bitcast.623), channel_id=1, source_target_pairs={{0,24},{4,28},{16,8},{20,12},{24,0},{28,4},{8,16},{12,20},{1,25},{... | collective-permute-start | bytes 1572872 | tf_op jit(solution)/shard_map/ppermute | solution.py:219
  210.6 110.8 %collective-permute-start.19 = (bf16[2,4,128,1024]{3,2,1,0:T(8,128)(2,1)}, bf16[2,4,128,1024]{3,2,1,0:T(8,128)(2,1)}, u32[]{:S(2)}, u32[]{:S(2)}) collective-permute-start(bf16[2,4,128,1024]{3,2,1,0:T(8,128)(2,1)} %pad_maximum_fusion.9), channel_id=1, source_target_pairs={{0,4},{4,0},{8,12},{12,8},{16,20},{20,16},{24,28},{28,24},{1,5},{5... | collective-permute-start | bytes 6291464 | tf_op jit(solution)/shard_map/ppermute | solution.py:98
  239.4 73.6 %collective-permute-start.1 = (bf16[2,8,64,768]{3,2,1,0:T(8,128)(2,1)}, bf16[2,8,64,768]{3,2,1,0:T(8,128)(2,1)}, u32[]{:S(2)}, u32[]{:S(2)}) collective-permute-start(bf16[2,8,64,768]{3,2,1,0:T(8,128)(2,1)} %pad_maximum_fusion.13), channel_id=1, source_target_pairs={{0,2},{1,3},{2,0},{3,1},{4,6},{5,7},{6,4},{7,5},{8,10},{9,11},{10,... | collective-permute-start | bytes 4718600 | tf_op jit(solution)/shard_map/ppermute | solution.py:98
  239.4 83.7 %collective-permute-start.20 = (bf16[2,4,128,1024]{3,2,1,0:T(8,128)(2,1)}, bf16[2,4,128,1024]{3,2,1,0:T(8,128)(2,1)}, u32[]{:S(2)}, u32[]{:S(2)}) collective-permute-start(bf16[2,4,128,1024]{3,2,1,0:T(8,128)(2,1)} %pad_maximum_fusion.10), channel_id=1, source_target_pairs={{0,2},{1,3},{2,0},{3,1},{4,6},{5,7},{6,4},{7,5},{8,10},{9,11},{10,... | collective-permute-start | bytes 6291464 | tf_op jit(solution)/shard_map/ppermute | solution.py:98
  370.6 795.3 %reduce-scatter.2.cloned.1.call-start = ((), (), s32[]{:S(2)}) async-start(), calls=%async_computation.10 | async-start | bytes 8650752 | tf_op jit(solution)/shard_map/reduce_scatter | solution.py:74
  378.1 117.3 %collective-permute-start.21 = (bf16[4,4,128,2048]{3,2,1,0:T(8,128)(2,1)}, bf16[4,4,128,2048]{3,2,1,0:T(8,128)(2,1)}, u32[]{:S(2)}, u32[]{:S(2)}) collective-permute-start(bf16[4,4,128,2048]{3,2,1,0:T(8,128)(2,1)} %pad_maximum_fusion.ya), channel_id=1, source_target_pairs={{0,1},{1,0},{2,3},{3,2},{4,5},{5,4},{6,7},{7,6},{8,9},{9,8},{10,11... | collective-permute-start | bytes 25165832 | tf_op jit(solution)/shard_map/ppermute | solution.py:98
  490.0 63.7 %collective-permute-start.32 = (bf16[512,2176]{1,0:T(8,128)(2,1)}, bf16[512,2176]{1,0:T(8,128)(2,1)}, u32[]{:S(2)}, u32[]{:S(2)}) collective-permute-start(bf16[512,2176]{1,0:T(8,128)(2,1)} %bitcast.101.xa), channel_id=1, source_target_pairs={{0,1},{1,0},{2,3},{3,2},{4,5},{5,4},{6,7},{7,6},{8,9},{9,8},{10,11... | collective-permute-start | bytes 6684680 | tf_op jit(solution)/shard_map/ppermute | solution.py:98
  494.2 91.5 %collective-permute-start.44 = (bf16[512,2176]{1,0:T(8,128)(2,1)}, bf16[512,2176]{1,0:T(8,128)(2,1)}, u32[]{:S(2)}, u32[]{:S(2)}) collective-permute-start(bf16[512,2176]{1,0:T(8,128)(2,1)} %bitcast.122.xa), channel_id=1, source_target_pairs={{0,1},{1,0},{2,3},{3,2},{4,5},{5,4},{6,7},{7,6},{8,9},{9,8},{10,11... | collective-permute-start | bytes 6684680 | tf_op jit(solution)/shard_map/ppermute | solution.py:98
  521.2 133.5 %collective-permute-start.22 = (bf16[512,2176]{1,0:T(8,128)(2,1)}, bf16[512,2176]{1,0:T(8,128)(2,1)}, u32[]{:S(2)}, u32[]{:S(2)}) collective-permute-start(bf16[512,2176]{1,0:T(8,128)(2,1)} %get-tuple-element.70), channel_id=1, source_target_pairs={{0,1},{1,0},{2,3},{3,2},{4,5},{5,4},{6,7},{7,6},{8,9},{9,8},{10,11... | collective-permute-start | bytes 6684680 | tf_op jit(solution)/shard_map/ppermute | solution.py:98
  553.1 117.5 %collective-permute-start.57 = (bf16[512,2176]{1,0:T(8,128)(2,1)}, bf16[512,2176]{1,0:T(8,128)(2,1)}, u32[]{:S(2)}, u32[]{:S(2)}) collective-permute-start(bf16[512,2176]{1,0:T(8,128)(2,1)} %get-tuple-element.77), channel_id=1, source_target_pairs={{0,1},{1,0},{2,3},{3,2},{4,5},{5,4},{6,7},{7,6},{8,9},{9,8},{10,11... | collective-permute-start | bytes 6684680 | tf_op jit(solution)/shard_map/ppermute | solution.py:98
  579.2 95.4 %collective-permute-start.33 = (bf16[512,2176]{1,0:T(8,128)(2,1)}, bf16[512,2176]{1,0:T(8,128)(2,1)S(1)}, u32[]{:S(2)}, u32[]{:S(2)}) collective-permute-start(bf16[512,2176]{1,0:T(8,128)(2,1)} %get-tuple-element.72), channel_id=1, source_target_pairs={{0,1},{1,0},{2,3},{3,2},{4,5},{5,4},{6,7},{7,6},{8,9},{9,8},{10,11... | collective-permute-start | bytes 6684680 | tf_op jit(solution)/shard_map/ppermute | solution.py:98
  611.2 87.1 %collective-permute-start.45 = (bf16[512,2176]{1,0:T(8,128)(2,1)}, bf16[512,2176]{1,0:T(8,128)(2,1)S(1)}, u32[]{:S(2)}, u32[]{:S(2)}) collective-permute-start(bf16[512,2176]{1,0:T(8,128)(2,1)} %get-tuple-element.75), channel_id=1, source_target_pairs={{0,1},{1,0},{2,3},{3,2},{4,5},{5,4},{6,7},{7,6},{8,9},{9,8},{10,11... | collective-permute-start | bytes 6684680 | tf_op jit(solution)/shard_map/ppermute | solution.py:98
  670.5 72.9 %collective-permute-start.24 = (bf16[128,1024]{1,0:T(8,128)(2,1)S(1)}, bf16[128,1024]{1,0:T(8,128)(2,1)S(1)}, u32[]{:S(2)}, u32[]{:S(2)}) collective-permute-start(bf16[128,1024]{1,0:T(8,128)(2,1)S(1)} %fusion.68), channel_id=1, source_target_pairs={{0,4},{4,0},{8,12},{12,8},{16,20},{20,16},{24,28},{28,24},{1,5},{5... | collective-permute-start | bytes 786440 | tf_op jit(solution)/shard_map/ppermute | solution.py:98
  785.6 129.8 %collective-permute-start.63 = (bf16[4,4,128,2048]{3,2,1,0:T(8,128)(2,1)}, bf16[4,4,128,2048]{3,2,1,0:T(8,128)(2,1)}, u32[]{:S(2)}, u32[]{:S(2)}) collective-permute-start(bf16[4,4,128,2048]{3,2,1,0:T(8,128)(2,1)} %pad_maximum_fusion.1), channel_id=1, source_target_pairs={{0,1},{1,0},{2,3},{3,2},{4,5},{5,4},{6,7},{7,6},{8,9},{9,8},{10,11... | collective-permute-start | bytes 25165832 | tf_op jit(solution)/shard_map/ppermute | solution.py:98
  836.5 90.1 %collective-permute-start.78 = (bf16[256,1024]{1,0:T(8,128)(2,1)}, bf16[256,1024]{1,0:T(8,128)(2,1)}, u32[]{:S(2)}, u32[]{:S(2)}) collective-permute-start(bf16[256,1024]{1,0:T(8,128)(2,1)} %get-tuple-element.218), channel_id=1, source_target_pairs={{0,4},{4,0},{16,20},{20,16},{24,28},{28,24},{8,12},{12,8},{1,5},{5... | collective-permute-start | bytes 1572872 | tf_op jit(solution)/shard_map/ppermute | solution.py:219
  836.8 90.2 %collective-permute-start.79 = (bf16[256,1024]{1,0:T(8,128)(2,1)}, bf16[256,1024]{1,0:T(8,128)(2,1)}, u32[]{:S(2)}, u32[]{:S(2)}) collective-permute-start(bf16[256,1024]{1,0:T(8,128)(2,1)} %get-tuple-element.217), channel_id=1, source_target_pairs={{0,16},{4,20},{16,24},{20,28},{24,8},{28,12},{8,0},{12,4},{1,17},{... | collective-permute-start | bytes 1572872 | tf_op jit(solution)/shard_map/ppermute | solution.py:219
  836.9 91.7 %collective-permute-start.80 = (bf16[256,1024]{1,0:T(8,128)(2,1)}, bf16[256,1024]{1,0:T(8,128)(2,1)}, u32[]{:S(2)}, u32[]{:S(2)}) collective-permute-start(bf16[256,1024]{1,0:T(8,128)(2,1)} %get-tuple-element.216), channel_id=1, source_target_pairs={{0,20},{4,16},{16,28},{20,24},{24,12},{28,8},{8,4},{12,0},{1,21},{... | collective-permute-start | bytes 1572872 | tf_op jit(solution)/shard_map/ppermute | solution.py:219
  840.1 89.6 %collective-permute-start.81 = (bf16[256,1024]{1,0:T(8,128)(2,1)}, bf16[256,1024]{1,0:T(8,128)(2,1)}, u32[]{:S(2)}, u32[]{:S(2)}) collective-permute-start(bf16[256,1024]{1,0:T(8,128)(2,1)} %get-tuple-element.215), channel_id=1, source_target_pairs={{0,24},{4,28},{16,8},{20,12},{24,0},{28,4},{8,16},{12,20},{1,25},{... | collective-permute-start | bytes 1572872 | tf_op jit(solution)/shard_map/ppermute | solution.py:219
  908.0 186.8 %all-to-all-start.5 = ((bf16[4,8,64,768]{3,2,1,0:T(8,128)(2,1)}), bf16[4,8,64,768]{3,2,1,0:T(8,128)(2,1)}, u32[]{:S(2)}, u32[]{:S(2)}) async-start(bf16[4,8,64,768]{3,2,1,0:T(8,128)(2,1)} %bitcast.539), calls=%async_computation.5 | async-start | bytes 6291456 | tf_op jit(solution)/shard_map/all_to_all | solution.py:66
  927.0 60.4 %collective-permute-start.74 = (bf16[128,2048]{1,0:T(8,128)(2,1)S(1)}, bf16[128,2048]{1,0:T(8,128)(2,1)S(1)}, u32[]{:S(2)}, u32[]{:S(2)}) collective-permute-start(bf16[128,2048]{1,0:T(8,128)(2,1)S(1)} %get-tuple-element.222), channel_id=1, source_target_pairs={{0,4},{4,0},{8,12},{12,8},{16,20},{20,16},{24,28},{28,24},{1,5},{5... | collective-permute-start | bytes 1572872 | tf_op jit(solution)/shard_map/ppermute | solution.py:98
  929.5 60.8 %collective-permute-start.82 = (bf16[256,1024]{1,0:T(8,128)(2,1)S(1)}, bf16[256,1024]{1,0:T(8,128)(2,1)S(1)}, u32[]{:S(2)}, u32[]{:S(2)}) collective-permute-start(bf16[256,1024]{1,0:T(8,128)(2,1)S(1)} %copy-done.57), channel_id=1, source_target_pairs={{0,28},{4,24},{16,12},{20,8},{24,4},{28,0},{8,20},{12,16},{1,29},{... | collective-permute-start | bytes 1572872 | tf_op jit(solution)/shard_map/ppermute | solution.py:219
  929.7 62.0 %collective-permute-start.83 = (bf16[256,1024]{1,0:T(8,128)(2,1)S(1)}, bf16[256,1024]{1,0:T(8,128)(2,1)S(1)}, u32[]{:S(2)}, u32[]{:S(2)}) collective-permute-start(bf16[256,1024]{1,0:T(8,128)(2,1)S(1)} %copy-done.56), channel_id=1, source_target_pairs={{0,8},{4,12},{16,0},{20,4},{24,16},{28,20},{8,24},{12,28},{1,9},{5... | collective-permute-start | bytes 1572872 | tf_op jit(solution)/shard_map/ppermute | solution.py:219
  934.5 57.2 %collective-permute-start.84 = (bf16[256,1024]{1,0:T(8,128)(2,1)S(1)}, bf16[256,1024]{1,0:T(8,128)(2,1)S(1)}, u32[]{:S(2)}, u32[]{:S(2)}) collective-permute-start(bf16[256,1024]{1,0:T(8,128)(2,1)S(1)} %copy-done.55), channel_id=1, source_target_pairs={{0,12},{4,8},{16,4},{20,0},{24,20},{28,16},{8,28},{12,24},{1,13},{... | collective-permute-start | bytes 1572872 | tf_op jit(solution)/shard_map/ppermute | solution.py:219
  991.7 100.9 %collective-permute-start.77 = (bf16[128,2048]{1,0:T(8,128)(2,1)}, bf16[128,2048]{1,0:T(8,128)(2,1)}, u32[]{:S(2)}, u32[]{:S(2)}) collective-permute-start(bf16[128,2048]{1,0:T(8,128)(2,1)} %get-tuple-element.225), channel_id=1, source_target_pairs={{0,16},{4,20},{16,24},{20,28},{24,8},{28,12},{8,0},{12,4},{1,17},{... | collective-permute-start | bytes 1572872 | tf_op jit(solution)/shard_map/ppermute | solution.py:93
  991.7 100.9 %collective-permute-start.75 = (bf16[128,2048]{1,0:T(8,128)(2,1)}, bf16[128,2048]{1,0:T(8,128)(2,1)}, u32[]{:S(2)}, u32[]{:S(2)}) collective-permute-start(bf16[128,2048]{1,0:T(8,128)(2,1)} %get-tuple-element.226), channel_id=1, source_target_pairs={{0,24},{4,28},{16,8},{20,12},{24,0},{28,4},{8,16},{12,20},{1,25},{... | collective-permute-start | bytes 1572872 | tf_op jit(solution)/shard_map/ppermute | solution.py:93
  1025.4 67.2 %collective-permute-start.73 = (bf16[128,2048]{1,0:T(8,128)(2,1)}, bf16[128,2048]{1,0:T(8,128)(2,1)}, u32[]{:S(2)}, u32[]{:S(2)}) collective-permute-start(bf16[128,2048]{1,0:T(8,128)(2,1)} %get-tuple-element.224), channel_id=1, source_target_pairs={{0,8},{4,12},{16,0},{20,4},{24,16},{28,20},{8,24},{12,28},{1,9},{5... | collective-permute-start | bytes 1572872 | tf_op jit(solution)/shard_map/ppermute | solution.py:93
  1033.9 68.5 %collective-permute-start.65 = (bf16[4,128,1024]{2,1,0:T(8,128)(2,1)}, bf16[4,128,1024]{2,1,0:T(8,128)(2,1)}, u32[]{:S(2)}, u32[]{:S(2)}) collective-permute-start(bf16[4,128,1024]{2,1,0:T(8,128)(2,1)} %fusion.19), channel_id=1, source_target_pairs={{0,4},{4,0},{8,12},{12,8},{16,20},{20,16},{24,28},{28,24},{1,5},{5... | collective-permute-start | bytes 3145736 | tf_op jit(solution)/shard_map/ppermute | solution.py:98
  1045.1 57.4 %collective-permute-start.67 = (bf16[4,128,1024]{2,1,0:T(8,128)(2,1)}, bf16[4,128,1024]{2,1,0:T(8,128)(2,1)}, u32[]{:S(2)}, u32[]{:S(2)}) collective-permute-start(bf16[4,128,1024]{2,1,0:T(8,128)(2,1)} %fusion.16), channel_id=1, source_target_pairs={{0,2},{1,3},{2,0},{3,1},{4,6},{5,7},{6,4},{7,5},{8,10},{9,11},{10,... | collective-permute-start | bytes 3145736 | tf_op jit(solution)/shard_map/ppermute | solution.py:98
  (151 other events, 3758.6 us)
Sparse Core Ops, SparseCore 0:
  10.1 121.6 all-gather.2
  134.7 130.0 all-gather.4
  795.5 180.1 reduce-scatter.1

commit v6 on v5

--- a/solution.py
+++ b/solution.py
@@ -118,10 +118,10 @@
     return [(inner, bits) for bits in range(0, size, 2) for inner in range(2)][1:]
 
 
-def ring_blocks(vals):
+def ring_blocks(vals, urgent=False):
     blocks = [vals]
     for step in range(1, lax.axis_size("dp") // 2):
-        blocks.append(ring_shift(after(vals, blocks[1]) if step == 2 else vals, step))
+        blocks.append(ring_shift(after(vals, blocks[1]) if urgent and step > 1 else vals, step))
     return blocks
 
 
@@ -219,7 +219,7 @@
             block = lax.ppermute(block, "dp", walk_perm(n_dp, index))
         moved.append(block)
     if wait_for is not None:
-        moved = [after(block, wait_for) for block in moved]
+        moved = [after(block, *wait_for) for block in moved]
     return pick_rows(jnp.stack(moved), step_of)
 
 
@@ -519,7 +519,7 @@
     lean = n_all * rows > 4096
     n2_sets, mix_parts, home_parts, pre_grads, gated_inners = [], [], [], [], []
     w1_grad, down_grad = 0.0, 0.0
-    for step, block in enumerate(ring_blocks(payload)):
+    for step, block in enumerate(ring_blocks(payload, True)):
         near = gather_peers(block).reshape(-1, block.shape[-1])
         far = core_flip(near)
         ma, mb, ra, rb, pre_grad, gated_inner = experts(
@@ -548,7 +548,7 @@
     if not lean:
         mix_near = jnp.stack([m[0].reshape(-1, rows, width) for m in mix_parts], axis=1)
         mix_far = jnp.stack([m[1].reshape(-1, rows, width) for m in mix_parts], axis=1)
-        mix_far = after(mix_far, returned)
+        mix_far = after(mix_far, part)
         mix_near = add(mix_near, core_flip(mix_far))
         mix_parts = list(reduce_peers(mix_near))
         by_chunk = jnp.stack([g.reshape(2, -1, rows, half) for g in gated_inners], axis=2)
@@ -602,7 +602,7 @@
     for step in range(n_dp // 2):
         sums.append(add(part_bf[step, 0], flip(part_bf[step, 1], "dp", 1)))
     normed_one_grad = home(sums)
-    w1_grad = walk_swap(w1_grad.reshape(n_dp, cols, -1), tables, sums[-1])
+    w1_grad = walk_swap(w1_grad.reshape(n_dp, cols, -1), tables, (sums[-1], mix_parts[-1]))
 
     def unpack(blocks):
         blocks = blocks.reshape(n_dp, cols, local_count, ff_part).transpose(2, 1, 0, 3)

time: 1190 us -> 1260 us (1.059)
  waiting for transfers between devices: 471 us -> 509 us
  starting transfers between devices: 116 us -> 141 us
    ppermute x14, waiting for transfers between devices: 78.4 us -> 157 us  [walk_swap(): block = lax.ppermute(block, 'dp', walk_perm(n_dp, index))]
    ppermute x56, waiting for transfers between devices: 203 us -> 160 us  [flip(): return lax.ppermute(vals, axis, [(i, i ^ bit) for i in range(size)])]
    all_to_all x7, starting transfers between devices: 41.3 us -> 66.3 us  [swap(): return lax.all_to_all(blocks, axes, split_axis=0, concat_axis=0, tiled=True)]
    unnamed x210 -> x208, local copies, waits for them, and re-layouts: 76.1 us -> 75 us
  transfers between devices with their start and end apart: 95 -> 95, of which waited for: 41 -> 44; matrix products, arithmetic and copies ran while one was open for 36% -> 34% of each run, Pallas kernels for 11% -> 10%
where the time goes in v6:
time: 1260 us; the launch traced here: 1230 us
  waiting for transfers between devices  509 us (40%)
  local copies, waits for them, and re-layouts  221 us (18%)
  starting transfers between devices  141 us (11%)
  Pallas kernels  124 us (10%)
  other arithmetic  123 us (10%)
  matrix products  85.9 us (7%)
  between operations  31.4 us (2%)
    ppermute x56, waiting for transfers between devices, flip(): return lax.ppermute(vals, axis, [(i, i ^ bit) for i in range(size)])  160 us
    ppermute x14, waiting for transfers between devices, walk_swap(): block = lax.ppermute(block, 'dp', walk_perm(n_dp, index))  157 us
    ppermute x15, waiting for transfers between devices, ring_shift(): return lax.ppermute(vals, 'dp', ring_perm(lax.axis_size('dp'), steps))  128 us
    pallas_call x4, Pallas kernels, experts(): pl.pallas_call(body, grid=(2 * halves,), in_specs=[pl.BlockSpec((tile, wi...  102 us
    unnamed x208, local copies, waits for them, and re-layouts  75 us
    all_to_all x7, starting transfers between devices, swap(): return lax.all_to_all(blocks, axes, split_axis=0, concat_axis=0, tiled=True)  66.3 us
    all_to_all x7, waiting for transfers between devices, swap(): return lax.all_to_all(blocks, axes, split_axis=0, concat_axis=0, tiled=True)  63 us
    dot_general x6, matrix products, dot_rows(): lax.dot_general(left_mat, right_mat, (((0,), (0,)), ((), ())), preferred_...  61 us
  transfers between devices with their start and end apart: 95, of which 44 were waited for; matrix products, arithmetic and copies ran while one was open for 34% of the time, Pallas kernels for 10%

profile of v6, /device:TPU:13, one launch (start us, length us, event | category | flops | bytes accessed | tf_op | source)
XLA Modules:
  0.0 1234.1 jit_solution(997247543208646134)
XLA Ops:
  41.5 10.8 all-to-all-done
  60.8 10.1 all-to-all-done.1
  78.8 34.3 %collective-permute-done.16 = bf16[128,2048]{1,0:T(8,128)(2,1)S(1)} collective-permute-done((bf16[128,2048]{1,0:T(8,128)(2,1)}, bf16[128,2048]{1,0:T(8,128)(2,1)S(1)}, u32[]{:S(2)}, u32[]{:S(2)}) %collective-permute-start.16) | collective-permute-done | bytes 524320 | tf_op jit(solution)/shard_map/ppermute | solution.py:93
  113.1 30.9 %collective-permute-done.15 = bf16[128,2048]{1,0:T(8,128)(2,1)S(1)} collective-permute-done((bf16[128,2048]{1,0:T(8,128)(2,1)}, bf16[128,2048]{1,0:T(8,128)(2,1)S(1)}, u32[]{:S(2)}, u32[]{:S(2)}) %collective-permute-start.15) | collective-permute-done | bytes 524320 | tf_op jit(solution)/shard_map/ppermute | solution.py:93
  210.3 28.3 %collective-permute-done.2 = bf16[256,1024]{1,0:T(8,128)(2,1)} collective-permute-done((bf16[256,1024]{1,0:T(8,128)(2,1)}, bf16[256,1024]{1,0:T(8,128)(2,1)}, u32[]{:S(2)}, u32[]{:S(2)}) %collective-permute-start.2) | collective-permute-done | bytes 524320 | tf_op jit(solution)/shard_map/ppermute | solution.py:219
  244.2 24.7 %collective-permute-done.5 = bf16[256,1024]{1,0:T(8,128)(2,1)S(1)} collective-permute-done((bf16[256,1024]{1,0:T(8,128)(2,1)S(1)}, bf16[256,1024]{1,0:T(8,128)(2,1)S(1)}, u32[]{:S(2)}, u32[]{:S(2)}) %collective-permute-start.5) | collective-permute-done | bytes 524320 | tf_op jit(solution)/shard_map/ppermute | solution.py:219
  290.0 10.4 collective-permute-done.8
  434.1 17.2 %collective-permute-done.39 = bf16[128,2176]{1,0:T(8,128)(2,1)S(1)} collective-permute-done((bf16[128,2176]{1,0:T(8,128)(2,1)}, bf16[128,2176]{1,0:T(8,128)(2,1)S(1)}, u32[]{:S(2)}, u32[]{:S(2)}) %collective-permute-start.39) | collective-permute-done | bytes 557088 | tf_op jit(solution)/shard_map/ppermute | solution.py:93
  481.0 10.0 collective-permute-done.43
  500.1 25.5 %experts.4 = (bf16[512,2048]{1,0:T(8,128)(2,1)}, bf16[512,2048]{1,0:T(8,128)(2,1)}, bf16[512,2176]{1,0:T(8,128)(2,1)}, bf16[512,2176]{1,0:T(8,128)(2,1)}, bf16[1...) custom-call(bf16[512,2176]{1,0:T(8,128)(2,1)} %bitcast.544, bf16[512,2176]{1,0:T(8,128)(2,1)} %collective-permute-done.13.xb, ...), custom_call_target="tpu_custom_call" | custom-call | flops 12884901888 | bytes 20971520 | tf_op jit(solution)/shard_map/experts/pallas_call | solution.py:290
  532.1 25.4 %experts.5 = (bf16[512,2048]{1,0:T(8,128)(2,1)}, bf16[512,2048]{1,0:T(8,128)(2,1)}, bf16[512,2176]{1,0:T(8,128)(2,1)}, bf16[512,2176]{1,0:T(8,128)(2,1)}, bf16[1...) custom-call(bf16[512,2176]{1,0:T(8,128)(2,1)} %bitcast.101.xa, bf16[512,2176]{1,0:T(8,128)(2,1)} %collective-permute-done.32.xb, ...), custom_call_target="tpu_custom_call" | custom-call | flops 12884901888 | bytes 20971520 | tf_op jit(solution)/shard_map/experts/pallas_call | solution.py:290
  564.5 25.6 %experts.7 = (bf16[512,2048]{1,0:T(8,128)(2,1)}, bf16[512,2048]{1,0:T(8,128)(2,1)}, bf16[512,2176]{1,0:T(8,128)(2,1)}, bf16[512,2176]{1,0:T(8,128)(2,1)}, bf16[1...) custom-call(bf16[512,2176]{1,0:T(8,128)(2,1)} %bitcast.143.xa, bf16[512,2176]{1,0:T(8,128)(2,1)} %collective-permute-done.56.xb, ...), custom_call_target="tpu_custom_call" | custom-call | flops 12884901888 | bytes 20971520 | tf_op jit(solution)/shard_map/experts/pallas_call | solution.py:290
  590.2 25.5 %experts.6 = (bf16[512,2048]{1,0:T(8,128)(2,1)}, bf16[512,2048]{1,0:T(8,128)(2,1)}, bf16[512,2176]{1,0:T(8,128)(2,1)}, bf16[512,2176]{1,0:T(8,128)(2,1)}, bf16[1...) custom-call(bf16[512,2176]{1,0:T(8,128)(2,1)} %bitcast.122.xa, bf16[512,2176]{1,0:T(8,128)(2,1)} %collective-permute-done.44.xb, ...), custom_call_target="tpu_custom_call" | custom-call | flops 12884901888 | bytes 20971520 | tf_op jit(solution)/shard_map/experts/pallas_call | solution.py:290
  636.4 24.0 %fusion.13 = bf16[2048,1024]{1,0:T(8,128)(2,1)} fusion(bf16[4096,2048]{1,0:T(8,128)(2,1)} %slice_dynamic-update-slice_fusion, bf16[1024,1024]{1,0:T(8,128)(2,1)S(1)} %copy-done.85, bf16[1024,1024]{1,0:T(8,128)(2,1)S(1)} %copy-done.86, bf16[1024,1024]{1,0:T(8,128)(2,1)S(1)} %copy-done.84, bf16[1024,1024]{1,0:T(8,128)(2,1)S(1)} %copy-done.83), kind=kOutput, calls=%fused_computation.35 | convolution fusion | flops 17215520768 | bytes 29360128 | tf_op jit(solution)/shard_map/dot_general | solution.py:51
  664.6 11.7 collective-permute-done.23
  696.6 12.1 collective-permute-done.36
  716.2 12.0 collective-permute-done.58
  728.3 11.1 collective-permute-done.46
  767.4 10.4 collective-permute-done.62
  777.8 26.1 %collective-permute-done.50 = bf16[128,2176]{1,0:T(8,128)(2,1)S(1)} collective-permute-done((bf16[128,2176]{1,0:T(8,128)(2,1)S(1)}, bf16[128,2176]{1,0:T(8,128)(2,1)S(1)}, u32[]{:S(2)}, u32[]{:S(2)}) %collective-permute-start.50) | collective-permute-done | bytes 557088 | tf_op jit(solution)/shard_map/ppermute | solution.py:93
  824.3 10.6 fusion.121
  839.0 13.3 %attend_back.1 = (f32[1024,256]{1,0:T(8,128)}, f32[1024,256]{1,0:T(8,128)}, bf16[1024,256]{1,0:T(8,128)(2,1)}) custom-call(bf16[1024,256]{1,0:T(8,128)(2,1)} %copy.375.q, bf16[1024,256]{1,0:T(8,128)(2,1)} %copy.376.k, bf16[1024,256]{1,0:T(8,128)(2,1)} %copy.384.v, f32[1,1024]{1,0:T(1,128)} %bitcast.632, bf16[1024,256]{1,0:T(8,128)(2,1)} %bitcast.627), custom_call_target="tpu_custom_call" | custom-call | flops 2684354560 | bytes 5242880 | tf_op jit(solution)/shard_map/attend_back/pallas_call | solution.py:383
  883.0 13.3 %all-to-all-start.4 = ((f32[32,1,1160]{2,1,0:T(1,128)}), f32[32,1,1160]{2,1,0:T(1,128)S(1)}, u32[]{:S(2)}, u32[]{:S(2)}) async-start(f32[32,1,1160]{2,1,0:T(1,128)} %copy.357), calls=%async_computation.4 | async-start | bytes 327680 | tf_op jit(solution)/shard_map/all_to_all | solution.py:66
  920.9 21.2 %all-to-all-done.4 = f32[32,1,1160]{2,1,0:T(1,128)S(1)} async-done(((f32[32,1,1160]{2,1,0:T(1,128)}), f32[32,1,1160]{2,1,0:T(1,128)S(1)}, u32[]{:S(2)}, u32[]{:S(2)}) %all-to-all-start.4) | async-done | bytes 148512 | tf_op jit(solution)/shard_map/all_to_all | solution.py:66
  947.5 11.9 convolution_add_fusion
  966.1 29.0 %collective-permute-done.71 = bf16[128,2048]{1,0:T(8,128)(2,1)S(1)} collective-permute-done((bf16[128,2048]{1,0:T(8,128)(2,1)S(1)}, bf16[128,2048]{1,0:T(8,128)(2,1)S(1)}, u32[]{:S(2)}, u32[]{:S(2)}) %collective-permute-start.71) | collective-permute-done | bytes 524320 | tf_op jit(solution)/shard_map/ppermute | solution.py:98
  1010.6 13.7 %all-to-all-done.5 = bf16[4,8,64,768]{3,2,1,0:T(8,128)(2,1)} async-done(((bf16[4,8,64,768]{3,2,1,0:T(8,128)(2,1)}), bf16[4,8,64,768]{3,2,1,0:T(8,128)(2,1)}, u32[]{:S(2)}, u32[]{:S(2)}) %all-to-all-start.5) | async-done | bytes 3145760 | tf_op jit(solution)/shard_map/all_to_all | solution.py:66
  1027.8 22.5 %all-to-all-start.6 = ((bf16[8,64,768]{2,1,0:T(8,128)(2,1)}), bf16[8,64,768]{2,1,0:T(8,128)(2,1)}, u32[]{:S(2)}, u32[]{:S(2)}) async-start(bf16[8,64,768]{2,1,0:T(8,128)(2,1)} %reduce_sum.224), calls=%async_computation.6 | async-start | bytes 1572864 | tf_op jit(solution)/shard_map/all_to_all | solution.py:66
  1093.1 18.1 %collective-permute-done.81 = bf16[256,1024]{1,0:T(8,128)(2,1)S(1)} collective-permute-done((bf16[256,1024]{1,0:T(8,128)(2,1)S(1)}, bf16[256,1024]{1,0:T(8,128)(2,1)S(1)}, u32[]{:S(2)}, u32[]{:S(2)}) %collective-permute-start.81) | collective-permute-done | bytes 524320 | tf_op jit(solution)/shard_map/ppermute | solution.py:219
  1111.2 17.5 %collective-permute-done.82 = bf16[256,1024]{1,0:T(8,128)(2,1)S(1)} collective-permute-done((bf16[256,1024]{1,0:T(8,128)(2,1)S(1)}, bf16[256,1024]{1,0:T(8,128)(2,1)S(1)}, u32[]{:S(2)}, u32[]{:S(2)}) %collective-permute-start.82) | collective-permute-done | bytes 524320 | tf_op jit(solution)/shard_map/ppermute | solution.py:219
  1128.9 30.6 %collective-permute-done.83 = bf16[256,1024]{1,0:T(8,128)(2,1)S(1)} collective-permute-done((bf16[256,1024]{1,0:T(8,128)(2,1)S(1)}, bf16[256,1024]{1,0:T(8,128)(2,1)S(1)}, u32[]{:S(2)}, u32[]{:S(2)}) %collective-permute-start.83) | collective-permute-done | bytes 524320 | tf_op jit(solution)/shard_map/ppermute | solution.py:219
  1159.5 11.2 collective-permute-done.84
  (638 shorter events, 603.6 us)
Async XLA Ops:
  7.2 323.4 %all-gather.3.cloned.1.call-start = ((), (), s32[]{:S(2)}) async-start(), calls=%async_computation.8 | async-start | bytes 4718592 | tf_op jit(solution)/shard_map/all_gather | solution.py:70
  7.9 379.9 %all-gather.5.cloned.1.call-start = ((), (), s32[]{:S(2)}) async-start(), calls=%async_computation.9 | async-start | bytes 8650752 | tf_op jit(solution)/shard_map/all_gather | solution.py:70
  71.6 72.4 %collective-permute-start.15 = (bf16[128,2048]{1,0:T(8,128)(2,1)}, bf16[128,2048]{1,0:T(8,128)(2,1)S(1)}, u32[]{:S(2)}, u32[]{:S(2)}) collective-permute-start(bf16[128,2048]{1,0:T(8,128)(2,1)} %param.20), channel_id=1, source_target_pairs={{0,24},{4,28},{16,8},{20,12},{24,0},{28,4},{8,16},{12,20},{1,25},{... | collective-permute-start | bytes 1572872 | tf_op jit(solution)/shard_map/ppermute | solution.py:93
  73.0 71.0 %collective-permute-start.14 = (bf16[128,2048]{1,0:T(8,128)(2,1)}, bf16[128,2048]{1,0:T(8,128)(2,1)}, u32[]{:S(2)}, u32[]{:S(2)}) collective-permute-start(bf16[128,2048]{1,0:T(8,128)(2,1)} %param.20), channel_id=1, source_target_pairs={{0,16},{4,20},{16,24},{20,28},{24,8},{28,12},{8,0},{12,4},{1,17},{... | collective-permute-start | bytes 1572872 | tf_op jit(solution)/shard_map/ppermute | solution.py:93
  77.1 111.3 %collective-permute-start = (bf16[1,8,64,768]{3,2,1,0:T(8,128)(2,1)S(1)}, bf16[1,8,64,768]{3,2,1,0:T(8,128)(2,1)}, u32[]{:S(2)}, u32[]{:S(2)}) collective-permute-start(bf16[1,8,64,768]{3,2,1,0:T(8,128)(2,1)S(1)} %reshape.783), channel_id=1, source_target_pairs={{0,1},{1,0},{2,3},{3,2},{4,5},{5,4},{6,7},{7,6},{8,9},{9,8},{10,11... | collective-permute-start | bytes 2359304 | tf_op jit(solution)/shard_map/ppermute | solution.py:98
  208.7 112.5 %collective-permute-start.19 = (bf16[2,4,128,1024]{3,2,1,0:T(8,128)(2,1)}, bf16[2,4,128,1024]{3,2,1,0:T(8,128)(2,1)}, u32[]{:S(2)}, u32[]{:S(2)}) collective-permute-start(bf16[2,4,128,1024]{3,2,1,0:T(8,128)(2,1)} %pad_maximum_fusion.9), channel_id=1, source_target_pairs={{0,4},{4,0},{8,12},{12,8},{16,20},{20,16},{24,28},{28,24},{1,5},{5... | collective-permute-start | bytes 6291464 | tf_op jit(solution)/shard_map/ppermute | solution.py:98
  239.0 73.7 %collective-permute-start.1 = (bf16[2,8,64,768]{3,2,1,0:T(8,128)(2,1)}, bf16[2,8,64,768]{3,2,1,0:T(8,128)(2,1)}, u32[]{:S(2)}, u32[]{:S(2)}) collective-permute-start(bf16[2,8,64,768]{3,2,1,0:T(8,128)(2,1)} %pad_maximum_fusion.13), channel_id=1, source_target_pairs={{0,2},{1,3},{2,0},{3,1},{4,6},{5,7},{6,4},{7,5},{8,10},{9,11},{10,... | collective-permute-start | bytes 4718600 | tf_op jit(solution)/shard_map/ppermute | solution.py:98
  239.0 83.9 %collective-permute-start.20 = (bf16[2,4,128,1024]{3,2,1,0:T(8,128)(2,1)}, bf16[2,4,128,1024]{3,2,1,0:T(8,128)(2,1)}, u32[]{:S(2)}, u32[]{:S(2)}) collective-permute-start(bf16[2,4,128,1024]{3,2,1,0:T(8,128)(2,1)} %pad_maximum_fusion.10), channel_id=1, source_target_pairs={{0,2},{1,3},{2,0},{3,1},{4,6},{5,7},{6,4},{7,5},{8,10},{9,11},{10,... | collective-permute-start | bytes 6291464 | tf_op jit(solution)/shard_map/ppermute | solution.py:98
  378.2 121.9 %collective-permute-start.21 = (bf16[4,4,128,2048]{3,2,1,0:T(8,128)(2,1)}, bf16[4,4,128,2048]{3,2,1,0:T(8,128)(2,1)}, u32[]{:S(2)}, u32[]{:S(2)}) collective-permute-start(bf16[4,4,128,2048]{3,2,1,0:T(8,128)(2,1)} %pad_maximum_fusion.ya), channel_id=1, source_target_pairs={{0,1},{1,0},{2,3},{3,2},{4,5},{5,4},{6,7},{7,6},{8,9},{9,8},{10,11... | collective-permute-start | bytes 25165832 | tf_op jit(solution)/shard_map/ppermute | solution.py:98
  496.7 67.8 %collective-permute-start.56 = (bf16[512,2176]{1,0:T(8,128)(2,1)}, bf16[512,2176]{1,0:T(8,128)(2,1)}, u32[]{:S(2)}, u32[]{:S(2)}) collective-permute-start(bf16[512,2176]{1,0:T(8,128)(2,1)} %bitcast.143.xa), channel_id=1, source_target_pairs={{0,1},{1,0},{2,3},{3,2},{4,5},{5,4},{6,7},{7,6},{8,9},{9,8},{10,11... | collective-permute-start | bytes 6684680 | tf_op jit(solution)/shard_map/ppermute | solution.py:98
  498.6 91.6 %collective-permute-start.44 = (bf16[512,2176]{1,0:T(8,128)(2,1)}, bf16[512,2176]{1,0:T(8,128)(2,1)}, u32[]{:S(2)}, u32[]{:S(2)}) collective-permute-start(bf16[512,2176]{1,0:T(8,128)(2,1)} %bitcast.122.xa), channel_id=1, source_target_pairs={{0,1},{1,0},{2,3},{3,2},{4,5},{5,4},{6,7},{7,6},{8,9},{9,8},{10,11... | collective-permute-start | bytes 6684680 | tf_op jit(solution)/shard_map/ppermute | solution.py:98
  525.6 134.7 %collective-permute-start.22 = (bf16[512,2176]{1,0:T(8,128)(2,1)}, bf16[512,2176]{1,0:T(8,128)(2,1)}, u32[]{:S(2)}, u32[]{:S(2)}) collective-permute-start(bf16[512,2176]{1,0:T(8,128)(2,1)} %get-tuple-element.67), channel_id=1, source_target_pairs={{0,1},{1,0},{2,3},{3,2},{4,5},{5,4},{6,7},{7,6},{8,9},{9,8},{10,11... | collective-permute-start | bytes 6684680 | tf_op jit(solution)/shard_map/ppermute | solution.py:98
  557.5 120.0 %collective-permute-start.33 = (bf16[512,2176]{1,0:T(8,128)(2,1)}, bf16[512,2176]{1,0:T(8,128)(2,1)}, u32[]{:S(2)}, u32[]{:S(2)}) collective-permute-start(bf16[512,2176]{1,0:T(8,128)(2,1)} %get-tuple-element.69), channel_id=1, source_target_pairs={{0,1},{1,0},{2,3},{3,2},{4,5},{5,4},{6,7},{7,6},{8,9},{9,8},{10,11... | collective-permute-start | bytes 6684680 | tf_op jit(solution)/shard_map/ppermute | solution.py:98
  590.1 102.3 %collective-permute-start.57 = (bf16[512,2176]{1,0:T(8,128)(2,1)}, bf16[512,2176]{1,0:T(8,128)(2,1)S(1)}, u32[]{:S(2)}, u32[]{:S(2)}) collective-permute-start(bf16[512,2176]{1,0:T(8,128)(2,1)} %get-tuple-element.74), channel_id=1, source_target_pairs={{0,1},{1,0},{2,3},{3,2},{4,5},{5,4},{6,7},{7,6},{8,9},{9,8},{10,11... | collective-permute-start | bytes 6684680 | tf_op jit(solution)/shard_map/ppermute | solution.py:98
  615.7 78.7 %collective-permute-start.45 = (bf16[512,2176]{1,0:T(8,128)(2,1)}, bf16[512,2176]{1,0:T(8,128)(2,1)S(1)}, u32[]{:S(2)}, u32[]{:S(2)}) collective-permute-start(bf16[512,2176]{1,0:T(8,128)(2,1)} %get-tuple-element.72), channel_id=1, source_target_pairs={{0,1},{1,0},{2,3},{3,2},{4,5},{5,4},{6,7},{7,6},{8,9},{9,8},{10,11... | collective-permute-start | bytes 6684680 | tf_op jit(solution)/shard_map/ppermute | solution.py:98
  623.3 281.3 %collective-permute-start.63 = (bf16[4,4,128,2048]{3,2,1,0:T(8,128)(2,1)}, bf16[4,4,128,2048]{3,2,1,0:T(8,128)(2,1)}, u32[]{:S(2)}, u32[]{:S(2)}) collective-permute-start(bf16[4,4,128,2048]{3,2,1,0:T(8,128)(2,1)} %pad_maximum_fusion.1), channel_id=1, source_target_pairs={{0,1},{1,0},{2,3},{3,2},{4,5},{5,4},{6,7},{7,6},{8,9},{9,8},{10,11... | collective-permute-start | bytes 25165832 | tf_op jit(solution)/shard_map/ppermute | solution.py:98
  690.1 76.0 %collective-permute-start.24 = (bf16[128,1024]{1,0:T(8,128)(2,1)S(1)}, bf16[128,1024]{1,0:T(8,128)(2,1)S(1)}, u32[]{:S(2)}, u32[]{:S(2)}) collective-permute-start(bf16[128,1024]{1,0:T(8,128)(2,1)S(1)} %fusion.68), channel_id=1, source_target_pairs={{0,4},{4,0},{8,12},{12,8},{16,20},{20,16},{24,28},{28,24},{1,5},{5... | collective-permute-start | bytes 786440 | tf_op jit(solution)/shard_map/ppermute | solution.py:98
  817.3 408.3 %reduce-scatter.2.cloned.1.call-start = ((), (), s32[]{:S(2)}) async-start(), calls=%async_computation.10 | async-start | bytes 8650752 | tf_op jit(solution)/shard_map/reduce_scatter | solution.py:74
  879.3 80.2 %collective-permute-start.72 = (bf16[128,2048]{1,0:T(8,128)(2,1)}, bf16[128,2048]{1,0:T(8,128)(2,1)}, u32[]{:S(2)}, u32[]{:S(2)}) collective-permute-start(bf16[128,2048]{1,0:T(8,128)(2,1)} %get-tuple-element.219), channel_id=1, source_target_pairs={{0,4},{4,0},{8,12},{12,8},{16,20},{20,16},{24,28},{28,24},{1,5},{5... | collective-permute-start | bytes 1572872 | tf_op jit(solution)/shard_map/ppermute | solution.py:98
  880.2 79.3 %collective-permute-start.76 = (bf16[128,2048]{1,0:T(8,128)(2,1)}, bf16[128,2048]{1,0:T(8,128)(2,1)}, u32[]{:S(2)}, u32[]{:S(2)}) collective-permute-start(bf16[128,2048]{1,0:T(8,128)(2,1)} %get-tuple-element.217), channel_id=1, source_target_pairs={{0,4},{4,0},{8,12},{12,8},{16,20},{20,16},{24,28},{28,24},{1,5},{5... | collective-permute-start | bytes 1572872 | tf_op jit(solution)/shard_map/ppermute | solution.py:98
  880.7 78.8 %collective-permute-start.74 = (bf16[128,2048]{1,0:T(8,128)(2,1)}, bf16[128,2048]{1,0:T(8,128)(2,1)}, u32[]{:S(2)}, u32[]{:S(2)}) collective-permute-start(bf16[128,2048]{1,0:T(8,128)(2,1)} %get-tuple-element.218), channel_id=1, source_target_pairs={{0,4},{4,0},{8,12},{12,8},{16,20},{20,16},{24,28},{28,24},{1,5},{5... | collective-permute-start | bytes 1572872 | tf_op jit(solution)/shard_map/ppermute | solution.py:98
  917.8 132.5 %collective-permute-start.64 = (bf16[2,4,128,1024]{3,2,1,0:T(8,128)(2,1)}, bf16[2,4,128,1024]{3,2,1,0:T(8,128)(2,1)}, u32[]{:S(2)}, u32[]{:S(2)}) collective-permute-start(bf16[2,4,128,1024]{3,2,1,0:T(8,128)(2,1)} %pad_maximum_fusion.11), channel_id=1, source_target_pairs={{0,2},{1,3},{2,0},{3,1},{4,6},{5,7},{6,4},{7,5},{8,10},{9,11},{10,... | collective-permute-start | bytes 6291464 | tf_op jit(solution)/shard_map/ppermute | solution.py:98
  920.6 133.0 %collective-permute-start.66 = (bf16[2,4,128,1024]{3,2,1,0:T(8,128)(2,1)}, bf16[2,4,128,1024]{3,2,1,0:T(8,128)(2,1)}, u32[]{:S(2)}, u32[]{:S(2)}) collective-permute-start(bf16[2,4,128,1024]{3,2,1,0:T(8,128)(2,1)} %pad_maximum_fusion.12), channel_id=1, source_target_pairs={{0,4},{4,0},{8,12},{12,8},{16,20},{20,16},{24,28},{28,24},{1,5},{5... | collective-permute-start | bytes 6291464 | tf_op jit(solution)/shard_map/ppermute | solution.py:98
  942.1 82.2 %all-to-all-start.5 = ((bf16[4,8,64,768]{3,2,1,0:T(8,128)(2,1)}), bf16[4,8,64,768]{3,2,1,0:T(8,128)(2,1)}, u32[]{:S(2)}, u32[]{:S(2)}) async-start(bf16[4,8,64,768]{3,2,1,0:T(8,128)(2,1)} %bitcast.539), calls=%async_computation.5 | async-start | bytes 6291456 | tf_op jit(solution)/shard_map/all_to_all | solution.py:66
  1002.7 73.0 %collective-permute-start.78 = (bf16[256,1024]{1,0:T(8,128)(2,1)}, bf16[256,1024]{1,0:T(8,128)(2,1)}, u32[]{:S(2)}, u32[]{:S(2)}) collective-permute-start(bf16[256,1024]{1,0:T(8,128)(2,1)} %get-tuple-element.214), channel_id=1, source_target_pairs={{0,4},{4,0},{16,20},{20,16},{24,28},{28,24},{8,12},{12,8},{1,5},{5... | collective-permute-start | bytes 1572872 | tf_op jit(solution)/shard_map/ppermute | solution.py:219
  1002.7 73.4 %collective-permute-start.79 = (bf16[256,1024]{1,0:T(8,128)(2,1)}, bf16[256,1024]{1,0:T(8,128)(2,1)}, u32[]{:S(2)}, u32[]{:S(2)}) collective-permute-start(bf16[256,1024]{1,0:T(8,128)(2,1)} %get-tuple-element.213), channel_id=1, source_target_pairs={{0,16},{4,20},{16,24},{20,28},{24,8},{28,12},{8,0},{12,4},{1,17},{... | collective-permute-start | bytes 1572872 | tf_op jit(solution)/shard_map/ppermute | solution.py:219
  1008.5 83.2 %collective-permute-start.80 = (bf16[256,1024]{1,0:T(8,128)(2,1)}, bf16[256,1024]{1,0:T(8,128)(2,1)}, u32[]{:S(2)}, u32[]{:S(2)}) collective-permute-start(bf16[256,1024]{1,0:T(8,128)(2,1)} %get-tuple-element.212), channel_id=1, source_target_pairs={{0,20},{4,16},{16,28},{20,24},{24,12},{28,8},{8,4},{12,0},{1,21},{... | collective-permute-start | bytes 1572872 | tf_op jit(solution)/shard_map/ppermute | solution.py:219
  1084.7 74.9 %collective-permute-start.83 = (bf16[256,1024]{1,0:T(8,128)(2,1)S(1)}, bf16[256,1024]{1,0:T(8,128)(2,1)S(1)}, u32[]{:S(2)}, u32[]{:S(2)}) collective-permute-start(bf16[256,1024]{1,0:T(8,128)(2,1)S(1)} %copy-done.54), channel_id=1, source_target_pairs={{0,8},{4,12},{16,0},{20,4},{24,16},{28,20},{8,24},{12,28},{1,9},{5... | collective-permute-start | bytes 1572872 | tf_op jit(solution)/shard_map/ppermute | solution.py:219
  1084.9 85.9 %collective-permute-start.84 = (bf16[256,1024]{1,0:T(8,128)(2,1)S(1)}, bf16[256,1024]{1,0:T(8,128)(2,1)S(1)}, u32[]{:S(2)}, u32[]{:S(2)}) collective-permute-start(bf16[256,1024]{1,0:T(8,128)(2,1)S(1)} %copy-done.53), channel_id=1, source_target_pairs={{0,12},{4,8},{16,4},{20,0},{24,20},{28,16},{8,28},{12,24},{1,13},{... | collective-permute-start | bytes 1572872 | tf_op jit(solution)/shard_map/ppermute | solution.py:219
  1091.7 131.4 %collective-permute-start.70 = (bf16[128,2048]{1,0:T(8,128)(2,1)}, bf16[128,2048]{1,0:T(8,128)(2,1)}, u32[]{:S(2)}, u32[]{:S(2)}) collective-permute-start(bf16[128,2048]{1,0:T(8,128)(2,1)} %get-tuple-element.256), channel_id=1, source_target_pairs={{0,16},{4,20},{16,24},{20,28},{24,8},{28,12},{8,0},{12,4},{1,17},{... | collective-permute-start | bytes 1572872 | tf_op jit(solution)/shard_map/ppermute | solution.py:93
  1111.2 111.8 %collective-permute-start.69 = (bf16[128,2048]{1,0:T(8,128)(2,1)}, bf16[128,2048]{1,0:T(8,128)(2,1)}, u32[]{:S(2)}, u32[]{:S(2)}) collective-permute-start(bf16[128,2048]{1,0:T(8,128)(2,1)} %get-tuple-element.257), channel_id=1, source_target_pairs={{0,24},{4,28},{16,8},{20,12},{24,0},{28,4},{8,16},{12,20},{1,25},{... | collective-permute-start | bytes 1572872 | tf_op jit(solution)/shard_map/ppermute | solution.py:93
  1128.8 94.3 %collective-permute-start.68 = (bf16[128,2048]{1,0:T(8,128)(2,1)}, bf16[128,2048]{1,0:T(8,128)(2,1)}, u32[]{:S(2)}, u32[]{:S(2)}) collective-permute-start(bf16[128,2048]{1,0:T(8,128)(2,1)} %get-tuple-element.255), channel_id=1, source_target_pairs={{0,8},{4,12},{16,0},{20,4},{24,16},{28,20},{8,24},{12,28},{1,9},{5... | collective-permute-start | bytes 1572872 | tf_op jit(solution)/shard_map/ppermute | solution.py:93
  (150 other events, 3784.5 us)
Sparse Core Ops, SparseCore 0:
  10.1 122.9 all-gather.2
  135.9 128.8 all-gather.4
  824.4 146.0 reduce-scatter.1

commit v7 on v6

--- a/solution.py
+++ b/solution.py
@@ -466,13 +466,8 @@
     w1 = w1.transpose(3, 2, 0, 1, 4).reshape(n_dp, cols, -1)
     w1 = after(w1, gains_all)
     dy_ring = jnp.stack(ring_blocks(after(cotangent, gains_all)))
-    w1 = walk_swap(w1, tables)
-    w1 = w1.reshape(width, -1)
     w2 = w_down.astype(BF).reshape(local_count * ff_part, width)
     half = local_count * ff_part
-    w1t, w2t = w1.T, w2.T
-    dy_near = gather_peers(dy_ring)
-    dy_far = core_flip(dy_near)
 
     seq_in = seq_tokens.astype(F32)
     normed_one = rms_scale(seq_in, gain_one).astype(BF)
@@ -491,8 +486,9 @@
     bias = jnp.where(visible, 0.0, -jnp.inf).astype(F32)[None, :]
     attended = attend(query_bf, key_bf, value_bf, bias, score_scale)
     attended = swap(attended.reshape(n_dp, rows, cols), "dp")
+    dy_near = gather_peers(after(dy_ring, attended))
+    dy_far = core_flip(dy_near)
     attended = attended.transpose(1, 0, 2).reshape(rows, width)
-    attended, w1, w1t, w2t = lax.optimization_barrier((attended, w1, w1t, w2t))
 
     inputs = tokens.astype(F32)
     hidden_one = inputs + dot(attended, wo_all)
@@ -508,6 +504,9 @@
     payload = jnp.concatenate(
         [normed_two, gates_hi, gates_lo, jnp.zeros((rows, spare), BF)], axis=1
     )
+    w1 = walk_swap(w1, tables, (payload,))
+    w1 = w1.reshape(width, -1)
+    w1t, w2t = w1.T, w2.T
     unit = jnp.arange(half, dtype=jnp.int32) // ff_part + seq_id * local_count
     gate_col = jnp.arange(lanes(2 * expert_total), dtype=jnp.int32)
     pick = (
@@ -548,7 +547,7 @@
     if not lean:
         mix_near = jnp.stack([m[0].reshape(-1, rows, width) for m in mix_parts], axis=1)
         mix_far = jnp.stack([m[1].reshape(-1, rows, width) for m in mix_parts], axis=1)
-        mix_far = after(mix_far, part)
+        mix_far = after(mix_far, returned)
         mix_near = add(mix_near, core_flip(mix_far))
         mix_parts = list(reduce_peers(mix_near))
         by_chunk = jnp.stack([g.reshape(2, -1, rows, half) for g in gated_inners], axis=2)
@@ -560,7 +559,8 @@
         pre_all = jnp.concatenate(pre_grads, axis=0)
         w1_grad = dot_rows(n2_all, pre_all)
     w1_grad = w1_grad.astype(BF)
-    w1_grad = after(w1_grad, returned)
+    if not lean:
+        w1_grad = after(w1_grad, part)
     token_grads = returned[:, :width]
     gg = returned[:, width : width + expert_total * n_dp].reshape(rows, expert_total, n_dp)
     gg = jnp.sum(gg, axis=-1)

time: 1260 us -> 1250 us (level)
  waiting for transfers between devices: 509 us -> 467 us
  blocking collectives: 0 us -> 38 us
    ppermute x14, waiting for transfers between devices: 157 us -> 117 us  [walk_swap(): block = lax.ppermute(block, 'dp', walk_perm(n_dp, index))]
    all_to_all x0 -> x1, blocking collectives: none -> 38 us  [swap(): return lax.all_to_all(blocks, axes, split_axis=0, concat_axis=0, tiled=True)]
    ppermute x14, starting transfers between devices: 9.97 us -> 44.3 us  [walk_swap(): block = lax.ppermute(block, 'dp', walk_perm(n_dp, index))]
    all_to_all x7 -> x6, starting transfers between devices: 66.3 us -> 33.2 us  [swap(): return lax.all_to_all(blocks, axes, split_axis=0, concat_axis=0, tiled=True)]
    optimization_barrier x2 -> x0, local copies, waits for them, and re-layouts: 12.8 us -> none  [the longest x1 6.44 us: after(): return lax.optimization_barrier((vals,) + others)[0]]
    unnamed x208 -> x220, local copies, waits for them, and re-layouts: 75 us -> 82.9 us
    all_to_all x7 -> x6, waiting for transfers between devices: 63 us -> 57.8 us  [swap(): return lax.all_to_all(blocks, axes, split_axis=0, concat_axis=0, tiled=True)]
  transfers between devices with their start and end apart: 95 -> 94, of which waited for: 44 -> 39; matrix products, arithmetic and copies ran while one was open for 34% -> 32% of each run, Pallas kernels for 10% -> 10%
where the time goes in v7:
time: 1250 us; the launch traced here: 1230 us
  waiting for transfers between devices  467 us (37%)
  local copies, waits for them, and re-layouts  223 us (18%)
  starting transfers between devices  152 us (12%)
  Pallas kernels  124 us (10%)
  other arithmetic  113 us (9%)
  matrix products  85.7 us (7%)
  blocking collectives  38 us (3%)
  between operations  31.6 us (3%)
    ppermute x56, waiting for transfers between devices, flip(): return lax.ppermute(vals, axis, [(i, i ^ bit) for i in range(size)])  172 us
    ppermute x15, waiting for transfers between devices, ring_shift(): return lax.ppermute(vals, 'dp', ring_perm(lax.axis_size('dp'), steps))  119 us
    ppermute x14, waiting for transfers between devices, walk_swap(): block = lax.ppermute(block, 'dp', walk_perm(n_dp, index))  117 us
    pallas_call x4, Pallas kernels, experts(): pl.pallas_call(body, grid=(2 * halves,), in_specs=[pl.BlockSpec((tile, wi...  102 us
    unnamed x220, local copies, waits for them, and re-layouts  82.9 us
    dot_general x6, matrix products, dot_rows(): lax.dot_general(left_mat, right_mat, (((0,), (0,)), ((), ())), preferred_...  60.5 us
    all_to_all x6, waiting for transfers between devices, swap(): return lax.all_to_all(blocks, axes, split_axis=0, concat_axis=0, tiled=True)  57.8 us
    ppermute x56, starting transfers between devices, flip(): return lax.ppermute(vals, axis, [(i, i ^ bit) for i in range(size)])  57.4 us
  transfers between devices with their start and end apart: 94, of which 39 were waited for; matrix products, arithmetic and copies ran while one was open for 32% of the time, Pallas kernels for 10%

profile of v7, /device:TPU:13, one launch (start us, length us, event | category | flops | bytes accessed | tf_op | source)
XLA Modules:
  0.0 1233.7 jit_solution(485764859795520098)
XLA Ops:
  11.4 38.0 %all_to_all.43 = bf16[8,64,3,256]{3,1,2,0:T(8,128)(2,1)S(1)} all-to-all(bf16[8,64,3,256]{3,1,2,0:T(8,128)(2,1)S(1)} %copy.315), channel_id=1, replica_groups=mesh['dp'=8,'expert'=4] {'dp'}, dimensions={0} | all-to-all | bytes 1572864 | tf_op jit(solution)/shard_map/all_to_all | solution.py:66
  67.4 27.5 %all-to-all-done.1 = f32[32,1,1160]{2,1,0:T(1,128)} async-done(((f32[32,1,1160]{2,1,0:T(1,128)}), f32[32,1,1160]{2,1,0:T(1,128)}, u32[]{:S(2)}, u32[]{:S(2)}) %all-to-all-start.1) | async-done | bytes 148512 | tf_op jit(solution)/shard_map/all_to_all | solution.py:66
  127.8 8.5 attend.1
  162.0 51.2 %collective-permute-done.9 = bf16[128,2048]{1,0:T(8,128)(2,1)} collective-permute-done((bf16[128,2048]{1,0:T(8,128)(2,1)}, bf16[128,2048]{1,0:T(8,128)(2,1)}, u32[]{:S(2)}, u32[]{:S(2)}) %collective-permute-start.9) | collective-permute-done | bytes 524320 | tf_op jit(solution)/shard_map/ppermute | solution.py:93
  213.2 12.3 collective-permute-done.8
  237.6 18.0 %collective-permute-done.11 = bf16[4,128,1024]{2,1,0:T(8,128)(2,1)S(1)} collective-permute-done((bf16[4,128,1024]{2,1,0:T(8,128)(2,1)S(1)}, bf16[4,128,1024]{2,1,0:T(8,128)(2,1)S(1)}, u32[]{:S(2)}, u32[]{:S(2)}) %collective-permute-start.11) | collective-permute-done | bytes 1048608 | tf_op jit(solution)/shard_map/ppermute | solution.py:98
  364.6 30.2 %collective-permute-done.20 = bf16[256,1024]{1,0:T(8,128)(2,1)S(1)} collective-permute-done((bf16[256,1024]{1,0:T(8,128)(2,1)}, bf16[256,1024]{1,0:T(8,128)(2,1)S(1)}, u32[]{:S(2)}, u32[]{:S(2)}) %collective-permute-start.20) | collective-permute-done | bytes 524320 | tf_op jit(solution)/shard_map/ppermute | solution.py:219
  395.4 11.9 collective-permute-start.3
  454.1 20.4 %collective-permute-done.39 = bf16[128,2176]{1,0:T(8,128)(2,1)S(1)} collective-permute-done((bf16[128,2176]{1,0:T(8,128)(2,1)}, bf16[128,2176]{1,0:T(8,128)(2,1)S(1)}, u32[]{:S(2)}, u32[]{:S(2)}) %collective-permute-start.39) | collective-permute-done | bytes 557088 | tf_op jit(solution)/shard_map/ppermute | solution.py:93
  504.3 10.7 collective-permute-done.43
  534.0 25.6 %experts.4 = (bf16[512,2048]{1,0:T(8,128)(2,1)}, bf16[512,2048]{1,0:T(8,128)(2,1)}, bf16[512,2176]{1,0:T(8,128)(2,1)}, bf16[512,2176]{1,0:T(8,128)(2,1)}, bf16[1...) custom-call(bf16[512,2176]{1,0:T(8,128)(2,1)} %bitcast.546, bf16[512,2176]{1,0:T(8,128)(2,1)} %copy-done.46, ...), custom_call_target="tpu_custom_call" | custom-call | flops 12884901888 | bytes 20971520 | tf_op jit(solution)/shard_map/experts/pallas_call | solution.py:290
  559.8 25.4 %experts.5 = (bf16[512,2048]{1,0:T(8,128)(2,1)}, bf16[512,2048]{1,0:T(8,128)(2,1)}, bf16[512,2176]{1,0:T(8,128)(2,1)}, bf16[512,2176]{1,0:T(8,128)(2,1)}, bf16[1...) custom-call(bf16[512,2176]{1,0:T(8,128)(2,1)} %bitcast.103.xa, bf16[512,2176]{1,0:T(8,128)(2,1)} %collective-permute-done.32.xb, ...), custom_call_target="tpu_custom_call" | custom-call | flops 12884901888 | bytes 20971520 | tf_op jit(solution)/shard_map/experts/pallas_call | solution.py:290
  592.1 25.5 %experts.7 = (bf16[512,2048]{1,0:T(8,128)(2,1)}, bf16[512,2048]{1,0:T(8,128)(2,1)}, bf16[512,2176]{1,0:T(8,128)(2,1)}, bf16[512,2176]{1,0:T(8,128)(2,1)}, bf16[1...) custom-call(bf16[512,2176]{1,0:T(8,128)(2,1)} %bitcast.145.xa, bf16[512,2176]{1,0:T(8,128)(2,1)} %collective-permute-done.56.xb, ...), custom_call_target="tpu_custom_call" | custom-call | flops 12884901888 | bytes 20971520 | tf_op jit(solution)/shard_map/experts/pallas_call | solution.py:290
  617.7 25.3 %experts.6 = (bf16[512,2048]{1,0:T(8,128)(2,1)}, bf16[512,2048]{1,0:T(8,128)(2,1)}, bf16[512,2176]{1,0:T(8,128)(2,1)}, bf16[512,2176]{1,0:T(8,128)(2,1)}, bf16[1...) custom-call(bf16[512,2176]{1,0:T(8,128)(2,1)} %bitcast.124.xa, bf16[512,2176]{1,0:T(8,128)(2,1)} %collective-permute-done.44.xb, ...), custom_call_target="tpu_custom_call" | custom-call | flops 12884901888 | bytes 20971520 | tf_op jit(solution)/shard_map/experts/pallas_call | solution.py:290
  657.9 23.5 %fusion.13 = bf16[2048,1024]{1,0:T(8,128)(2,1)} fusion(bf16[4096,2048]{1,0:T(8,128)(2,1)} %slice_dynamic-update-slice_fusion, bf16[1024,1024]{1,0:T(8,128)(2,1)S(1)} %copy-done.91, bf16[1024,1024]{1,0:T(8,128)(2,1)S(1)} %copy-done.92, bf16[1024,1024]{1,0:T(8,128)(2,1)S(1)} %copy-done.90, bf16[1024,1024]{1,0:T(8,128)(2,1)S(1)} %copy-done.89), kind=kOutput, calls=%fused_computation.35 | convolution fusion | flops 17215520768 | bytes 29360128 | tf_op jit(solution)/shard_map/dot_general | solution.py:51
  689.7 9.1 collective-permute-done.23
  700.8 10.4 collective-permute-done.34
  726.0 10.3 collective-permute-done.58
  738.2 9.3 collective-permute-done.46
  762.6 8.1 collective-permute-done.49
  773.1 28.8 %collective-permute-done.50 = bf16[128,2176]{1,0:T(8,128)(2,1)S(1)} collective-permute-done((bf16[128,2176]{1,0:T(8,128)(2,1)S(1)}, bf16[128,2176]{1,0:T(8,128)(2,1)S(1)}, u32[]{:S(2)}, u32[]{:S(2)}) %collective-permute-start.50) | collective-permute-done | bytes 557088 | tf_op jit(solution)/shard_map/ppermute | solution.py:93
  824.6 10.6 fusion.120
  839.4 13.3 %attend_back.1 = (f32[1024,256]{1,0:T(8,128)}, f32[1024,256]{1,0:T(8,128)}, bf16[1024,256]{1,0:T(8,128)(2,1)}) custom-call(bf16[1024,256]{1,0:T(8,128)(2,1)} %copy.375.q, bf16[1024,256]{1,0:T(8,128)(2,1)} %copy.376.k, bf16[1024,256]{1,0:T(8,128)(2,1)} %copy.384.v, f32[1,1024]{1,0:T(1,128)} %bitcast.636, bf16[1024,256]{1,0:T(8,128)(2,1)} %bitcast.631), custom_call_target="tpu_custom_call" | custom-call | flops 2684354560 | bytes 5242880 | tf_op jit(solution)/shard_map/attend_back/pallas_call | solution.py:383
  914.4 21.2 %all-to-all-done.4 = f32[32,1,1160]{2,1,0:T(1,128)S(1)} async-done(((f32[32,1,1160]{2,1,0:T(1,128)}), f32[32,1,1160]{2,1,0:T(1,128)S(1)}, u32[]{:S(2)}, u32[]{:S(2)}) %all-to-all-start.4) | async-done | bytes 148512 | tf_op jit(solution)/shard_map/all_to_all | solution.py:66
  940.8 11.9 convolution_add_fusion
  960.1 36.8 %collective-permute-done.71 = bf16[128,2048]{1,0:T(8,128)(2,1)S(1)} collective-permute-done((bf16[128,2048]{1,0:T(8,128)(2,1)S(1)}, bf16[128,2048]{1,0:T(8,128)(2,1)S(1)}, u32[]{:S(2)}, u32[]{:S(2)}) %collective-permute-start.71) | collective-permute-done | bytes 524320 | tf_op jit(solution)/shard_map/ppermute | solution.py:98
  1012.9 26.7 %collective-permute-start.80 = (bf16[256,1024]{1,0:T(8,128)(2,1)}, bf16[256,1024]{1,0:T(8,128)(2,1)}, u32[]{:S(2)}, u32[]{:S(2)}) collective-permute-start(bf16[256,1024]{1,0:T(8,128)(2,1)} %get-tuple-element.222), channel_id=1, source_target_pairs={{0,20},{4,16},{16,28},{20,24},{24,12},{28,8},{8,4},{12,0},{1,21},{... | collective-permute-start | bytes 1572872 | tf_op jit(solution)/shard_map/ppermute | solution.py:219
  1058.4 9.0 all-to-all-done.6
  1091.2 19.6 %collective-permute-done.81 = bf16[256,1024]{1,0:T(8,128)(2,1)S(1)} collective-permute-done((bf16[256,1024]{1,0:T(8,128)(2,1)S(1)}, bf16[256,1024]{1,0:T(8,128)(2,1)S(1)}, u32[]{:S(2)}, u32[]{:S(2)}) %collective-permute-start.81) | collective-permute-done | bytes 524320 | tf_op jit(solution)/shard_map/ppermute | solution.py:219
  1110.7 18.2 %collective-permute-done.82 = bf16[256,1024]{1,0:T(8,128)(2,1)S(1)} collective-permute-done((bf16[256,1024]{1,0:T(8,128)(2,1)S(1)}, bf16[256,1024]{1,0:T(8,128)(2,1)S(1)}, u32[]{:S(2)}, u32[]{:S(2)}) %collective-permute-start.82) | collective-permute-done | bytes 524320 | tf_op jit(solution)/shard_map/ppermute | solution.py:219
  1129.1 30.0 %collective-permute-done.83 = bf16[256,1024]{1,0:T(8,128)(2,1)S(1)} collective-permute-done((bf16[256,1024]{1,0:T(8,128)(2,1)S(1)}, bf16[256,1024]{1,0:T(8,128)(2,1)S(1)}, u32[]{:S(2)}, u32[]{:S(2)}) %collective-permute-start.83) | collective-permute-done | bytes 524320 | tf_op jit(solution)/shard_map/ppermute | solution.py:219
  1159.1 11.2 collective-permute-done.84
  (648 shorter events, 563.3 us)
Async XLA Ops:
  7.2 99.1 %all-gather.3.cloned.1.call-start = ((), (), s32[]{:S(2)}) async-start(), calls=%async_computation.8 | async-start | bytes 4718592 | tf_op jit(solution)/shard_map/all_gather | solution.py:70
  7.9 337.3 %all-gather.5.cloned.1.call-start = ((), (), s32[]{:S(2)}) async-start(), calls=%async_computation.9 | async-start | bytes 8650752 | tf_op jit(solution)/shard_map/all_gather | solution.py:70
  138.4 90.2 %all-to-all-start.2 = ((bf16[8,128,256]{1,2,0:T(8,128)(2,1)}), bf16[8,128,256]{1,2,0:T(8,128)(2,1)}, u32[]{:S(2)}, u32[]{:S(2)}) async-start(bf16[8,128,256]{1,2,0:T(8,128)(2,1)} %copy.321), calls=%async_computation.2 | async-start | bytes 1048576 | tf_op jit(solution)/shard_map/all_to_all | solution.py:66
  157.3 68.2 %collective-permute-start.8 = (bf16[128,2048]{1,0:T(8,128)(2,1)}, bf16[128,2048]{1,0:T(8,128)(2,1)}, u32[]{:S(2)}, u32[]{:S(2)}) collective-permute-start(bf16[128,2048]{1,0:T(8,128)(2,1)} %param.20), channel_id=1, source_target_pairs={{0,24},{4,28},{16,8},{20,12},{24,0},{28,4},{8,16},{12,20},{1,25},{... | collective-permute-start | bytes 1572872 | tf_op jit(solution)/shard_map/ppermute | solution.py:93
  157.3 68.2 %collective-permute-start.7 = (bf16[128,2048]{1,0:T(8,128)(2,1)}, bf16[128,2048]{1,0:T(8,128)(2,1)}, u32[]{:S(2)}, u32[]{:S(2)}) collective-permute-start(bf16[128,2048]{1,0:T(8,128)(2,1)} %param.20), channel_id=1, source_target_pairs={{0,16},{4,20},{16,24},{20,28},{24,8},{28,12},{8,0},{12,4},{1,17},{... | collective-permute-start | bytes 1572872 | tf_op jit(solution)/shard_map/ppermute | solution.py:93
  258.1 68.6 %collective-permute-start.12 = (bf16[2,4,128,1024]{3,2,1,0:T(8,128)(2,1)}, bf16[2,4,128,1024]{3,2,1,0:T(8,128)(2,1)}, u32[]{:S(2)}, u32[]{:S(2)}) collective-permute-start(bf16[2,4,128,1024]{3,2,1,0:T(8,128)(2,1)} %pad_maximum_fusion.9), channel_id=1, source_target_pairs={{0,4},{4,0},{8,12},{12,8},{16,20},{20,16},{24,28},{28,24},{1,5},{5... | collective-permute-start | bytes 6291464 | tf_op jit(solution)/shard_map/ppermute | solution.py:98
  305.8 89.5 %collective-permute-start.17 = (bf16[256,1024]{1,0:T(8,128)(2,1)}, bf16[256,1024]{1,0:T(8,128)(2,1)}, u32[]{:S(2)}, u32[]{:S(2)}) collective-permute-start(bf16[256,1024]{1,0:T(8,128)(2,1)} %bitcast.627), channel_id=1, source_target_pairs={{0,20},{4,16},{16,28},{20,24},{24,12},{28,8},{8,4},{12,0},{1,21},{... | collective-permute-start | bytes 1572872 | tf_op jit(solution)/shard_map/ppermute | solution.py:219
  333.1 78.0 %collective-permute-start.19 = (bf16[256,1024]{1,0:T(8,128)(2,1)}, bf16[256,1024]{1,0:T(8,128)(2,1)}, u32[]{:S(2)}, u32[]{:S(2)}) collective-permute-start(bf16[256,1024]{1,0:T(8,128)(2,1)} %bitcast.68), channel_id=1, source_target_pairs={{0,28},{4,24},{16,12},{20,8},{24,4},{28,0},{8,20},{12,16},{1,29},{... | collective-permute-start | bytes 1572872 | tf_op jit(solution)/shard_map/ppermute | solution.py:219
  363.3 164.9 %collective-permute-start.14 = (bf16[4,4,128,2048]{3,2,1,0:T(8,128)(2,1)}, bf16[4,4,128,2048]{3,2,1,0:T(8,128)(2,1)}, u32[]{:S(2)}, u32[]{:S(2)}) collective-permute-start(bf16[4,4,128,2048]{3,2,1,0:T(8,128)(2,1)} %pad_maximum_fusion.ya), channel_id=1, source_target_pairs={{0,1},{1,0},{2,3},{3,2},{4,5},{5,4},{6,7},{7,6},{8,9},{9,8},{10,11... | collective-permute-start | bytes 25165832 | tf_op jit(solution)/shard_map/ppermute | solution.py:98
  520.4 71.7 %collective-permute-start.56 = (bf16[512,2176]{1,0:T(8,128)(2,1)}, bf16[512,2176]{1,0:T(8,128)(2,1)}, u32[]{:S(2)}, u32[]{:S(2)}) collective-permute-start(bf16[512,2176]{1,0:T(8,128)(2,1)} %bitcast.145.xa), channel_id=1, source_target_pairs={{0,1},{1,0},{2,3},{3,2},{4,5},{5,4},{6,7},{7,6},{8,9},{9,8},{10,11... | collective-permute-start | bytes 6684680 | tf_op jit(solution)/shard_map/ppermute | solution.py:98
  522.3 95.4 %collective-permute-start.44 = (bf16[512,2176]{1,0:T(8,128)(2,1)}, bf16[512,2176]{1,0:T(8,128)(2,1)}, u32[]{:S(2)}, u32[]{:S(2)}) collective-permute-start(bf16[512,2176]{1,0:T(8,128)(2,1)} %bitcast.124.xa), channel_id=1, source_target_pairs={{0,1},{1,0},{2,3},{3,2},{4,5},{5,4},{6,7},{7,6},{8,9},{9,8},{10,11... | collective-permute-start | bytes 6684680 | tf_op jit(solution)/shard_map/ppermute | solution.py:98
  559.7 122.8 %collective-permute-start.22 = (bf16[512,2176]{1,0:T(8,128)(2,1)}, bf16[512,2176]{1,0:T(8,128)(2,1)}, u32[]{:S(2)}, u32[]{:S(2)}) collective-permute-start(bf16[512,2176]{1,0:T(8,128)(2,1)} %get-tuple-element.77), channel_id=1, source_target_pairs={{0,1},{1,0},{2,3},{3,2},{4,5},{5,4},{6,7},{7,6},{8,9},{9,8},{10,11... | collective-permute-start | bytes 6684680 | tf_op jit(solution)/shard_map/ppermute | solution.py:98
  585.2 100.5 %collective-permute-start.33 = (bf16[512,2176]{1,0:T(8,128)(2,1)}, bf16[512,2176]{1,0:T(8,128)(2,1)}, u32[]{:S(2)}, u32[]{:S(2)}) collective-permute-start(bf16[512,2176]{1,0:T(8,128)(2,1)} %get-tuple-element.79), channel_id=1, source_target_pairs={{0,1},{1,0},{2,3},{3,2},{4,5},{5,4},{6,7},{7,6},{8,9},{9,8},{10,11... | collective-permute-start | bytes 6684680 | tf_op jit(solution)/shard_map/ppermute | solution.py:98
  617.6 94.2 %collective-permute-start.57 = (bf16[512,2176]{1,0:T(8,128)(2,1)}, bf16[512,2176]{1,0:T(8,128)(2,1)S(1)}, u32[]{:S(2)}, u32[]{:S(2)}) collective-permute-start(bf16[512,2176]{1,0:T(8,128)(2,1)} %get-tuple-element.84), channel_id=1, source_target_pairs={{0,1},{1,0},{2,3},{3,2},{4,5},{5,4},{6,7},{7,6},{8,9},{9,8},{10,11... | collective-permute-start | bytes 6684680 | tf_op jit(solution)/shard_map/ppermute | solution.py:98
  643.1 71.1 %collective-permute-start.45 = (bf16[512,2176]{1,0:T(8,128)(2,1)}, bf16[512,2176]{1,0:T(8,128)(2,1)S(1)}, u32[]{:S(2)}, u32[]{:S(2)}) collective-permute-start(bf16[512,2176]{1,0:T(8,128)(2,1)} %get-tuple-element.82), channel_id=1, source_target_pairs={{0,1},{1,0},{2,3},{3,2},{4,5},{5,4},{6,7},{7,6},{8,9},{9,8},{10,11... | collective-permute-start | bytes 6684680 | tf_op jit(solution)/shard_map/ppermute | solution.py:98
  700.3 70.7 %collective-permute-start.24 = (bf16[128,1024]{1,0:T(8,128)(2,1)S(1)}, bf16[128,1024]{1,0:T(8,128)(2,1)S(1)}, u32[]{:S(2)}, u32[]{:S(2)}) collective-permute-start(bf16[128,1024]{1,0:T(8,128)(2,1)S(1)} %fusion.68), channel_id=1, source_target_pairs={{0,4},{4,0},{8,12},{12,8},{16,20},{20,16},{24,28},{28,24},{1,5},{5... | collective-permute-start | bytes 786440 | tf_op jit(solution)/shard_map/ppermute | solution.py:98
  802.2 95.7 %collective-permute-start.63 = (bf16[4,4,128,2048]{3,2,1,0:T(8,128)(2,1)}, bf16[4,4,128,2048]{3,2,1,0:T(8,128)(2,1)}, u32[]{:S(2)}, u32[]{:S(2)}) collective-permute-start(bf16[4,4,128,2048]{3,2,1,0:T(8,128)(2,1)} %pad_maximum_fusion.1), channel_id=1, source_target_pairs={{0,1},{1,0},{2,3},{3,2},{4,5},{5,4},{6,7},{7,6},{8,9},{9,8},{10,11... | collective-permute-start | bytes 25165832 | tf_op jit(solution)/shard_map/ppermute | solution.py:98
  817.7 407.5 %reduce-scatter.2.cloned.1.call-start = ((), (), s32[]{:S(2)}) async-start(), calls=%async_computation.10 | async-start | bytes 8650752 | tf_op jit(solution)/shard_map/reduce_scatter | solution.py:74
  879.6 73.0 %collective-permute-start.72 = (bf16[128,2048]{1,0:T(8,128)(2,1)}, bf16[128,2048]{1,0:T(8,128)(2,1)}, u32[]{:S(2)}, u32[]{:S(2)}) collective-permute-start(bf16[128,2048]{1,0:T(8,128)(2,1)} %get-tuple-element.229), channel_id=1, source_target_pairs={{0,4},{4,0},{8,12},{12,8},{16,20},{20,16},{24,28},{28,24},{1,5},{5... | collective-permute-start | bytes 1572872 | tf_op jit(solution)/shard_map/ppermute | solution.py:98
  880.3 72.5 %collective-permute-start.76 = (bf16[128,2048]{1,0:T(8,128)(2,1)}, bf16[128,2048]{1,0:T(8,128)(2,1)}, u32[]{:S(2)}, u32[]{:S(2)}) collective-permute-start(bf16[128,2048]{1,0:T(8,128)(2,1)} %get-tuple-element.227), channel_id=1, source_target_pairs={{0,4},{4,0},{8,12},{12,8},{16,20},{20,16},{24,28},{28,24},{1,5},{5... | collective-permute-start | bytes 1572872 | tf_op jit(solution)/shard_map/ppermute | solution.py:98
  881.1 71.7 %collective-permute-start.74 = (bf16[128,2048]{1,0:T(8,128)(2,1)}, bf16[128,2048]{1,0:T(8,128)(2,1)}, u32[]{:S(2)}, u32[]{:S(2)}) collective-permute-start(bf16[128,2048]{1,0:T(8,128)(2,1)} %get-tuple-element.228), channel_id=1, source_target_pairs={{0,4},{4,0},{8,12},{12,8},{16,20},{20,16},{24,28},{28,24},{1,5},{5... | collective-permute-start | bytes 1572872 | tf_op jit(solution)/shard_map/ppermute | solution.py:98
  911.2 138.2 %collective-permute-start.64 = (bf16[2,4,128,1024]{3,2,1,0:T(8,128)(2,1)}, bf16[2,4,128,1024]{3,2,1,0:T(8,128)(2,1)}, u32[]{:S(2)}, u32[]{:S(2)}) collective-permute-start(bf16[2,4,128,1024]{3,2,1,0:T(8,128)(2,1)} %pad_maximum_fusion.11), channel_id=1, source_target_pairs={{0,2},{1,3},{2,0},{3,1},{4,6},{5,7},{6,4},{7,5},{8,10},{9,11},{10,... | collective-permute-start | bytes 6291464 | tf_op jit(solution)/shard_map/ppermute | solution.py:98
  914.1 138.6 %collective-permute-start.66 = (bf16[2,4,128,1024]{3,2,1,0:T(8,128)(2,1)}, bf16[2,4,128,1024]{3,2,1,0:T(8,128)(2,1)}, u32[]{:S(2)}, u32[]{:S(2)}) collective-permute-start(bf16[2,4,128,1024]{3,2,1,0:T(8,128)(2,1)} %pad_maximum_fusion.12), channel_id=1, source_target_pairs={{0,4},{4,0},{8,12},{12,8},{16,20},{20,16},{24,28},{28,24},{1,5},{5... | collective-permute-start | bytes 6291464 | tf_op jit(solution)/shard_map/ppermute | solution.py:98
  935.6 106.1 %all-to-all-start.5 = ((bf16[4,8,64,768]{3,2,1,0:T(8,128)(2,1)}), bf16[4,8,64,768]{3,2,1,0:T(8,128)(2,1)}, u32[]{:S(2)}, u32[]{:S(2)}) async-start(bf16[4,8,64,768]{3,2,1,0:T(8,128)(2,1)} %bitcast.541), calls=%async_computation.5 | async-start | bytes 6291456 | tf_op jit(solution)/shard_map/all_to_all | solution.py:66
  1004.5 70.8 %collective-permute-start.78 = (bf16[256,1024]{1,0:T(8,128)(2,1)}, bf16[256,1024]{1,0:T(8,128)(2,1)}, u32[]{:S(2)}, u32[]{:S(2)}) collective-permute-start(bf16[256,1024]{1,0:T(8,128)(2,1)} %get-tuple-element.224), channel_id=1, source_target_pairs={{0,4},{4,0},{16,20},{20,16},{24,28},{28,24},{8,12},{12,8},{1,5},{5... | collective-permute-start | bytes 1572872 | tf_op jit(solution)/shard_map/ppermute | solution.py:219
  1004.5 70.8 %collective-permute-start.79 = (bf16[256,1024]{1,0:T(8,128)(2,1)}, bf16[256,1024]{1,0:T(8,128)(2,1)}, u32[]{:S(2)}, u32[]{:S(2)}) collective-permute-start(bf16[256,1024]{1,0:T(8,128)(2,1)} %get-tuple-element.223), channel_id=1, source_target_pairs={{0,16},{4,20},{16,24},{20,28},{24,8},{28,12},{8,0},{12,4},{1,17},{... | collective-permute-start | bytes 1572872 | tf_op jit(solution)/shard_map/ppermute | solution.py:219
  1012.9 77.0 %collective-permute-start.80 = (bf16[256,1024]{1,0:T(8,128)(2,1)}, bf16[256,1024]{1,0:T(8,128)(2,1)}, u32[]{:S(2)}, u32[]{:S(2)}) collective-permute-start(bf16[256,1024]{1,0:T(8,128)(2,1)} %get-tuple-element.222), channel_id=1, source_target_pairs={{0,20},{4,16},{16,28},{20,24},{24,12},{28,8},{8,4},{12,0},{1,21},{... | collective-permute-start | bytes 1572872 | tf_op jit(solution)/shard_map/ppermute | solution.py:219
  1081.5 77.6 %collective-permute-start.83 = (bf16[256,1024]{1,0:T(8,128)(2,1)S(1)}, bf16[256,1024]{1,0:T(8,128)(2,1)S(1)}, u32[]{:S(2)}, u32[]{:S(2)}) collective-permute-start(bf16[256,1024]{1,0:T(8,128)(2,1)S(1)} %copy-done.59), channel_id=1, source_target_pairs={{0,8},{4,12},{16,0},{20,4},{24,16},{28,20},{8,24},{12,28},{1,9},{5... | collective-permute-start | bytes 1572872 | tf_op jit(solution)/shard_map/ppermute | solution.py:219
  1083.5 86.9 %collective-permute-start.84 = (bf16[256,1024]{1,0:T(8,128)(2,1)S(1)}, bf16[256,1024]{1,0:T(8,128)(2,1)S(1)}, u32[]{:S(2)}, u32[]{:S(2)}) collective-permute-start(bf16[256,1024]{1,0:T(8,128)(2,1)S(1)} %copy-done.58), channel_id=1, source_target_pairs={{0,12},{4,8},{16,4},{20,0},{24,20},{28,16},{8,28},{12,24},{1,13},{... | collective-permute-start | bytes 1572872 | tf_op jit(solution)/shard_map/ppermute | solution.py:219
  1089.8 132.9 %collective-permute-start.70 = (bf16[128,2048]{1,0:T(8,128)(2,1)}, bf16[128,2048]{1,0:T(8,128)(2,1)}, u32[]{:S(2)}, u32[]{:S(2)}) collective-permute-start(bf16[128,2048]{1,0:T(8,128)(2,1)} %get-tuple-element.267), channel_id=1, source_target_pairs={{0,16},{4,20},{16,24},{20,28},{24,8},{28,12},{8,0},{12,4},{1,17},{... | collective-permute-start | bytes 1572872 | tf_op jit(solution)/shard_map/ppermute | solution.py:93
  1110.7 112.0 %collective-permute-start.69 = (bf16[128,2048]{1,0:T(8,128)(2,1)}, bf16[128,2048]{1,0:T(8,128)(2,1)}, u32[]{:S(2)}, u32[]{:S(2)}) collective-permute-start(bf16[128,2048]{1,0:T(8,128)(2,1)} %get-tuple-element.268), channel_id=1, source_target_pairs={{0,24},{4,28},{16,8},{20,12},{24,0},{28,4},{8,16},{12,20},{1,25},{... | collective-permute-start | bytes 1572872 | tf_op jit(solution)/shard_map/ppermute | solution.py:93
  1129.0 93.7 %collective-permute-start.68 = (bf16[128,2048]{1,0:T(8,128)(2,1)}, bf16[128,2048]{1,0:T(8,128)(2,1)}, u32[]{:S(2)}, u32[]{:S(2)}) collective-permute-start(bf16[128,2048]{1,0:T(8,128)(2,1)} %get-tuple-element.266), channel_id=1, source_target_pairs={{0,8},{4,12},{16,0},{20,4},{24,16},{28,20},{8,24},{12,28},{1,9},{5... | collective-permute-start | bytes 1572872 | tf_op jit(solution)/shard_map/ppermute | solution.py:93
  (155 other events, 2991.7 us)
Sparse Core Ops, SparseCore 0:
  10.1 86.3 all-gather.2
  99.4 104.2 all-gather.4
  824.7 139.0 reduce-scatter.1
